TPU v7x, 128 devices: a whole 4x4x4 slice. The times are simulated.
128 devices in a mesh: src: 8 (over y, x_hi), reg: 16 (over z, x_lo, core).
Axes of the slice: x: 4 (x_hi: 2, x_lo: 2; x = x_hi * 2 + x_lo), y: 4, z: 4, core: 2. Of those that a mesh axis runs over, the one named last changes fastest.
Arguments:
- displacement: float32 [3, 5, 1024, 2048], P(None, None, 'src', 'reg'), may hold values from -0.06 to 0.06
- velocity: float32 [3, 5, 1024, 2048], P(None, None, 'src', 'reg'), may hold values from -6 to 6
- modulus: float32 [5, 1024, 2048], P(None, 'src', 'reg'), may hold values from 0.5 to 2
- density: float32 [5, 1024, 2048], P(None, 'src', 'reg'), may hold values from 0.8 to 1.25
- traces: float32 [128, 512, 9, 128], P(('src', 'reg')), may hold values from -18 to 18
- record_row: int32 [128, 512], P(('src', 'reg')), may hold values from 0 to 127, as said below
Outputs:
- final_displacement: float32 [3, 5, 1024, 2048], P(None, None, 'src', 'reg')
- final_velocity: float32 [3, 5, 1024, 2048], P(None, None, 'src', 'reg')
Inputs may be any that keep to these rules, and one draw needn't show every extreme that they name: `record_row`: for every destination device d and step t, the entries of slots (d * 4 + t) + k, k < 1, taken over all segmenting buffers in order, form a permutation of 0 to 127.
All inputs are finite; a program needn't handle non-finite values.
Results may differ from a plain program's by a relative error of at most 0.000061.
Values sent between devices are 32-bit elements; how exact they have to be, the bound alone decides.
No kernel may reach another device: no remote copies, remote signals or barrier semaphores. Data moves between devices by JAX's collectives and lax.ppermute only.
A program may use at most 128 MiB of HBM per device.

v0:
```python
import math

import jax
import jax.numpy as jnp
import numpy as np
from jax import lax
from jax.experimental import pallas as pl
from jax.experimental.pallas import tpu as pltpu
from jax.sharding import PartitionSpec as P


F32 = jnp.float32
BF16 = jnp.bfloat16
STEPS = 4
DT = 0.02
N = 128
H = 16
E = 40
FORCE_ROWS = ((12, 0), (8, 12), (4, 20))
VMEM_LIMIT = 28 * 1024 * 1024


def gll():
    inner = math.sqrt(3.0 / 7.0)
    x = np.array([-1.0, -inner, 0.0, inner, 1.0])
    w = np.array([0.1, 49.0 / 90.0, 32.0 / 45.0, 49.0 / 90.0, 0.1])
    leg = (35.0 * x**4 - 30.0 * x**2 + 3.0) / 8.0
    d = np.zeros((5, 5))
    for i in range(5):
        for j in range(5):
            if i != j:
                d[i, j] = leg[i] / (leg[j] * (x[i] - x[j]))
    d[0, 0] = -5.0
    d[4, 4] = 5.0
    return d, w


DER, W = gll()
BACK = (DER * W[:, None]).T
PERIODIC = [2 * W[0], W[1], W[2], W[3]]


def apply5(m, v):
    s0, s1, m0, m1 = v[0] + v[4], v[1] + v[3], v[0] - v[4], v[1] - v[3]
    f = lambda a: float(np.float32(a))
    out = [None] * 5
    for i in (0, 1):
        p = f((m[i, 0] - m[i, 4]) / 2) * m0 + f((m[i, 1] - m[i, 3]) / 2) * m1
        q = f((m[i, 0] + m[i, 4]) / 2) * s0 + f((m[i, 1] + m[i, 3]) / 2) * s1 + f(m[i, 2]) * v[2]
        out[i], out[4 - i] = p + q, p - q
    out[2] = f(m[2, 0]) * m0 + f(m[2, 1]) * m1
    return out


def column_of(x, comp):
    if 0 <= x < N:
        return x
    return N + 32 * comp + (x - N if x >= N else x + 32)


def east_tables():
    grad = np.zeros((3, 256, 256))
    sel = np.zeros((256, 256))
    weight = np.zeros((1, 256))
    for k in range(E):
        for i in range(5):
            q = i * E + k
            xi = 4 * (k - 4) + i
            weight[0, q] = 0.5 * W[i]
            if xi < N + H:
                sel[column_of(xi, 0), q] = 1.0
            for comp in range(3):
                for j in range(5):
                    xj = 4 * (k - 4) + j
                    if xj < N + H:
                        grad[comp, column_of(xj, comp), q] = DER[i, j]

    def two(a):
        hi = a.astype(np.float32).astype(jnp.bfloat16)
        lo = (a - hi.astype(np.float64)).astype(np.float32).astype(jnp.bfloat16)
        return np.stack([hi, lo], axis=1)

    back = np.ascontiguousarray(np.swapaxes(grad, 1, 2))
    return two(grad), two(back), sel.astype(jnp.bfloat16), weight.astype(np.float32)


def shifted(block, axis, distance):
    n = lax.axis_size(axis)
    return lax.ppermute(block, axis, [((i - distance) % n, i) for i in range(n)])


def in_hbm(*arrays):
    return [pltpu.with_memory_space_constraint(x, pltpu.HBM) for x in arrays]


def dot(a, b):
    return jnp.dot(a, b, preferred_element_type=F32)


def split2(x):
    hi = x.astype(BF16)
    return hi, (x - hi.astype(F32)).astype(BF16)


def lane_ids(shape):
    return lax.broadcasted_iota(jnp.int32, shape, len(shape) - 1)


def east_weight(shape):
    r = lane_ids(shape) % 4
    f = lambda a: float(np.float32(a))
    return jnp.where(r == 0, f(PERIODIC[0]), jnp.where(r == 2, f(PERIODIC[2]), f(PERIODIC[1])))


def lane_move(x, shift, start, width=16):
    shift %= 128
    y = pltpu.roll(x, shift, x.ndim - 1) if shift else x
    lane = lane_ids(x.shape)
    return jnp.where((lane >= start) & (lane < start + width), y, 0.0)


def pack_kernel(tr_ref, id_ref, out_ref, buf, in_sem, out_sem):
    copy = pltpu.make_async_copy
    part = N // 4
    loads = []
    for q in range(4):
        at = pl.ds(q * part, part)
        loads.append(
            [
                copy((tr_ref.at[k, at] if k < 9 else id_ref.at[at]), buf.at[at, k], in_sem.at[q, k])
                for k in range(10)
            ]
        )
        for c in loads[q]:
            c.start()
    stores = []
    for q in range(4):
        for c in loads[q]:
            c.wait()
        at = pl.ds(q * part, part)
        stores.append(copy(buf.at[at], out_ref.at[at], out_sem.at[q]))
        stores[q].start()
    for c in stores:
        c.wait()


def pack(records, rows):
    return pl.pallas_call(
        pack_kernel,
        in_specs=[pl.BlockSpec(memory_space=pltpu.HBM)] * 2,
        out_specs=pl.BlockSpec(memory_space=pltpu.HBM),
        out_shape=pltpu.HBM((128, 10, STEPS, 128), F32),
        scratch_shapes=[
            pltpu.VMEM((N, 10, STEPS, N), F32),
            pltpu.SemaphoreType.DMA((4, 10)),
            pltpu.SemaphoreType.DMA((4,)),
        ],
        compiler_params=pltpu.CompilerParams(vmem_limit_bytes=8 * 1024 * 1024),
        name="pack",
    )(*in_hbm(records, rows))


def strips_kernel(
    d_ref, v_ref, m_ref, r_ref, west_ref, east_ref, north_ref, south_ref, ln_ref, ls_ref,
    buf, west_buf, east_buf, in_sem, row_sem, out_sem,
):
    copy = pltpu.make_async_copy
    loads = []
    for z in range(5):
        loads.append(
            [
                copy(d_ref.at[:, z], buf.at[z, 0:3], in_sem.at[z, 0]),
                copy(v_ref.at[:, z], buf.at[z, 3:6], in_sem.at[z, 1]),
                copy(m_ref.at[z], buf.at[z, 6], in_sem.at[z, 2]),
                copy(r_ref.at[z], buf.at[z, 7], in_sem.at[z, 3]),
            ]
        )
        for c in loads[z]:
            c.start()
    lane = lane_ids((N, N))
    stores = []
    for z in range(5):
        for c in loads[z]:
            c.wait()
        for i, (at, top, low) in enumerate(
            ((slice(0, 6), north_ref, south_ref), (slice(6, 8), ln_ref, ls_ref))
        ):
            stores.append(copy(buf.at[z, at, N - H : N], top.at[:, z], row_sem.at[z, 2 * i]))
            stores.append(copy(buf.at[z, at, 0:H], low.at[:, z], row_sem.at[z, 2 * i + 1]))
        for c in stores[-4:]:
            c.start()
        west = buf[z, 0]
        east = pltpu.roll(west, N - 112, 1)
        for a in range(1, 8):
            x = buf[z, a]
            west = jnp.where(lane < 16 * a, west, pltpu.roll(x, 16 * a, 1))
            east = jnp.where(
                lane < 16 * a, east, pltpu.roll(x, (16 * a - 112) % N, 1) if a != 7 else x
            )
        west_buf[z] = west
        east_buf[z] = east
        stores.append(copy(west_buf.at[z], west_ref.at[z], out_sem.at[z, 0]))
        stores.append(copy(east_buf.at[z], east_ref.at[z], out_sem.at[z, 1]))
        for c in stores[-2:]:
            c.start()
    for c in stores:
        c.wait()


def strips(d, v, m, r):
    hbm = pl.BlockSpec(memory_space=pltpu.HBM)
    dma = pltpu.SemaphoreType.DMA
    return pl.pallas_call(
        strips_kernel,
        in_specs=[hbm] * 4,
        out_specs=[hbm] * 6,
        out_shape=[pltpu.HBM((5, N, N), F32)] * 2
        + [pltpu.HBM((6, 5, H, N), F32)] * 2
        + [pltpu.HBM((2, 5, H, N), F32)] * 2,
        scratch_shapes=[
            pltpu.VMEM((5, 8, N, N), F32),
            pltpu.VMEM((5, N, N), F32),
            pltpu.VMEM((5, N, N), F32),
            dma((5, 4)),
            dma((5, 4)),
            dma((5, 2)),
        ],
        compiler_params=pltpu.CompilerParams(vmem_limit_bytes=16 * 1024 * 1024),
        name="strips",
    )(*in_hbm(d, v, m, r))


def place_kernel(
    arr_ref, mod_ref, rho_ref, b_ref, west_ref, east_ref, inj_ref, last_ref, m_ref, r_ref, vid_ref, ids_ref, sem
):
    own = [
        pltpu.make_async_copy(mod_ref.at[0:1], m_ref, sem.at[0]),
        pltpu.make_async_copy(rho_ref.at[0:1], r_ref, sem.at[1]),
    ]
    for c in own:
        c.start()
    vid_ref[...] = arr_ref[:, 36, :].astype(jnp.int32)
    to_scalar = pltpu.make_async_copy(vid_ref, ids_ref, sem.at[2])
    to_scalar.start()
    to_scalar.wait()
    for c in own:
        c.wait()

    def body(s, carry):
        for t in range(STEPS):
            r = ids_ref[s, t]
            at = pl.multiple_of((t * N + r) * 8, 8)
            inj_ref[pl.ds(at, 8), :] = arr_ref[s, pl.ds(t, 8, stride=4), :]
            last_ref[pl.ds(t * N + r, 1), :] = arr_ref[s, 32 + t : 33 + t, :]
        return carry

    lax.fori_loop(0, 128, body, 0, unroll=8)
    ew = east_weight((8, N))
    row = lax.broadcasted_iota(jnp.int32, (8, N), 0) % 4
    f = lambda a: float(np.float32(a))
    nw = jnp.where(row == 0, f(PERIODIC[0]), jnp.where(row == 2, f(PERIODIC[2]), f(PERIODIC[1])))
    area = 0.25 * ew * nw

    def combine(k, carry):
        y = pl.multiple_of(k * 8, 8)
        mod = m_ref[0, pl.ds(y, 8), :]
        imp = jnp.sqrt(r_ref[0, pl.ds(y, 8), :] * mod)
        spring = 0.5 * mod
        for t in range(STEPS):
            west = east = None
            for c in range(3):
                base = (t * N + y) * 8
                inc = inj_ref[pl.ds(base + c, 8, stride=8), :]
                vel = inj_ref[pl.ds(base + 3 + c, 8, stride=8), :]
                if c < 2:
                    dis = inj_ref[pl.ds(base + 6 + c, 8, stride=8), :]
                else:
                    dis = last_ref[pl.ds(t * N + y, 8), :]
                b = area * (inc + imp * vel + spring * dis)
                b_ref[t, c, pl.ds(y, 8), :] = b
                if t < 3:
                    w = lane_move(b, 32 * c, 32 * c)
                    e = lane_move(b, 32 * c + 16 - 112, 32 * c + 16)
                    west = w if c == 0 else west + w
                    east = e if c == 0 else east + e
            if t < 3:
                west_ref[t, pl.ds(y, 8), :] = west
                east_ref[t, pl.ds(y, 8), :] = east
        return carry

    lax.fori_loop(0, 16, combine, 0)


def place(arrived, mod, rho):
    whole = pl.BlockSpec(memory_space=pltpu.VMEM)
    hbm = pl.BlockSpec(memory_space=pltpu.HBM)
    return pl.pallas_call(
        place_kernel,
        in_specs=[whole, hbm, hbm],
        out_specs=[whole] * 3,
        out_shape=[
            jax.ShapeDtypeStruct((STEPS, 3, N, N), F32),
            jax.ShapeDtypeStruct((3, N, N), F32),
            jax.ShapeDtypeStruct((3, N, N), F32),
        ],
        scratch_shapes=[
            pltpu.VMEM((STEPS * N * 8, N), F32),
            pltpu.VMEM((STEPS * N, N), F32),
            pltpu.VMEM((1, N, N), F32),
            pltpu.VMEM((1, N, N), F32),
            pltpu.VMEM((N, N), jnp.int32),
            pltpu.SMEM((N, N), jnp.int32),
            pltpu.SemaphoreType.DMA((3,)),
        ],
        compiler_params=pltpu.CompilerParams(vmem_limit_bytes=VMEM_LIMIT),
        name="place",
    )(arrived, *in_hbm(mod, rho))


def rows_kernel(b_ref, e_ref, w_ref, strip_ref, north_ref, south_ref):
    for t in range(3):
        s = e_ref[t] + w_ref[t]
        strip_ref[t] = s
        n, at = FORCE_ROWS[t]
        for ch in range(4):
            x = b_ref.at[t, ch] if ch < 3 else strip_ref.at[t]
            north_ref[ch, at : at + n] = x[N - n :, :]
            south_ref[ch, at : at + n] = x[:n, :]


def force_rows(b, from_east, from_west):
    whole = pl.BlockSpec(memory_space=pltpu.VMEM)
    return pl.pallas_call(
        rows_kernel,
        in_specs=[whole] * 3,
        out_specs=[whole] * 3,
        out_shape=[
            jax.ShapeDtypeStruct((3, N, N), F32),
            jax.ShapeDtypeStruct((4, 24, N), F32),
            jax.ShapeDtypeStruct((4, 24, N), F32),
        ],
        compiler_params=pltpu.CompilerParams(vmem_limit_bytes=VMEM_LIMIT),
        name="force_rows",
    )(b, from_east, from_west)


def line_forces(d, k, kn, mn_ref, ce_ref, grad_ref, back_ref, channels, emit):
    rows = 5 * 4 * E

    def north(ch):
        m = ch // 3
        for z in range(5):
            v = [d[ch][z, j] for j in range(4)]
            v.append(pltpu.roll(v[0], E - 1, 0))
            g = apply5(DER, v)
            r = apply5(BACK * W[z], [g[i] * mn_ref[m, z, i] for i in range(5)])
            r[0] = r[0] + pltpu.roll(r[4], 1, 0)
            for j in range(4):
                kn[ch][z, j] = r[j]

    def depth(ch):
        m = ch // 3
        for j in range(4):
            x = [d[ch][z, j] for z in range(5)]
            g = apply5(DER, x)
            r = apply5(BACK * PERIODIC[j], [g[z] * mn_ref[m, z, j] for z in range(5)])
            for z in range(5):
                emit(ch, j, z, x[z], (k[ch][z, j] + kn[ch][z, j]) + r[z])

    sh, sl = split2(d[3][...].reshape(rows, N))
    strip = None
    for c in range(3):
        mh, ml = split2(d[c][...].reshape(rows, N))
        hi = jnp.concatenate([mh, sh], axis=1)
        lo = jnp.concatenate([ml, sl], axis=1)
        g = dot(hi, grad_ref[c, 0]) + dot(lo, grad_ref[c, 0]) + dot(hi, grad_ref[c, 1])
        fh, fl = split2(g * ce_ref[...])
        f = dot(fh, back_ref[c, 0]) + dot(fl, back_ref[c, 0]) + dot(fh, back_ref[c, 1])
        k[c][...] = f[:, :N].reshape(5, 4, E, N)
        if channels == 4:
            strip = f[:, N:] if strip is None else strip + f[:, N:]
        north(c)
        if c:
            depth(c - 1)
    if channels == 4:
        north(3)
        k[3][...] = strip.reshape(5, 4, E, N)
    depth(2)
    if channels == 4:
        depth(3)


def prepare_kernel(
    d_in, v_in, m_in, r_in, re_ref, rw_ref, n_ref, s_ref, cn_ref, cs_ref, sel_ref, qw_ref, grad_ref, back_ref,
    d0, d1, d2, d3, v0, v1, v2, v3, mn_ref, di_ref, ce_ref, ai_ref, as_ref,
    k0, k1, k2, k3, n0, n1, n2, n3, mod_ref,
):
    d_ref, v_ref = (d0, d1, d2, d3), (v0, v1, v2, v3)
    f = lambda a: float(np.float32(a))
    shape = (E, N)
    ew = east_weight(shape)
    lane = lane_ids(shape)

    def ext(own, at, j, north=n_ref, south=s_ref):
        halo = (*at, pl.ds(j, 4, stride=4), slice(None))
        return jnp.concatenate([own(j), north[halo], south[halo]], axis=0)

    for z in range(5):
        for j in range(4):
            own = lambda ref, *at: lambda j: ref[(*at, pl.ds(j, 32, stride=4), slice(None))]
            xe = ext(own(re_ref, z), (2, z), j, cn_ref, cs_ref)
            xw = ext(own(rw_ref, z), (3, z), j, cn_ref, cs_ref)

            def strip(src, step):
                out = None
                for c in range(3):
                    p = lane_move(xe, 32 * c - src - step * c, 32 * c)
                    p = p + lane_move(xw, 32 * c + 16 - src - step * c, 32 * c + 16)
                    out = p if out is None else out + p
                return out

            v_all, d_all = [], []
            for c in range(3):
                d_all.append(ext(own(d_in, c, z), (c, z), j))
                v_all.append(ext(own(v_in, c, z), (3 + c, z), j))
            d_all.append(strip(0, 16))
            v_all.append(strip(48, 16))
            for ch in range(4):
                v_ref[ch][z, j] = v_all[ch]
                d_ref[ch][z, j] = d_all[ch] + DT * v_all[ch]
            mods = [ext(own(m_in, z), (0, z), j, cn_ref, cs_ref), strip(96, 0)]
            rhos = [ext(own(r_in, z), (1, z), j, cn_ref, cs_ref), jnp.where(lane < 96, strip(112, 0), 1.0)]
            for m in range(2):
                mod_ref[m, z, j] = mods[m]
                mn = 0.5 * mods[m] * ew
                mn_ref[m, z, j] = mn
                if j == 0:
                    mn_ref[m, z, 4] = pltpu.roll(mn, E - 1, 0)
                nd = f(PERIODIC[j]) * f(W[z])
                di_ref[m, z, j] = DT / (0.125 * rhos[m] * ew * nd)
                if z == 0:
                    area = 0.25 * ew * f(PERIODIC[j])
                    ai_ref[m, j] = area * jnp.sqrt(rhos[m] * mods[m])
                    as_ref[m, j] = area * (0.5 * mods[m])
    for z in range(5):
        x = jnp.concatenate(
            [mod_ref[0, z].reshape(4 * E, N), mod_ref[1, z].reshape(4 * E, N)], axis=1
        )
        hi = x.astype(BF16)
        x = x - hi.astype(F32)
        mid, lo = split2(x)
        c = dot(hi, sel_ref[...]) + dot(mid, sel_ref[...]) + dot(lo, sel_ref[...])
        c = c * (qw_ref[...] * f(W[z]))
        for j in range(4):
            at = (z * 4 + j) * E
            ce_ref[at : at + E, :] = c[j * E : j * E + E] * f(PERIODIC[j])

    def emit(ch, j, z, d, k):
        m = ch // 3
        v = v_ref[ch][z, j]
        if z == 0:
            k = k + ai_ref[m, j] * v + as_ref[m, j] * d
        v_ref[ch][z, j] = v - di_ref[m, z, j] * k

    line_forces(
        d_ref, (k0, k1, k2, k3), (n0, n1, n2, n3), mn_ref, ce_ref, grad_ref, back_ref, 4, emit
    )


def prepare(d, v, m, r, re, rw, rn, rs, cn, cs, tables):
    grad, back, sel, qw = tables
    whole = pl.BlockSpec(memory_space=pltpu.VMEM)
    state = jax.ShapeDtypeStruct((5, 4, E, N), F32)
    return pl.pallas_call(
        prepare_kernel,
        in_specs=[whole] * 14,
        out_specs=[whole] * 13,
        out_shape=[
            *[state] * 8,
            jax.ShapeDtypeStruct((2, 5, 5, E, N), F32),
            jax.ShapeDtypeStruct((2, 5, 4, E, N), F32),
            jax.ShapeDtypeStruct((5 * 4 * E, 256), F32),
            jax.ShapeDtypeStruct((2, 4, E, N), F32),
            jax.ShapeDtypeStruct((2, 4, E, N), F32),
        ],
        scratch_shapes=[pltpu.VMEM((5, 4, E, N), F32)] * 8 + [pltpu.VMEM((2, 5, 4, E, N), F32)],
        compiler_params=pltpu.CompilerParams(vmem_limit_bytes=VMEM_LIMIT),
        name="prepare",
    )(d, v, m, r, re, rw, rn, rs, cn, cs, sel, qw, grad, back)


def steps_kernel(
    i0, i1, i2, i3, u0, u1, u2, u3, mn_ref, di_ref, ce_ref, ai_ref, as_ref,
    b_ref, bs_ref, bn_ref, bo_ref, grad_ref, back_ref,
    dout_ref, vout_ref,
    d0, d1, d2, d3, v0, v1, v2, v3, k0, k1, k2, k3, n0, n1, n2, n3, f_ref,
):
    d_in, v_in = (i0, i1, i2, i3), (u0, u1, u2, u3)
    d_ref, v_ref = (d0, d1, d2, d3), (v0, v1, v2, v3)
    k_ref, kn_ref = (k0, k1, k2, k3), (n0, n1, n2, n3)
    for t in range(3):
        n, at = FORCE_ROWS[t]
        gap = jnp.zeros((8 - n // 2, N), F32)
        for ch in range(4):
            for j in range(4):
                own = pl.ds(j, 32, stride=4)
                x = b_ref[t, ch, own, :] if ch < 3 else bs_ref[t, own, :]
                halo = pl.ds(at + j, n // 4, stride=4)
                f_ref[t, ch, j] = jnp.concatenate(
                    [x, bn_ref[ch, halo, :], gap, bo_ref[ch, halo, :]], axis=0
                )
    for ch in range(3):
        for j in range(4):
            x = b_ref[3, ch, pl.ds(j, 32, stride=4), :]
            f_ref[3, ch, j] = jnp.concatenate([x, jnp.zeros((8, N), F32)], axis=0)

    for ch in range(4):
        for j in range(4):
            for z in range(5):
                v = v_in[ch][z, j]
                if z == 0:
                    v = v + di_ref[ch // 3, z, j] * f_ref[0, ch, j]
                v_ref[ch][z, j] = v
                d_ref[ch][z, j] = d_in[ch][z, j] + DT * v

    def velocity(t, ch, j, z, d, k):
        m = ch // 3
        v = v_ref[ch][z, j]
        if z == 0:
            k = k + ai_ref[m, j] * v + as_ref[m, j] * d - f_ref[t, ch, j]
        return v - di_ref[m, z, j] * k

    def step(t, carry):
        def emit(ch, j, z, d, k):
            v = velocity(t, ch, j, z, d, k)
            v_ref[ch][z, j] = v
            d_ref[ch][z, j] = d + DT * v

        line_forces(d_ref, k_ref, kn_ref, mn_ref, ce_ref, grad_ref, back_ref, 4, emit)
        return carry

    lax.fori_loop(1, 3, step, 0)

    def final(ch, j, z, d, k):
        dout_ref[ch, z, pl.ds(j, 32, stride=4), :] = d[:32]
        vout_ref[ch, z, pl.ds(j, 32, stride=4), :] = velocity(3, ch, j, z, d, k)[:32]

    line_forces(d_ref, k_ref, kn_ref, mn_ref, ce_ref, grad_ref, back_ref, 3, final)


def steps(prepared, b, bs, bn, bo, tables):
    grad, back = tables[:2]
    whole = pl.BlockSpec(memory_space=pltpu.VMEM)
    return pl.pallas_call(
        steps_kernel,
        in_specs=[whole] * 19,
        out_specs=[whole] * 2,
        out_shape=[jax.ShapeDtypeStruct((3, 5, N, N), F32)] * 2,
        scratch_shapes=[pltpu.VMEM((5, 4, E, N), F32)] * 16 + [pltpu.VMEM((4, 4, 4, E, N), F32)],
        compiler_params=pltpu.CompilerParams(vmem_limit_bytes=VMEM_LIMIT),
        name="steps",
    )(*prepared, b, bs, bn, bo, grad, back)


def local(displacement, velocity, modulus, density, traces, record_row):
    tables = tuple(jnp.asarray(t) for t in east_tables())
    west, east, north, south, late_north, late_south = strips(
        displacement, velocity, modulus, density
    )
    from_east = shifted(west, "reg", -1)
    from_west = shifted(east, "reg", 1)
    from_north = shifted(south, "src", -1)
    from_south = shifted(north, "src", 1)
    rows = record_row.reshape(N, 1, STEPS).astype(F32)
    rows = jnp.pad(rows, ((0, 0), (0, STEPS - 1), (0, N - STEPS)))
    records = jnp.transpose(traces[0], (1, 0, 2)).reshape(9, N, STEPS, N)
    sent = pack(records, rows)
    arrived = lax.all_to_all(sent, ("src", "reg"), split_axis=0, concat_axis=0, tiled=True)
    arrived = arrived.reshape(N, 40, N)
    corner = jnp.stack([from_east, from_west])
    late_south = jnp.concatenate([late_south, corner[:, :, :H]], axis=0)
    late_north = jnp.concatenate([late_north, corner[:, :, N - H :]], axis=0)
    corner_north = shifted(late_south, "src", -1)
    corner_south = shifted(late_north, "src", 1)
    b, b_west, b_east = place(arrived, modulus, density)
    b_from_east = shifted(b_west, "reg", -1)
    b_from_west = shifted(b_east, "reg", 1)
    from_north, from_south, corner_north, corner_south, _ = lax.optimization_barrier(
        (from_north, from_south, corner_north, corner_south, b)
    )
    prepared = prepare(
        displacement, velocity, modulus, density, from_east, from_west,
        from_north, from_south, corner_north, corner_south, tables,
    )
    b_strip, b_north, b_south = force_rows(b, b_from_east, b_from_west)
    b_from_south = shifted(b_north, "src", 1)
    b_from_north = shifted(b_south, "src", -1)
    return steps(prepared, b, b_strip, b_from_north, b_from_south, tables)


def solution(mesh):
    state = P(None, None, "src", "reg")
    field = P(None, "src", "reg")
    in_specs = (state, state, field, field, P(("src", "reg"), None, None, None), P(("src", "reg"), None))
    return jax.shard_map(local, mesh=mesh, in_specs=in_specs, out_specs=(state, state), check_vma=False)
```

profile of v0, /device:TPU:1, one launch (start us, length us, event | category | flops | bytes accessed | tf_op | source)
XLA Modules:
  0.0 101.4 jit_solution(2068515278246937485)
XLA Ops:
  0.6 0.7 convert_reduce_fusion
  1.3 0.1 convert_element_type.17
  1.4 0.8 pad.4.id_ref
  2.2 3.0 %pack.1 = f32[128,10,4,128]{3,2,1,0:T(4,128)} custom-call(f32[9,128,4,128]{3,2,1,0:T(4,128)} %bitcast.12, f32[128,4,128]{2,1,0:T(4,128)} %pad.4.id_ref), custom_call_target="tpu_custom_call" | custom-call | tf_op jit(solution)/shard_map/pack/pallas_call | solution.py:148
  5.2 11.5 %all-to-all-start = ((f32[128,10,4,128]{3,2,1,0:T(4,128)}), f32[128,10,4,128]{3,2,1,0:T(4,128)S(1)}, u32[]{:S(2)}, u32[]{:S(2)}) async-start(f32[128,10,4,128]{3,2,1,0:T(4,128)} %pack.1), calls=%async_computation | async-start | bytes 5242880 | tf_op jit(solution)/shard_map/all_to_all | solution.py:578
  16.7 3.7 %strips.1 = (f32[5,128,128]{2,1,0:T(8,128)}, f32[5,128,128]{2,1,0:T(8,128)}, f32[6,5,16,128]{3,2,1,0:T(8,128)}, f32[6,5,16,128]{3,2,1,0:T(8,128)}, f32[2,5,16,128]{3,2,1,0:T(8,128)}, /*index=5*/f32[2,5,16,128]{3,2,1,0:T(8,128)}) custom-call(f32[3,5,128,128]{3,2,1,0:T(8,128)} %d_in.1, f32[3,5,128,128]{3,2,1,0:T(8,128)} %v_in.1, f32[5,128,128]{2,1,0:T(8,128)} %m_in.1, ...), custom_call_target="tpu_custom_call" | custom-call | tf_op jit(solution)/shard_map/strips/pallas_call | solution.py:213
  20.4 1.1 %collective-permute-start = (f32[5,128,128]{2,1,0:T(8,128)}, f32[5,128,128]{2,1,0:T(8,128)S(1)}, u32[]{:S(2)}, u32[]{:S(2)}) collective-permute-start(f32[5,128,128]{2,1,0:T(8,128)} %get-tuple-element.31), channel_id=1, source_target_pairs={{1,0},{2,1},{3,2},{4,3},{5,4},{6,5},{7,6},{8,7},{9,8},{10,9},{11,1... | collective-permute-start | bytes 983048 | tf_op jit(solution)/shard_map/ppermute | solution.py:89
  21.6 0.7 collective-permute-start.1
  22.2 31.1 %all-to-all-done = f32[128,10,4,128]{3,2,1,0:T(4,128)S(1)} async-done(((f32[128,10,4,128]{3,2,1,0:T(4,128)}), f32[128,10,4,128]{3,2,1,0:T(4,128)S(1)}, u32[]{:S(2)}, u32[]{:S(2)}) %all-to-all-start) | async-done | bytes 2621472 | tf_op jit(solution)/shard_map/all_to_all | solution.py:578
  53.3 0.0 copy-start.2
  53.3 0.0 copy-start.3
  53.3 0.0 copy-start.4
  53.4 0.0 copy-start.5
  53.4 0.0 copy-start.6
  53.4 0.0 copy-start.7
  53.4 4.2 %place.1 = (f32[4,3,128,128]{3,2,1,0:T(8,128)S(1)}, f32[3,128,128]{2,1,0:T(8,128)S(1)}, f32[3,128,128]{2,1,0:T(8,128)S(1)}) custom-call(f32[128,40,128]{2,1,0:T(8,128)S(1)} %bitcast.9, f32[5,128,128]{2,1,0:T(8,128)} %m_in.1, f32[5,128,128]{2,1,0:T(8,128)} %r_in.1), custom_call_target="tpu_custom_call" | custom-call | tf_op jit(solution)/shard_map/place/pallas_call | solution.py:297
  57.6 1.5 %collective-permute-start.6 = (f32[3,128,128]{2,1,0:T(8,128)S(1)}, f32[3,128,128]{2,1,0:T(8,128)S(1)}, u32[]{:S(2)}, u32[]{:S(2)}) collective-permute-start(f32[3,128,128]{2,1,0:T(8,128)S(1)} %get-tuple-element.55), channel_id=1, source_target_pairs={{1,0},{2,1},{3,2},{4,3},{5,4},{6,5},{7,6},{8,7},{9,8},{10,9},{11,1... | collective-permute-start | bytes 589832 | tf_op jit(solution)/shard_map/ppermute | solution.py:89
  59.1 0.7 collective-permute-start.2
  59.7 2.3 %collective-permute-start.3 = (f32[6,5,16,128]{3,2,1,0:T(8,128)S(1)}, f32[6,5,16,128]{3,2,1,0:T(8,128)S(1)}, u32[]{:S(2)}, u32[]{:S(2)}) collective-permute-start(f32[6,5,16,128]{3,2,1,0:T(8,128)S(1)} %copy-done.10), channel_id=1, source_target_pairs={{112,0},{0,16},{16,32},{32,48},{48,64},{64,80},{80,96},{96,112},{1... | collective-permute-start | bytes 737288 | tf_op jit(solution)/shard_map/ppermute | solution.py:89
  62.1 0.0 collective-permute-done.re_ref
  62.1 0.9 collective-permute-start.7
  62.9 0.0 collective-permute-done.1.rw_ref
  63.0 1.6 %collective-permute-start.5 = (f32[4,5,16,128]{3,2,1,0:T(8,128)S(1)}, f32[4,5,16,128]{3,2,1,0:T(8,128)S(1)}, u32[]{:S(2)}, u32[]{:S(2)}) collective-permute-start(f32[4,5,16,128]{3,2,1,0:T(8,128)S(1)} %get-tuple-element.60), channel_id=1, source_target_pairs={{112,0},{0,16},{16,32},{32,48},{48,64},{64,80},{80,96},{96,112},{1... | collective-permute-start | bytes 491528 | tf_op jit(solution)/shard_map/ppermute | solution.py:89
  64.6 0.1 collective-permute-done.6.e_ref
  64.7 3.4 %collective-permute-start.4 = (f32[4,5,16,128]{3,2,1,0:T(8,128)S(1)}, f32[4,5,16,128]{3,2,1,0:T(8,128)S(1)}, u32[]{:S(2)}, u32[]{:S(2)}) collective-permute-start(f32[4,5,16,128]{3,2,1,0:T(8,128)S(1)} %get-tuple-element.61), channel_id=1, source_target_pairs={{16,0},{32,16},{48,32},{64,48},{80,64},{96,80},{112,96},{0,112},{1... | collective-permute-start | bytes 491528 | tf_op jit(solution)/shard_map/ppermute | solution.py:89
  68.1 6.9 %collective-permute-done.7.w_ref = f32[3,128,128]{2,1,0:T(8,128)S(1)} collective-permute-done((f32[3,128,128]{2,1,0:T(8,128)S(1)}, f32[3,128,128]{2,1,0:T(8,128)S(1)}, u32[]{:S(2)}, u32[]{:S(2)}) %collective-permute-start.7) | collective-permute-done | bytes 196640 | tf_op jit(solution)/shard_map/ppermute | solution.py:89
  75.0 2.4 %collective-permute-start.8 = (f32[4,24,128]{2,1,0:T(8,128)S(1)}, f32[4,24,128]{2,1,0:T(8,128)S(1)}, u32[]{:S(2)}, u32[]{:S(2)}) collective-permute-start(f32[4,24,128]{2,1,0:T(8,128)S(1)} %get-tuple-element.58), channel_id=1, source_target_pairs={{16,0},{32,16},{48,32},{64,48},{80,64},{96,80},{112,96},{0,112},{1... | collective-permute-start | bytes 147464 | tf_op jit(solution)/shard_map/ppermute | solution.py:89
  77.4 0.7 collective-permute-start.9
  78.1 3.2 %collective-permute-done.5.cs_ref = f32[4,5,16,128]{3,2,1,0:T(8,128)S(1)} collective-permute-done((f32[4,5,16,128]{3,2,1,0:T(8,128)S(1)}, f32[4,5,16,128]{3,2,1,0:T(8,128)S(1)}, u32[]{:S(2)}, u32[]{:S(2)}) %collective-permute-start.5) | collective-permute-done | bytes 163872 | tf_op jit(solution)/shard_map/ppermute | solution.py:89
  81.2 2.0 %collective-permute-done.4.cn_ref = f32[4,5,16,128]{3,2,1,0:T(8,128)S(1)} collective-permute-done((f32[4,5,16,128]{3,2,1,0:T(8,128)S(1)}, f32[4,5,16,128]{3,2,1,0:T(8,128)S(1)}, u32[]{:S(2)}, u32[]{:S(2)}) %collective-permute-start.4) | collective-permute-done | bytes 163872 | tf_op jit(solution)/shard_map/ppermute | solution.py:89
  83.3 5.4 %prepare.1 = (f32[5,4,40,128]{3,2,1,0:T(8,128)S(1)}, f32[5,4,40,128]{3,2,1,0:T(8,128)S(1)}, f32[5,4,40,128]{3,2,1,0:T(8,128)S(1)}, f32[5,4,40,128]{3,2,1,0:T(8,1...) custom-call(f32[3,5,128,128]{3,2,1,0:T(8,128)S(1)} %copy-done, ...), custom_call_target="tpu_custom_call" | custom-call | tf_op jit(solution)/shard_map/prepare/pallas_call | solution.py:474
  88.7 12.8 %steps.1 = (f32[3,5,128,128]{3,2,1,0:T(8,128)}, f32[3,5,128,128]{3,2,1,0:T(8,128)}) custom-call(f32[5,4,40,128]{3,2,1,0:T(8,128)S(1)} %get-tuple-element.42.i0, f32[5,4,40,128]{3,2,1,0:T(8,128)S(1)} %get-tuple-element.43.i1, f32[5,4,40,128]{3,2,1,0:T(8,128)S(1)} %get-tuple-element.44.i2, f32[5,4,40,128]{3,2,1,0:T(8,128)S(1)} %get-tuple-element.45.i3, ...), custom_call_target="tpu_custom_call" | custom-call | tf_op jit(solution)/shard_map/steps/pallas_call | solution.py:554
  (24 shorter events, 0.1 us)
Async XLA Ops:
  5.2 48.1 %all-to-all-start = ((f32[128,10,4,128]{3,2,1,0:T(4,128)}), f32[128,10,4,128]{3,2,1,0:T(4,128)S(1)}, u32[]{:S(2)}, u32[]{:S(2)}) async-start(f32[128,10,4,128]{3,2,1,0:T(4,128)} %pack.1), calls=%async_computation | async-start | bytes 5242880 | tf_op jit(solution)/shard_map/all_to_all | solution.py:578
  20.4 42.5 %copy-start.8 = (f32[2,5,16,128]{3,2,1,0:T(8,128)S(1)}, f32[2,5,16,128]{3,2,1,0:T(8,128)}, u32[]{:S(2)}) copy-start(f32[2,5,16,128]{3,2,1,0:T(8,128)} %get-tuple-element.36) | copy-start | bytes 245764
  20.4 42.5 %copy-start.9 = (f32[2,5,16,128]{3,2,1,0:T(8,128)S(1)}, f32[2,5,16,128]{3,2,1,0:T(8,128)}, u32[]{:S(2)}) copy-start(f32[2,5,16,128]{3,2,1,0:T(8,128)} %get-tuple-element.35) | copy-start | bytes 245764
  20.4 41.6 %collective-permute-start = (f32[5,128,128]{2,1,0:T(8,128)}, f32[5,128,128]{2,1,0:T(8,128)S(1)}, u32[]{:S(2)}, u32[]{:S(2)}) collective-permute-start(f32[5,128,128]{2,1,0:T(8,128)} %get-tuple-element.31), channel_id=1, source_target_pairs={{1,0},{2,1},{3,2},{4,3},{5,4},{6,5},{7,6},{8,7},{9,8},{10,9},{11,1... | collective-permute-start | bytes 983048 | tf_op jit(solution)/shard_map/ppermute | solution.py:89
  21.6 41.4 %collective-permute-start.1 = (f32[5,128,128]{2,1,0:T(8,128)}, f32[5,128,128]{2,1,0:T(8,128)S(1)}, u32[]{:S(2)}, u32[]{:S(2)}) collective-permute-start(f32[5,128,128]{2,1,0:T(8,128)} %get-tuple-element.32), channel_id=1, source_target_pairs={{15,0},{0,1},{1,2},{2,3},{3,4},{4,5},{5,6},{6,7},{7,8},{8,9},{9,10... | collective-permute-start | bytes 983048 | tf_op jit(solution)/shard_map/ppermute | solution.py:89
  53.3 5.8 %copy-start.11 = (f32[6,5,16,128]{3,2,1,0:T(8,128)S(1)}, f32[6,5,16,128]{3,2,1,0:T(8,128)}, u32[]{:S(2)}) copy-start(f32[6,5,16,128]{3,2,1,0:T(8,128)} %get-tuple-element.33) | copy-start | bytes 737284
  53.3 6.4 %copy-start.10 = (f32[6,5,16,128]{3,2,1,0:T(8,128)S(1)}, f32[6,5,16,128]{3,2,1,0:T(8,128)}, u32[]{:S(2)}) copy-start(f32[6,5,16,128]{3,2,1,0:T(8,128)} %get-tuple-element.34) | copy-start | bytes 737284
  53.3 29.9 %copy-start = (f32[3,5,128,128]{3,2,1,0:T(8,128)S(1)}, f32[3,5,128,128]{3,2,1,0:T(8,128)}, u32[]{:S(2)}) copy-start(f32[3,5,128,128]{3,2,1,0:T(8,128)} %d_in.1) | copy-start | bytes 2949124
  53.3 29.9 %copy-start.1 = (f32[3,5,128,128]{3,2,1,0:T(8,128)S(1)}, f32[3,5,128,128]{3,2,1,0:T(8,128)}, u32[]{:S(2)}) copy-start(f32[3,5,128,128]{3,2,1,0:T(8,128)} %v_in.1) | copy-start | bytes 2949124
  53.3 29.9 %copy-start.2 = (bf16[3,2,256,256]{3,2,1,0:T(8,128)(2,1)S(1)}, bf16[3,2,256,256]{3,2,1,0:T(8,128)(2,1)}, u32[]{:S(2)}) copy-start(bf16[3,2,256,256]{3,2,1,0:T(8,128)(2,1)} %constant.12.clone.back_ref) | copy-start | bytes 2359300
  53.3 29.9 %copy-start.3 = (bf16[3,2,256,256]{3,2,1,0:T(8,128)(2,1)S(1)}, bf16[3,2,256,256]{3,2,1,0:T(8,128)(2,1)}, u32[]{:S(2)}) copy-start(bf16[3,2,256,256]{3,2,1,0:T(8,128)(2,1)} %constant.11.clone.grad_ref) | copy-start | bytes 2359300
  53.3 29.9 %copy-start.4 = (f32[5,128,128]{2,1,0:T(8,128)S(1)}, f32[5,128,128]{2,1,0:T(8,128)}, u32[]{:S(2)}) copy-start(f32[5,128,128]{2,1,0:T(8,128)} %m_in.1) | copy-start | bytes 983044
  53.4 29.9 %copy-start.5 = (f32[5,128,128]{2,1,0:T(8,128)S(1)}, f32[5,128,128]{2,1,0:T(8,128)}, u32[]{:S(2)}) copy-start(f32[5,128,128]{2,1,0:T(8,128)} %r_in.1) | copy-start | bytes 983044
  53.4 29.9 %copy-start.6 = (bf16[256,256]{1,0:T(8,128)(2,1)S(1)}, bf16[256,256]{1,0:T(8,128)(2,1)}, u32[]{:S(2)}) copy-start(bf16[256,256]{1,0:T(8,128)(2,1)} %constant.13.clone.sel_ref) | copy-start | bytes 393220
  53.4 29.9 %copy-start.7 = (f32[1,256]{1,0:T(1,128)S(1)}, f32[1,256]{1,0:T(1,128)}, u32[]{:S(2)}) copy-start(f32[1,256]{1,0:T(1,128)} %constant.14.clone.qw_ref) | copy-start | bytes 3076
  57.6 7.1 %collective-permute-start.6 = (f32[3,128,128]{2,1,0:T(8,128)S(1)}, f32[3,128,128]{2,1,0:T(8,128)S(1)}, u32[]{:S(2)}, u32[]{:S(2)}) collective-permute-start(f32[3,128,128]{2,1,0:T(8,128)S(1)} %get-tuple-element.55), channel_id=1, source_target_pairs={{1,0},{2,1},{3,2},{4,3},{5,4},{6,5},{7,6},{8,7},{9,8},{10,9},{11,1... | collective-permute-start | bytes 589832 | tf_op jit(solution)/shard_map/ppermute | solution.py:89
  59.1 18.3 %collective-permute-start.2 = (f32[6,5,16,128]{3,2,1,0:T(8,128)S(1)}, f32[6,5,16,128]{3,2,1,0:T(8,128)S(1)}, u32[]{:S(2)}, u32[]{:S(2)}) collective-permute-start(f32[6,5,16,128]{3,2,1,0:T(8,128)S(1)} %copy-done.11), channel_id=1, source_target_pairs={{16,0},{32,16},{48,32},{64,48},{80,64},{96,80},{112,96},{0,112},{1... | collective-permute-start | bytes 737288 | tf_op jit(solution)/shard_map/ppermute | solution.py:89
  59.7 18.3 %collective-permute-start.3 = (f32[6,5,16,128]{3,2,1,0:T(8,128)S(1)}, f32[6,5,16,128]{3,2,1,0:T(8,128)S(1)}, u32[]{:S(2)}, u32[]{:S(2)}) collective-permute-start(f32[6,5,16,128]{3,2,1,0:T(8,128)S(1)} %copy-done.10), channel_id=1, source_target_pairs={{112,0},{0,16},{16,32},{32,48},{48,64},{64,80},{80,96},{96,112},{1... | collective-permute-start | bytes 737288 | tf_op jit(solution)/shard_map/ppermute | solution.py:89
  62.1 12.9 %collective-permute-start.7 = (f32[3,128,128]{2,1,0:T(8,128)S(1)}, f32[3,128,128]{2,1,0:T(8,128)S(1)}, u32[]{:S(2)}, u32[]{:S(2)}) collective-permute-start(f32[3,128,128]{2,1,0:T(8,128)S(1)} %get-tuple-element.56), channel_id=1, source_target_pairs={{15,0},{0,1},{1,2},{2,3},{3,4},{4,5},{5,6},{6,7},{7,8},{8,9},{9,10... | collective-permute-start | bytes 589832 | tf_op jit(solution)/shard_map/ppermute | solution.py:89
  63.0 18.3 %collective-permute-start.5 = (f32[4,5,16,128]{3,2,1,0:T(8,128)S(1)}, f32[4,5,16,128]{3,2,1,0:T(8,128)S(1)}, u32[]{:S(2)}, u32[]{:S(2)}) collective-permute-start(f32[4,5,16,128]{3,2,1,0:T(8,128)S(1)} %get-tuple-element.60), channel_id=1, source_target_pairs={{112,0},{0,16},{16,32},{32,48},{48,64},{64,80},{80,96},{96,112},{1... | collective-permute-start | bytes 491528 | tf_op jit(solution)/shard_map/ppermute | solution.py:89
  64.7 18.5 %collective-permute-start.4 = (f32[4,5,16,128]{3,2,1,0:T(8,128)S(1)}, f32[4,5,16,128]{3,2,1,0:T(8,128)S(1)}, u32[]{:S(2)}, u32[]{:S(2)}) collective-permute-start(f32[4,5,16,128]{3,2,1,0:T(8,128)S(1)} %get-tuple-element.61), channel_id=1, source_target_pairs={{16,0},{32,16},{48,32},{64,48},{80,64},{96,80},{112,96},{0,112},{1... | collective-permute-start | bytes 491528 | tf_op jit(solution)/shard_map/ppermute | solution.py:89
  75.0 13.6 %collective-permute-start.8 = (f32[4,24,128]{2,1,0:T(8,128)S(1)}, f32[4,24,128]{2,1,0:T(8,128)S(1)}, u32[]{:S(2)}, u32[]{:S(2)}) collective-permute-start(f32[4,24,128]{2,1,0:T(8,128)S(1)} %get-tuple-element.58), channel_id=1, source_target_pairs={{16,0},{32,16},{48,32},{64,48},{80,64},{96,80},{112,96},{0,112},{1... | collective-permute-start | bytes 147464 | tf_op jit(solution)/shard_map/ppermute | solution.py:89
  77.4 11.3 %collective-permute-start.9 = (f32[4,24,128]{2,1,0:T(8,128)S(1)}, f32[4,24,128]{2,1,0:T(8,128)S(1)}, u32[]{:S(2)}, u32[]{:S(2)}) collective-permute-start(f32[4,24,128]{2,1,0:T(8,128)S(1)} %get-tuple-element.59), channel_id=1, source_target_pairs={{112,0},{0,16},{16,32},{32,48},{48,64},{64,80},{80,96},{96,112},{1... | collective-permute-start | bytes 147464 | tf_op jit(solution)/shard_map/ppermute | solution.py:89
where the time goes:
time: 102 us; the launch traced here: 101 us
  waiting for transfers between devices  43.2 us (42%)
  Pallas kernels  29.1 us (29%)
  starting transfers between devices  26.7 us (26%)
    all_to_all x1, waiting for transfers between devices, local(): lax.all_to_all(sent, ('src', 'reg'), split_axis=0, concat_axis=0, tiled=T...  31.1 us
    ppermute x10, starting transfers between devices, shifted(): lax.ppermute(block, axis, [((i - distance) % n, i) for i in range(n)])  15.2 us
    pallas_call x1, Pallas kernels, steps(): pl.pallas_call(steps_kernel, in_specs=[whole] * 19, out_specs=[whole] * 2...  12.8 us
    ppermute x10, waiting for transfers between devices, shifted(): lax.ppermute(block, axis, [((i - distance) % n, i) for i in range(n)])  12.1 us
    all_to_all x1, starting transfers between devices, local(): lax.all_to_all(sent, ('src', 'reg'), split_axis=0, concat_axis=0, tiled=T...  11.5 us
    pallas_call x1, Pallas kernels, prepare(): pl.pallas_call(prepare_kernel, in_specs=[whole] * 14, out_specs=[whole] *...  5.4 us
    pallas_call x1, Pallas kernels, place(): pl.pallas_call(place_kernel, in_specs=[whole, hbm, hbm], out_specs=[whole...  4.18 us
    pallas_call x1, Pallas kernels, strips(): pl.pallas_call(strips_kernel, in_specs=[hbm] * 4, out_specs=[hbm] * 6, ou...  3.7 us
  transfers between devices with their start and end apart: 11, of which 5 were waited for; matrix products, arithmetic and copies ran while one was open for 0% of the time, Pallas kernels for 13%

commit v1 on v0

v1 whole, which is shorter than its diff:
```python
import math

import jax
import jax.numpy as jnp
import numpy as np
from jax import lax
from jax.experimental import pallas as pl
from jax.experimental.pallas import tpu as pltpu
from jax.sharding import PartitionSpec as P


F32 = jnp.float32
BF16 = jnp.bfloat16
STEPS = 4
DT = 0.02
N = 128
H = 16
E = 40
FORCE_ROWS = ((12, 0), (8, 12), (4, 20))
VMEM_LIMIT = 28 * 1024 * 1024


def gll():
    inner = math.sqrt(3.0 / 7.0)
    x = np.array([-1.0, -inner, 0.0, inner, 1.0])
    w = np.array([0.1, 49.0 / 90.0, 32.0 / 45.0, 49.0 / 90.0, 0.1])
    leg = (35.0 * x**4 - 30.0 * x**2 + 3.0) / 8.0
    d = np.zeros((5, 5))
    for i in range(5):
        for j in range(5):
            if i != j:
                d[i, j] = leg[i] / (leg[j] * (x[i] - x[j]))
    d[0, 0] = -5.0
    d[4, 4] = 5.0
    return d, w


DER, W = gll()
BACK = (DER * W[:, None]).T
PERIODIC = [2 * W[0], W[1], W[2], W[3]]


def apply5(m, v):
    s0, s1, m0, m1 = v[0] + v[4], v[1] + v[3], v[0] - v[4], v[1] - v[3]
    f = lambda a: float(np.float32(a))
    out = [None] * 5
    for i in (0, 1):
        p = f((m[i, 0] - m[i, 4]) / 2) * m0 + f((m[i, 1] - m[i, 3]) / 2) * m1
        q = f((m[i, 0] + m[i, 4]) / 2) * s0 + f((m[i, 1] + m[i, 3]) / 2) * s1 + f(m[i, 2]) * v[2]
        out[i], out[4 - i] = p + q, p - q
    out[2] = f(m[2, 0]) * m0 + f(m[2, 1]) * m1
    return out


def column_of(x, comp):
    if 0 <= x < N:
        return x
    return N + 32 * comp + (x - N if x >= N else x + 32)


def east_tables():
    grad = np.zeros((3, 256, 256))
    sel = np.zeros((256, 256))
    weight = np.zeros((1, 256))
    for k in range(E):
        for i in range(5):
            q = i * E + k
            xi = 4 * (k - 4) + i
            weight[0, q] = 0.5 * W[i]
            if xi < N + H:
                sel[column_of(xi, 0), q] = 1.0
            for comp in range(3):
                for j in range(5):
                    xj = 4 * (k - 4) + j
                    if xj < N + H:
                        grad[comp, column_of(xj, comp), q] = DER[i, j]

    def two(a):
        hi = a.astype(np.float32).astype(jnp.bfloat16)
        lo = (a - hi.astype(np.float64)).astype(np.float32).astype(jnp.bfloat16)
        return np.stack([hi, lo], axis=1)

    back = np.ascontiguousarray(np.swapaxes(grad, 1, 2))
    return two(grad), two(back), sel.astype(jnp.bfloat16), weight.astype(np.float32)


def shifted(block, axis, distance):
    n = lax.axis_size(axis)
    return lax.ppermute(block, axis, [((i - distance) % n, i) for i in range(n)])


def in_hbm(*arrays):
    return [pltpu.with_memory_space_constraint(x, pltpu.HBM) for x in arrays]


def dot(a, b):
    return jnp.dot(a, b, preferred_element_type=F32)


def split2(x):
    hi = x.astype(BF16)
    return hi, (x - hi.astype(F32)).astype(BF16)


def lane_ids(shape):
    return lax.broadcasted_iota(jnp.int32, shape, len(shape) - 1)


def east_weight(shape):
    r = lane_ids(shape) % 4
    f = lambda a: float(np.float32(a))
    return jnp.where(r == 0, f(PERIODIC[0]), jnp.where(r == 2, f(PERIODIC[2]), f(PERIODIC[1])))


def lane_move(x, shift, start, width=16):
    shift %= 128
    y = pltpu.roll(x, shift, x.ndim - 1) if shift else x
    lane = lane_ids(x.shape)
    return jnp.where((lane >= start) & (lane < start + width), y, 0.0)


WEST_GROUPS = ((0, 12, 116, 0), (12, 8, 120, 1), (20, 4, 124, 2))
EAST_GROUPS = ((24, 9, 0, 0), (33, 5, 0, 1), (38, 1, 0, 2))


def begin_kernel(
    d_ref, v_ref, m_ref, r_ref, tr_ref, id_ref,
    west_ref, east_ref, north_ref, south_ref, ln_ref, ls_ref, sent_ref,
    buf, west_buf, east_buf, tr_buf, sent_buf, id_buf, in_sem, row_sem, out_sem, tr_sem, sent_sem,
):
    copy = pltpu.make_async_copy
    loads = []
    for z in range(5):
        loads.append(
            [
                copy(d_ref.at[:, z], buf.at[z, 0:3], in_sem.at[z, 0]),
                copy(v_ref.at[:, z], buf.at[z, 3:6], in_sem.at[z, 1]),
                copy(m_ref.at[z], buf.at[z, 6], in_sem.at[z, 2]),
                copy(r_ref.at[z], buf.at[z, 7], in_sem.at[z, 3]),
            ]
        )
        for c in loads[z]:
            c.start()
    records = []
    for g in range(8):
        at = pl.ds(64 * g, 64)
        records.append(copy(tr_ref.at[:, at], tr_buf.at[:, at], tr_sem.at[g]))
        records[g].start()
    mine = lane_ids((N, 4 * N)) // STEPS == lax.broadcasted_iota(jnp.int32, (N, 4 * N), 0)
    spread = jnp.where(mine, jnp.broadcast_to(id_ref[...].astype(F32), (N, 4 * N)), 0.0).astype(BF16)
    step = lax.broadcasted_iota(jnp.int32, (4 * N, N), 0) % STEPS == lane_ids((4 * N, N))
    id_buf[...] = dot(spread, jnp.where(step, 1.0, 0.0).astype(BF16))
    lane = lane_ids((N, N))
    stores = []
    for z in range(5):
        for c in loads[z]:
            c.wait()
        for i, (at, top, low) in enumerate(
            ((slice(0, 6), north_ref, south_ref), (slice(6, 8), ln_ref, ls_ref))
        ):
            stores.append(copy(buf.at[z, at, N - H : N], top.at[:, z], row_sem.at[z, 2 * i]))
            stores.append(copy(buf.at[z, at, 0:H], low.at[:, z], row_sem.at[z, 2 * i + 1]))
        for c in stores[-4:]:
            c.start()
        west = buf[z, 0]
        east = pltpu.roll(west, N - 112, 1)
        for a in range(1, 8):
            x = buf[z, a]
            west = jnp.where(lane < 16 * a, west, pltpu.roll(x, 16 * a, 1))
            east = jnp.where(
                lane < 16 * a, east, pltpu.roll(x, (16 * a - 112) % N, 1) if a != 7 else x
            )
        west_buf[z] = west
        east_buf[z] = east
        stores.append(copy(west_buf.at[z], west_ref.at[z], out_sem.at[z, 0]))
        stores.append(copy(east_buf.at[z], east_ref.at[z], out_sem.at[z, 1]))
        for c in stores[-2:]:
            c.start()
    lane = lane_ids((16, N))
    for g in range(8):
        records[g].wait()
        first = 640 * g
        for d in range(16):
            for k in range(9):
                sent_buf[pl.ds(first + 40 * d + 4 * k, 4), :] = tr_buf[k, pl.ds(64 * g + 4 * d, 4), :]
        ids = id_buf[16 * g : 16 * g + 16, :]
        ids = (
            ids
            + pltpu.roll(pltpu.roll(ids, 1, 0), 4, 1)
            + pltpu.roll(pltpu.roll(ids, 15, 0), 8, 1)
        )
        extra = [ids]
        for rho in range(3):
            sides = [jnp.zeros((16, N), F32)] * 2
            for c in range(3):
                for t in range(3):
                    x = tr_buf[3 * rho + c, pl.ds(64 * g + t, 16, stride=4), :]
                    for i, groups in enumerate((WEST_GROUPS, EAST_GROUPS)):
                        off, width, col, _ = groups[t]
                        at = 40 * c + off
                        y = pltpu.roll(x, (at - col) % N, 1) if (at - col) % N else x
                        sides[i] = jnp.where((lane >= at) & (lane < at + width), y, sides[i])
            extra.append(pltpu.roll(sides[0], 1, 0) + pltpu.roll(sides[1], 15, 0))
        for i, x in enumerate(extra):
            for h in range(2):
                sent_buf[pl.ds(first + 320 * h + 36 + i, 8, stride=40), :] = x[8 * h : 8 * h + 8]
        at = pl.ds(first, 640)
        stores.append(copy(sent_buf.at[at], sent_ref.at[at], sent_sem.at[g]))
        stores[-1].start()
    for c in stores:
        c.wait()


def begin(d, v, m, r, records, ids):
    hbm = pl.BlockSpec(memory_space=pltpu.HBM)
    dma = pltpu.SemaphoreType.DMA
    return pl.pallas_call(
        begin_kernel,
        in_specs=[hbm] * 5 + [pl.BlockSpec(memory_space=pltpu.VMEM)],
        out_specs=[hbm] * 7,
        out_shape=[pltpu.HBM((5, N, N), F32)] * 2
        + [pltpu.HBM((6, 5, H, N), F32)] * 2
        + [pltpu.HBM((2, 5, H, N), F32)] * 2
        + [pltpu.HBM((40 * N, N), F32)],
        scratch_shapes=[
            pltpu.VMEM((5, 8, N, N), F32),
            pltpu.VMEM((5, N, N), F32),
            pltpu.VMEM((5, N, N), F32),
            pltpu.VMEM((9, 4 * N, N), F32),
            pltpu.VMEM((40 * N, N), F32),
            pltpu.VMEM((N, N), F32),
            dma((5, 4)),
            dma((5, 4)),
            dma((5, 2)),
            dma((8,)),
            dma((8,)),
        ],
        compiler_params=pltpu.CompilerParams(vmem_limit_bytes=20 * 1024 * 1024),
        name="begin",
    )(*in_hbm(d, v, m, r, records), ids)


def coefs_kernel(m_ref, r_ref, re_ref, rw_ref, out_ref):
    f = lambda a: float(np.float32(a))
    shape = (N, N)
    lane = lane_ids(shape)
    row = lax.broadcasted_iota(jnp.int32, shape, 0) % 4
    pick = lambda n: jnp.where(
        n == 0, f(PERIODIC[0]), jnp.where(n == 2, f(PERIODIC[2]), f(PERIODIC[1]))
    )

    def three(at, mod, rho, ew):
        area = 0.25 * ew * pick(row)
        out_ref[at] = area
        out_ref[at + 1] = area * jnp.sqrt(rho * mod)
        out_ref[at + 2] = area * (0.5 * mod)

    three(0, m_ref[0], r_ref[0], pick(lane % 4))
    mod = rho = jnp.ones(shape, F32)
    node = jnp.zeros(shape, jnp.int32)
    for groups, src, base in ((WEST_GROUPS, rw_ref[0], 112), (EAST_GROUPS, re_ref[0], 0)):
        for c in range(3):
            for off, width, col, _ in groups:
                at = 40 * c + off
                mask = (lane >= at) & (lane < at + width)
                mod = jnp.where(mask, pltpu.roll(src, (at - 96 - (col - base)) % N, 1), mod)
                rho = jnp.where(mask, pltpu.roll(src, (at - 112 - (col - base)) % N, 1), rho)
                node = jnp.where(mask, lane - at, node)
    three(3, mod, rho, pick(node % 4))


def coefs(m, r, re, rw):
    plane = pl.BlockSpec((1, N, N), lambda i: (0, 0, 0))
    return pl.pallas_call(
        coefs_kernel,
        grid=(1,),
        in_specs=[plane] * 4,
        out_specs=pl.BlockSpec((6, N, N), lambda i: (0, 0, 0)),
        out_shape=jax.ShapeDtypeStruct((6, N, N), F32),
        name="coefs",
    )(m, r, re, rw)


def place_kernel(
    arr_ref, co_hbm, b_ref, strip_ref, north_ref, south_ref,
    inj_ref, last_ref, side_ref, vid_ref, ids_ref, co_ref, sem,
):
    to_co = pltpu.make_async_copy(co_hbm, co_ref, sem.at[1])
    to_co.start()
    lane = lane_ids((N, N))
    plane = jnp.where(lane < 4, lane, jnp.where(lane < 8, lane - 4, lane - 5))
    vid_ref[...] = arr_ref[:, 36, :].astype(jnp.int32) + N * plane
    to_scalar = pltpu.make_async_copy(vid_ref, ids_ref, sem.at[0])
    to_scalar.start()
    to_scalar.wait()

    def body(s, carry):
        for t in range(STEPS):
            r = ids_ref[s, t]
            inj_ref[pl.ds(pl.multiple_of(r * 8, 8), 8), :] = arr_ref[s, pl.ds(t, 8, stride=4), :]
            last_ref[pl.ds(r, 1), :] = arr_ref[s, 32 + t : 33 + t, :]
        sides = arr_ref[s, 36:40, :]
        for i in range(2):
            for t in range(3):
                at = pl.multiple_of(ids_ref[s, 4 + 4 * i + t] * 4, 4)
                side_ref[pl.ds(at, 4), :] = sides
        return carry

    lax.fori_loop(0, 128, body, 0, unroll=8)
    to_co.wait()
    lane = lane_ids((8, N))

    def combine(k, carry):
        y = pl.multiple_of(k * 8, 8)
        rows = pl.ds(y, 8)
        co = [co_ref[i, rows, :] for i in range(6)]
        for t in range(STEPS):
            for c in range(3):
                base = (t * N + y) * 8
                inc = inj_ref[pl.ds(base + c, 8, stride=8), :]
                vel = inj_ref[pl.ds(base + 3 + c, 8, stride=8), :]
                if c < 2:
                    dis = inj_ref[pl.ds(base + 6 + c, 8, stride=8), :]
                else:
                    dis = last_ref[pl.ds(t * N + y, 8), :]
                b_ref[t, c, rows, :] = co[0] * inc + co[1] * vel + co[2] * dis
        b = None
        for rho in range(3):
            x = jnp.zeros((8, N), F32)
            for i, groups in enumerate((WEST_GROUPS, EAST_GROUPS)):
                for off, width, _, t in groups:
                    part = side_ref[pl.ds(((3 * i + t) * N + y) * 4 + 1 + rho, 8, stride=4), :]
                    mask = (lane >= off) & (lane < off + width)
                    for c in (1, 2):
                        mask = mask | ((lane >= 40 * c + off) & (lane < 40 * c + off + width))
                    x = jnp.where(mask, part, x)
            b = co[3] * x if b is None else b + co[3 + rho] * x
        for t in range(3):
            out = None
            for c in range(3):
                off, width, col, _ = WEST_GROUPS[t]
                start = 32 * c + 16 + col - 112
                p = lane_move(b, start - 40 * c - off, start, width)
                off, width, _, _ = EAST_GROUPS[t]
                p = p + lane_move(b, 32 * c - 40 * c - off, 32 * c, width)
                out = p if out is None else out + p
            strip_ref[t, rows, :] = out
        return carry

    lax.fori_loop(0, 16, combine, 0)
    for t in range(3):
        n, at = FORCE_ROWS[t]
        for ch in range(4):
            x = b_ref.at[t, ch] if ch < 3 else strip_ref.at[t]
            north_ref[ch, at : at + n] = x[N - n :, :]
            south_ref[ch, at : at + n] = x[:n, :]


def place(arrived, co):
    whole = pl.BlockSpec(memory_space=pltpu.VMEM)
    return pl.pallas_call(
        place_kernel,
        in_specs=[whole, pl.BlockSpec(memory_space=pltpu.HBM)],
        out_specs=[whole] * 4,
        out_shape=[
            jax.ShapeDtypeStruct((STEPS, 3, N, N), F32),
            jax.ShapeDtypeStruct((3, N, N), F32),
            jax.ShapeDtypeStruct((4, 24, N), F32),
            jax.ShapeDtypeStruct((4, 24, N), F32),
        ],
        scratch_shapes=[
            pltpu.VMEM((STEPS * N * 8, N), F32),
            pltpu.VMEM((STEPS * N, N), F32),
            pltpu.VMEM((6 * N * 4, N), F32),
            pltpu.VMEM((N, N), jnp.int32),
            pltpu.SMEM((N, N), jnp.int32),
            pltpu.VMEM((6, N, N), F32),
            pltpu.SemaphoreType.DMA((2,)),
        ],
        compiler_params=pltpu.CompilerParams(vmem_limit_bytes=VMEM_LIMIT),
        name="place",
    )(arrived, *in_hbm(co))


def line_forces(d, k, kn, mn_ref, ce_ref, grad_ref, back_ref, channels, emit):
    live = E if channels == 4 else 32
    rows = 5 * 4 * live

    def north(ch):
        m = ch // 3
        for z in range(5):
            v = [d[ch][z, j] for j in range(4)]
            v.append(pltpu.roll(v[0], E - 1, 0))
            g = apply5(DER, v)
            r = apply5(BACK * W[z], [g[i] * mn_ref[m, z, i] for i in range(5)])
            r[0] = r[0] + pltpu.roll(r[4], 1, 0)
            for j in range(4):
                kn[ch][z, j] = r[j]

    def depth(ch):
        m = ch // 3
        for j in range(4):
            x = [d[ch][z, j, :live] for z in range(5)]
            g = apply5(DER, x)
            r = apply5(BACK * PERIODIC[j], [g[z] * mn_ref[m, z, j, :live] for z in range(5)])
            for z in range(5):
                emit(ch, j, z, x[z], (k[ch][z, j, :live] + kn[ch][z, j, :live]) + r[z])

    sh, sl = split2(d[3][:, :, :live].reshape(rows, N))
    strip = None
    for c in range(3):
        mh, ml = split2(d[c][:, :, :live].reshape(rows, N))
        hi = jnp.concatenate([mh, sh], axis=1)
        lo = jnp.concatenate([ml, sl], axis=1)
        g = dot(hi, grad_ref[c, 0]) + dot(lo, grad_ref[c, 0]) + dot(hi, grad_ref[c, 1])
        fh, fl = split2(g * ce_ref[:, :, :live].reshape(rows, 256))
        f = dot(fh, back_ref[c, 0]) + dot(fl, back_ref[c, 0]) + dot(fh, back_ref[c, 1])
        k[c][:, :, :live] = f[:, :N].reshape(5, 4, live, N)
        if channels == 4:
            strip = f[:, N:] if strip is None else strip + f[:, N:]
        north(c)
        if c:
            depth(c - 1)
    if channels == 4:
        north(3)
        k[3][...] = strip.reshape(5, 4, E, N)
    depth(2)
    if channels == 4:
        depth(3)


def expand(xe, xw, src, step):
    out = None
    for c in range(3):
        p = lane_move(xe, 32 * c - src - step * c, 32 * c)
        p = p + lane_move(xw, 32 * c + 16 - src - step * c, 32 * c + 16)
        out = p if out is None else out + p
    return out


def fields(mod, rho, j, z, put):
    f = lambda a: float(np.float32(a))
    ew = east_weight(mod.shape)
    put("mn", 0.5 * mod * ew)
    put("di", DT / (0.125 * rho * ew * (f(PERIODIC[j]) * f(W[z]))))
    if z == 0:
        area = 0.25 * ew * f(PERIODIC[j])
        put("ai", area * jnp.sqrt(rho * mod))
        put("as", area * (0.5 * mod))


def east_coefs(main, strip, sel, weight):
    x = jnp.concatenate([main, strip], axis=1)
    hi = x.astype(BF16)
    mid, lo = split2(x - hi.astype(F32))
    return (dot(hi, sel) + dot(mid, sel) + dot(lo, sel)) * weight


def strip_density(rho):
    return jnp.where(lane_ids(rho.shape) < 96, rho, 1.0)


def early_kernel(
    d_ref, v_ref, m_ref, r_ref, re_ref, rw_ref, sel_ref, qw_ref,
    d_out, v_out, mn_out, di_out, ce_out, ai_out, as_out,
):
    f = lambda a: float(np.float32(a))
    outs = {"mn": mn_out, "di": di_out, "ai": ai_out, "as": as_out}

    def plane(z):
        for j in range(4):
            own = pl.ds(j, 32, stride=4)
            xe, xw = re_ref[z, own, :], rw_ref[z, own, :]
            vs = [v_ref[c, z, own, :] for c in range(3)] + [expand(xe, xw, 48, 16)]
            ds = [d_ref[c, z, own, :] for c in range(3)] + [expand(xe, xw, 0, 16)]
            for ch in range(4):
                v_out[ch, z, j] = vs[ch]
                d_out[ch, z, j] = ds[ch] + DT * vs[ch]
            mods = [m_ref[z, own, :], expand(xe, xw, 96, 0)]
            rhos = [r_ref[z, own, :], strip_density(expand(xe, xw, 112, 0))]
            for m in range(2):

                def put(name, x):
                    at = (m, j) if name in ("ai", "as") else (m, z, j)
                    outs[name][at] = x

                fields(mods[m], rhos[m], j, z, put)
            weight = qw_ref[...] * (f(W[z]) * f(PERIODIC[j]))
            ce_out[z, j] = east_coefs(mods[0], mods[1], sel_ref[...], weight)

    for z in range(5):
        plane(z)


OWN_SHAPES = ((4, 5, 4, 32, N),) * 2 + ((2, 5, 4, 32, N),) * 2 + ((5, 4, 32, 256),) + ((2, 4, 32, N),) * 2


def early(d, v, m, r, re, rw, sel, qw):
    whole = pl.BlockSpec(memory_space=pltpu.VMEM)
    return pl.pallas_call(
        early_kernel,
        in_specs=[whole] * 8,
        out_specs=[whole] * 7,
        out_shape=[jax.ShapeDtypeStruct(x, F32) for x in OWN_SHAPES],
        compiler_params=pltpu.CompilerParams(vmem_limit_bytes=16 * 1024 * 1024),
        name="early",
    )(d, v, m, r, re, rw, sel, qw)


def prepare_kernel(*refs):
    own, halos, tables, refs = refs[:7], refs[7:11], refs[11:15], refs[15:]
    (d0, d1, d2, d3, v0, v1, v2, v3, mn_ref, di_ref, ce_ref, ai_ref, as_ref), refs = refs[:13], refs[13:]
    (k0, k1, k2, k3, n0, n1, n2, n3), refs = refs[:8], refs[8:]
    buffers, (own_sem, halo_sem) = refs[:8], refs[8:]
    d_ref, v_ref = (d0, d1, d2, d3), (v0, v1, v2, v3)
    copy = pltpu.make_async_copy
    node = pl.ds(0, 32)
    late = [copy(x, y, halo_sem.at[i]) for i, (x, y) in enumerate(zip((*halos, *tables), buffers))]
    moves = []
    for ch in range(4):
        moves.append((own[0].at[ch], d_ref[ch].at[:, :, node]))
        moves.append((own[1].at[ch], v_ref[ch].at[:, :, node]))
    for m in range(2):
        moves.append((own[2].at[m], mn_ref.at[m, :, 0:4, node]))
        moves.append((own[3].at[m], di_ref.at[m, :, :, node]))
    moves.append((own[4], ce_ref.at[:, :, node]))
    moves.append((own[5], ai_ref.at[:, :, node]))
    moves.append((own[6], as_ref.at[:, :, node]))
    moves = [copy(x, y, own_sem.at[i]) for i, (x, y) in enumerate(moves)]
    for c in late + moves:
        c.start()
    n_ref, s_ref, cn_ref, cs_ref, sel_ref, qw_ref, grad_ref, back_ref = buffers
    outs = {"mn": mn_ref, "di": di_ref, "ai": ai_ref, "as": as_ref}
    f = lambda a: float(np.float32(a))
    for c in late:
        c.wait()

    def halo(at, j, north=n_ref, south=s_ref):
        at = (*at, pl.ds(j, 4, stride=4), slice(None))
        return jnp.concatenate([north[at], south[at]], axis=0)

    rest = slice(32, E)
    mains, sides = [], []
    for z in range(5):
        for j in range(4):
            xe, xw, mod, rho = (halo((i, z), j, cn_ref, cs_ref) for i in (2, 3, 0, 1))
            vs = [halo((3 + c, z), j) for c in range(3)] + [expand(xe, xw, 48, 16)]
            ds = [halo((c, z), j) for c in range(3)] + [expand(xe, xw, 0, 16)]
            for ch in range(4):
                v_ref[ch][z, j, rest] = vs[ch]
                d_ref[ch][z, j, rest] = ds[ch] + DT * vs[ch]
            mods = [mod, expand(xe, xw, 96, 0)]
            rhos = [rho, strip_density(expand(xe, xw, 112, 0))]
            for m in range(2):

                def put(name, x):
                    at = (m, j, rest) if name in ("ai", "as") else (m, z, j, rest)
                    outs[name][at] = x

                fields(mods[m], rhos[m], j, z, put)
            mains.append(mods[0])
            sides.append(mods[1])
    c = east_coefs(jnp.concatenate(mains), jnp.concatenate(sides), sel_ref[...], qw_ref[...])
    for z in range(5):
        for j in range(4):
            at = (z * 4 + j) * 8
            ce_ref[z, j, rest] = c[at : at + 8] * (f(W[z]) * f(PERIODIC[j]))
    for c in moves:
        c.wait()
    for m in range(2):
        for z in range(5):
            mn_ref[m, z, 4] = pltpu.roll(mn_ref[m, z, 0], E - 1, 0)

    def emit(ch, j, z, d, k):
        m = ch // 3
        v = v_ref[ch][z, j]
        if z == 0:
            k = k + ai_ref[m, j] * v + as_ref[m, j] * d
        v_ref[ch][z, j] = v - di_ref[m, z, j] * k

    line_forces(
        d_ref, (k0, k1, k2, k3), (n0, n1, n2, n3), mn_ref, ce_ref, grad_ref, back_ref, 4, emit
    )


def prepare(own, halos, tables):
    grad, back, sel, qw = tables
    whole = pl.BlockSpec(memory_space=pltpu.VMEM)
    state = jax.ShapeDtypeStruct((5, 4, E, N), F32)
    late = (*halos, sel, qw, grad, back)
    return pl.pallas_call(
        prepare_kernel,
        in_specs=[pl.BlockSpec(memory_space=pltpu.HBM)] * 15,
        out_specs=[whole] * 13,
        out_shape=[
            *[state] * 8,
            jax.ShapeDtypeStruct((2, 5, 5, E, N), F32),
            jax.ShapeDtypeStruct((2, 5, 4, E, N), F32),
            jax.ShapeDtypeStruct((5, 4, E, 256), F32),
            jax.ShapeDtypeStruct((2, 4, E, N), F32),
            jax.ShapeDtypeStruct((2, 4, E, N), F32),
        ],
        scratch_shapes=[pltpu.VMEM((5, 4, E, N), F32)] * 8
        + [pltpu.VMEM(x.shape, x.dtype) for x in late]
        + [pltpu.SemaphoreType.DMA((15,)), pltpu.SemaphoreType.DMA((8,))],
        compiler_params=pltpu.CompilerParams(vmem_limit_bytes=VMEM_LIMIT),
        name="prepare",
    )(*in_hbm(*own, *late))


def steps_kernel(
    i0, i1, i2, i3, u0, u1, u2, u3, mn_ref, di_ref, ce_ref, ai_ref, as_ref,
    b_ref, bs_ref, bn_ref, bo_ref, grad_ref, back_ref,
    dout_ref, vout_ref,
    d0, d1, d2, d3, v0, v1, v2, v3, k0, k1, k2, k3, n0, n1, n2, n3, f_ref,
):
    d_in, v_in = (i0, i1, i2, i3), (u0, u1, u2, u3)
    d_ref, v_ref = (d0, d1, d2, d3), (v0, v1, v2, v3)
    k_ref, kn_ref = (k0, k1, k2, k3), (n0, n1, n2, n3)
    for t in range(3):
        n, at = FORCE_ROWS[t]
        gap = jnp.zeros((8 - n // 2, N), F32)
        for ch in range(4):
            for j in range(4):
                own = pl.ds(j, 32, stride=4)
                x = b_ref[t, ch, own, :] if ch < 3 else bs_ref[t, own, :]
                halo = pl.ds(at + j, n // 4, stride=4)
                f_ref[t, ch, j] = jnp.concatenate(
                    [x, bn_ref[ch, halo, :], gap, bo_ref[ch, halo, :]], axis=0
                )
    for ch in range(3):
        for j in range(4):
            x = b_ref[3, ch, pl.ds(j, 32, stride=4), :]
            f_ref[3, ch, j] = jnp.concatenate([x, jnp.zeros((8, N), F32)], axis=0)

    for ch in range(4):
        for j in range(4):
            for z in range(5):
                v = v_in[ch][z, j]
                if z == 0:
                    v = v + di_ref[ch // 3, z, j] * f_ref[0, ch, j]
                v_ref[ch][z, j] = v
                d_ref[ch][z, j] = d_in[ch][z, j] + DT * v

    def velocity(t, ch, j, z, d, k):
        m = ch // 3
        n = slice(0, d.shape[0])
        v = v_ref[ch][z, j, n]
        if z == 0:
            k = k + ai_ref[m, j, n] * v + as_ref[m, j, n] * d - f_ref[t, ch, j, n]
        return v - di_ref[m, z, j, n] * k

    def step(t, carry):
        def emit(ch, j, z, d, k):
            v = velocity(t, ch, j, z, d, k)
            v_ref[ch][z, j] = v
            d_ref[ch][z, j] = d + DT * v

        line_forces(d_ref, k_ref, kn_ref, mn_ref, ce_ref, grad_ref, back_ref, 4, emit)
        return carry

    lax.fori_loop(1, 3, step, 0)

    def final(ch, j, z, d, k):
        dout_ref[ch, z, pl.ds(j, 32, stride=4), :] = d
        vout_ref[ch, z, pl.ds(j, 32, stride=4), :] = velocity(3, ch, j, z, d, k)

    line_forces(d_ref, k_ref, kn_ref, mn_ref, ce_ref, grad_ref, back_ref, 3, final)


def steps(prepared, b, bs, bn, bo, tables):
    grad, back = tables[:2]
    whole = pl.BlockSpec(memory_space=pltpu.VMEM)
    return pl.pallas_call(
        steps_kernel,
        in_specs=[whole] * 19,
        out_specs=[whole] * 2,
        out_shape=[jax.ShapeDtypeStruct((3, 5, N, N), F32)] * 2,
        scratch_shapes=[pltpu.VMEM((5, 4, E, N), F32)] * 16 + [pltpu.VMEM((4, 4, 4, E, N), F32)],
        compiler_params=pltpu.CompilerParams(vmem_limit_bytes=VMEM_LIMIT),
        name="steps",
    )(*prepared, b, bs, bn, bo, grad, back)


def local(displacement, velocity, modulus, density, traces, record_row):
    tables = tuple(jnp.asarray(t) for t in east_tables())
    west, east, north, south, late_north, late_south, sent = begin(
        displacement, velocity, modulus, density, jnp.transpose(traces[0], (1, 0, 2)), record_row
    )
    from_east = shifted(west, "reg", -1)
    from_west = shifted(east, "reg", 1)
    from_north = shifted(south, "src", -1)
    from_south = shifted(north, "src", 1)
    arrived = lax.all_to_all(
        sent.reshape(N, 40, N), ("src", "reg"), split_axis=0, concat_axis=0, tiled=True
    )
    corner = jnp.stack([from_east, from_west])
    late_south = jnp.concatenate([late_south, corner[:, :, :H]], axis=0)
    late_north = jnp.concatenate([late_north, corner[:, :, N - H :]], axis=0)
    corner_north = shifted(late_south, "src", -1)
    corner_south = shifted(late_north, "src", 1)
    co = coefs(modulus, density, from_east, from_west)
    own = early(displacement, velocity, modulus, density, from_east, from_west, *tables[2:])
    b, b_strip, b_north, b_south = place(arrived, co)
    b_from_south = shifted(b_north, "src", 1)
    b_from_north = shifted(b_south, "src", -1)
    from_north, from_south, corner_north, corner_south, _ = lax.optimization_barrier(
        (from_north, from_south, corner_north, corner_south, b)
    )
    prepared = prepare(own, (from_north, from_south, corner_north, corner_south), tables)
    return steps(prepared, b, b_strip, b_from_north, b_from_south, tables)


def solution(mesh):
    state = P(None, None, "src", "reg")
    field = P(None, "src", "reg")
    in_specs = (state, state, field, field, P(("src", "reg"), None, None, None), P(("src", "reg"), None))
    return jax.shard_map(local, mesh=mesh, in_specs=in_specs, out_specs=(state, state), check_vma=False)
```

time: 102 us -> 103 us (level)
  the two profiles are of different devices: /device:TPU:1 before, /device:TPU:0 now
where the time goes in v1:
time: 103 us
  Pallas kernels  35.1 us (34%)
  waiting for transfers between devices  30.1 us (29%)
  starting transfers between devices  29.1 us (28%)
  local copies, waits for them, and re-layouts  6.7 us (7%)
    ppermute x8, waiting for transfers between devices, shifted(): lax.ppermute(block, axis, [((i - distance) % n, i) for i in range(n)])  30.1 us
    ppermute x8, starting transfers between devices, shifted(): lax.ppermute(block, axis, [((i - distance) % n, i) for i in range(n)])  17.9 us
    pallas_call x1, Pallas kernels, steps(): pl.pallas_call(steps_kernel, in_specs=[whole] * 19, out_specs=[whole] * 2...  12.3 us
    all_to_all x1, starting transfers between devices, local(): lax.all_to_all(sent.reshape(N, 40, N), ('src', 'reg'), split_axis=0, conc...  11.2 us
    pallas_call x1, Pallas kernels, prepare(): pl.pallas_call(prepare_kernel, in_specs=[pl.BlockSpec(memory_space=pltpu....  7.73 us
    unnamed x48, local copies, waits for them, and re-layouts  6.7 us
    pallas_call x1, Pallas kernels, begin(): pl.pallas_call(begin_kernel, in_specs=[hbm] * 5 + [pl.BlockSpec(memory_sp...  5.62 us
    pallas_call x1, Pallas kernels, place(): pl.pallas_call(place_kernel, in_specs=[whole, pl.BlockSpec(memory_space=p...  5.48 us
  transfers between devices with their start and end apart: 9, of which 2 were waited for; matrix products, arithmetic and copies ran while one was open for 1% of the time, Pallas kernels for 17%

profile of v1, /device:TPU:0, one launch (start us, length us, event | category | flops | bytes accessed | tf_op | source)
XLA Modules:
  0.0 102.6 jit_solution(803818202314369441)
XLA Ops:
  0.6 0.7 copy-done.19
  1.3 5.6 %begin.1 = (f32[5,128,128]{2,1,0:T(8,128)}, f32[5,128,128]{2,1,0:T(8,128)}, f32[6,5,16,128]{3,2,1,0:T(8,128)}, f32[6,5,16,128]{3,2,1,0:T(8,128)}, f32[2,5,16,128...) custom-call(f32[3,5,128,128]{3,2,1,0:T(8,128)} %d_ref.3, f32[3,5,128,128]{3,2,1,0:T(8,128)} %v_ref.3, ...), custom_call_target="tpu_custom_call" | custom-call | tf_op jit(solution)/shard_map/begin/pallas_call | solution.py:217
  6.9 0.0 copy-start.23
  7.0 0.0 copy-start.22
  7.0 11.2 %all-to-all-start = ((f32[128,40,128]{2,1,0:T(8,128)}), f32[128,40,128]{2,1,0:T(8,128)S(1)}, u32[]{:S(2)}, u32[]{:S(2)}) async-start(f32[128,40,128]{2,1,0:T(8,128)} %bitcast.8), calls=%async_computation | async-start | bytes 5242880 | tf_op jit(solution)/shard_map/all_to_all | solution.py:694
  18.2 3.5 %collective-permute-start = (f32[5,128,128]{2,1,0:T(8,128)S(1)}, f32[5,128,128]{2,1,0:T(8,128)S(1)}, u32[]{:S(2)}, u32[]{:S(2)}) collective-permute-start(f32[5,128,128]{2,1,0:T(8,128)S(1)} %copy-done.23), channel_id=1, source_target_pairs={{1,0},{2,1},{3,2},{4,3},{5,4},{6,5},{7,6},{8,7},{9,8},{10,9},{11,1... | collective-permute-start | bytes 983048 | tf_op jit(solution)/shard_map/ppermute | solution.py:89
  21.7 0.0 collective-permute-start.1
  21.7 5.0 %collective-permute-start.2 = (f32[6,5,16,128]{3,2,1,0:T(8,128)}, f32[6,5,16,128]{3,2,1,0:T(8,128)}, u32[]{:S(2)}, u32[]{:S(2)}) collective-permute-start(f32[6,5,16,128]{3,2,1,0:T(8,128)} %get-tuple-element.46), channel_id=1, source_target_pairs={{16,0},{32,16},{48,32},{64,48},{80,64},{96,80},{112,96},{0,112},{1... | collective-permute-start | bytes 737288 | tf_op jit(solution)/shard_map/ppermute | solution.py:89
  26.8 26.8 %collective-permute-done.re_ref = f32[5,128,128]{2,1,0:T(8,128)S(1)} collective-permute-done((f32[5,128,128]{2,1,0:T(8,128)S(1)}, f32[5,128,128]{2,1,0:T(8,128)S(1)}, u32[]{:S(2)}, u32[]{:S(2)}) %collective-permute-start) | collective-permute-done | bytes 327712 | tf_op jit(solution)/shard_map/ppermute | solution.py:89
  53.6 3.3 %collective-permute-done.1.rw_ref = f32[5,128,128]{2,1,0:T(8,128)S(1)} collective-permute-done((f32[5,128,128]{2,1,0:T(8,128)S(1)}, f32[5,128,128]{2,1,0:T(8,128)S(1)}, u32[]{:S(2)}, u32[]{:S(2)}) %collective-permute-start.1) | collective-permute-done | bytes 327712 | tf_op jit(solution)/shard_map/ppermute | solution.py:89
  56.9 0.8 fusion
  57.7 2.7 %collective-permute-start.5 = (f32[4,5,16,128]{3,2,1,0:T(8,128)}, f32[4,5,16,128]{3,2,1,0:T(8,128)}, u32[]{:S(2)}, u32[]{:S(2)}) collective-permute-start(f32[4,5,16,128]{3,2,1,0:T(8,128)} %get-tuple-element.72), channel_id=1, source_target_pairs={{112,0},{0,16},{16,32},{32,48},{48,64},{64,80},{80,96},{96,112},{1... | collective-permute-start | bytes 491528 | tf_op jit(solution)/shard_map/ppermute | solution.py:89
  60.4 0.0 copy-start.15
  60.4 0.0 copy-start.18
  60.4 3.0 %collective-permute-start.4 = (f32[4,5,16,128]{3,2,1,0:T(8,128)}, f32[4,5,16,128]{3,2,1,0:T(8,128)}, u32[]{:S(2)}, u32[]{:S(2)}) collective-permute-start(f32[4,5,16,128]{3,2,1,0:T(8,128)} %get-tuple-element.73), channel_id=1, source_target_pairs={{16,0},{32,16},{48,32},{64,48},{80,64},{96,80},{112,96},{0,112},{1... | collective-permute-start | bytes 491528 | tf_op jit(solution)/shard_map/ppermute | solution.py:89
  63.4 2.4 %coefs.1.co_hbm = f32[6,128,128]{2,1,0:T(8,128)} custom-call(f32[5,128,128]{2,1,0:T(8,128)} %m_ref.5, f32[5,128,128]{2,1,0:T(8,128)} %r_ref.5, f32[5,128,128]{2,1,0:T(8,128)} %copy-done.6, f32[5,128,128]{2,1,0:T(8,128)} %copy-done.8), custom_call_target="tpu_custom_call" | custom-call | tf_op jit(solution)/shard_map/coefs/pallas_call | solution.py:274
  65.8 0.0 copy-start.7
  65.8 5.5 %place.1 = (f32[4,3,128,128]{3,2,1,0:T(8,128)S(1)}, f32[3,128,128]{2,1,0:T(8,128)S(1)}, f32[4,24,128]{2,1,0:T(8,128)S(1)}, f32[4,24,128]{2,1,0:T(8,128)S(1)}) custom-call(f32[128,40,128]{2,1,0:T(8,128)S(1)} %all-to-all-done.arr_ref, f32[6,128,128]{2,1,0:T(8,128)} %coefs.1.co_hbm), custom_call_target="tpu_custom_call" | custom-call | tf_op jit(solution)/shard_map/place/pallas_call | solution.py:361
  71.3 2.9 %collective-permute-start.6 = (f32[4,24,128]{2,1,0:T(8,128)S(1)}, f32[4,24,128]{2,1,0:T(8,128)S(1)}, u32[]{:S(2)}, u32[]{:S(2)}) collective-permute-start(f32[4,24,128]{2,1,0:T(8,128)S(1)} %get-tuple-element.70), channel_id=1, source_target_pairs={{16,0},{32,16},{48,32},{64,48},{80,64},{96,80},{112,96},{0,112},{1... | collective-permute-start | bytes 147464 | tf_op jit(solution)/shard_map/ppermute | solution.py:89
  74.2 0.7 collective-permute-start.7
  75.0 1.5 %early.1 = (f32[4,5,4,32,128]{4,3,2,1,0:T(8,128)S(1)}, f32[4,5,4,32,128]{4,3,2,1,0:T(8,128)S(1)}, f32[2,5,4,32,128]{4,3,2,1,0:T(8,128)S(1)}, f32[2,5,4,32,128]{4...) custom-call(f32[3,5,128,128]{3,2,1,0:T(8,128)S(1)} %copy-done, ...), custom_call_target="tpu_custom_call" | custom-call | tf_op jit(solution)/shard_map/early/pallas_call | solution.py:500
  76.5 1.1 %copy-done.10 = f32[4,5,4,32,128]{4,3,2,1,0:T(8,128)} copy-done((f32[4,5,4,32,128]{4,3,2,1,0:T(8,128)}, f32[4,5,4,32,128]{4,3,2,1,0:T(8,128)S(1)}, u32[]{:S(2)}) %copy-start.10) | copy-done | bytes 1310744
  77.6 1.1 %copy-done.11 = f32[4,5,4,32,128]{4,3,2,1,0:T(8,128)} copy-done((f32[4,5,4,32,128]{4,3,2,1,0:T(8,128)}, f32[4,5,4,32,128]{4,3,2,1,0:T(8,128)S(1)}, u32[]{:S(2)}) %copy-start.11) | copy-done | bytes 1310744
  78.7 0.8 copy-done.12
  79.5 0.8 copy-done.13
  80.3 0.8 copy-done.14
  81.2 0.6 copy-done.16
  81.8 0.6 copy-done.17
  82.5 0.0 copy-start.2
  82.5 0.0 copy-start.3
  82.5 7.7 %prepare.1 = (f32[5,4,40,128]{3,2,1,0:T(8,128)S(1)}, f32[5,4,40,128]{3,2,1,0:T(8,128)S(1)}, f32[5,4,40,128]{3,2,1,0:T(8,128)S(1)}, f32[5,4,40,128]{3,2,1,0:T(8,1...) custom-call(f32[4,5,4,32,128]{4,3,2,1,0:T(8,128)} %copy-done.10, ...), custom_call_target="tpu_custom_call" | custom-call | tf_op jit(solution)/shard_map/prepare/pallas_call | solution.py:591
  90.3 12.3 %steps.1 = (f32[3,5,128,128]{3,2,1,0:T(8,128)}, f32[3,5,128,128]{3,2,1,0:T(8,128)}) custom-call(f32[5,4,40,128]{3,2,1,0:T(8,128)S(1)} %get-tuple-element.56.i0, f32[5,4,40,128]{3,2,1,0:T(8,128)S(1)} %get-tuple-element.57.i1, f32[5,4,40,128]{3,2,1,0:T(8,128)S(1)} %get-tuple-element.58.i2, f32[5,4,40,128]{3,2,1,0:T(8,128)S(1)} %get-tuple-element.59.i3, ...), custom_call_target="tpu_custom_call" | custom-call | tf_op jit(solution)/shard_map/steps/pallas_call | solution.py:674
  (41 shorter events, 0.1 us)
Async XLA Ops:
  0.6 0.7 copy-start.19
  6.9 11.2 %copy-start.23 = (f32[5,128,128]{2,1,0:T(8,128)S(1)}, f32[5,128,128]{2,1,0:T(8,128)}, u32[]{:S(2)}) copy-start(f32[5,128,128]{2,1,0:T(8,128)} %get-tuple-element.37) | copy-start | bytes 983044
  7.0 14.8 %copy-start.22 = (f32[5,128,128]{2,1,0:T(8,128)S(1)}, f32[5,128,128]{2,1,0:T(8,128)}, u32[]{:S(2)}) copy-start(f32[5,128,128]{2,1,0:T(8,128)} %get-tuple-element.38) | copy-start | bytes 983044
  7.0 49.9 %copy-start.20 = (f32[2,5,16,128]{3,2,1,0:T(8,128)S(1)}, f32[2,5,16,128]{3,2,1,0:T(8,128)}, u32[]{:S(2)}) copy-start(f32[2,5,16,128]{3,2,1,0:T(8,128)} %get-tuple-element.49) | copy-start | bytes 245764
  7.0 49.9 %copy-start.21 = (f32[2,5,16,128]{3,2,1,0:T(8,128)S(1)}, f32[2,5,16,128]{3,2,1,0:T(8,128)}, u32[]{:S(2)}) copy-start(f32[2,5,16,128]{3,2,1,0:T(8,128)} %get-tuple-element.48) | copy-start | bytes 245764
  7.0 58.8 %all-to-all-start = ((f32[128,40,128]{2,1,0:T(8,128)}), f32[128,40,128]{2,1,0:T(8,128)S(1)}, u32[]{:S(2)}, u32[]{:S(2)}) async-start(f32[128,40,128]{2,1,0:T(8,128)} %bitcast.8), calls=%async_computation | async-start | bytes 5242880 | tf_op jit(solution)/shard_map/all_to_all | solution.py:694
  18.2 35.4 %collective-permute-start = (f32[5,128,128]{2,1,0:T(8,128)S(1)}, f32[5,128,128]{2,1,0:T(8,128)S(1)}, u32[]{:S(2)}, u32[]{:S(2)}) collective-permute-start(f32[5,128,128]{2,1,0:T(8,128)S(1)} %copy-done.23), channel_id=1, source_target_pairs={{1,0},{2,1},{3,2},{4,3},{5,4},{6,5},{7,6},{8,7},{9,8},{10,9},{11,1... | collective-permute-start | bytes 983048 | tf_op jit(solution)/shard_map/ppermute | solution.py:89
  21.7 35.1 %collective-permute-start.1 = (f32[5,128,128]{2,1,0:T(8,128)S(1)}, f32[5,128,128]{2,1,0:T(8,128)S(1)}, u32[]{:S(2)}, u32[]{:S(2)}) collective-permute-start(f32[5,128,128]{2,1,0:T(8,128)S(1)} %copy-done.22), channel_id=1, source_target_pairs={{15,0},{0,1},{1,2},{2,3},{3,4},{4,5},{5,6},{6,7},{7,8},{8,9},{9,10... | collective-permute-start | bytes 983048 | tf_op jit(solution)/shard_map/ppermute | solution.py:89
  21.7 52.5 %collective-permute-start.2 = (f32[6,5,16,128]{3,2,1,0:T(8,128)}, f32[6,5,16,128]{3,2,1,0:T(8,128)}, u32[]{:S(2)}, u32[]{:S(2)}) collective-permute-start(f32[6,5,16,128]{3,2,1,0:T(8,128)} %get-tuple-element.46), channel_id=1, source_target_pairs={{16,0},{32,16},{48,32},{64,48},{80,64},{96,80},{112,96},{0,112},{1... | collective-permute-start | bytes 737288 | tf_op jit(solution)/shard_map/ppermute | solution.py:89
  26.8 55.7 %collective-permute-start.3 = (f32[6,5,16,128]{3,2,1,0:T(8,128)}, f32[6,5,16,128]{3,2,1,0:T(8,128)}, u32[]{:S(2)}, u32[]{:S(2)}) collective-permute-start(f32[6,5,16,128]{3,2,1,0:T(8,128)} %get-tuple-element.47), channel_id=1, source_target_pairs={{112,0},{0,16},{16,32},{32,48},{48,64},{64,80},{80,96},{96,112},{1... | collective-permute-start | bytes 737288 | tf_op jit(solution)/shard_map/ppermute | solution.py:89
  53.6 6.8 %copy-start.6 = (f32[5,128,128]{2,1,0:T(8,128)}, f32[5,128,128]{2,1,0:T(8,128)S(1)}, u32[]{:S(2)}) copy-start(f32[5,128,128]{2,1,0:T(8,128)S(1)} %collective-permute-done.re_ref) | copy-start | bytes 983044
  56.9 3.5 %copy-start.8 = (f32[5,128,128]{2,1,0:T(8,128)}, f32[5,128,128]{2,1,0:T(8,128)S(1)}, u32[]{:S(2)}) copy-start(f32[5,128,128]{2,1,0:T(8,128)S(1)} %collective-permute-done.1.rw_ref) | copy-start | bytes 983044
  57.7 24.8 %collective-permute-start.5 = (f32[4,5,16,128]{3,2,1,0:T(8,128)}, f32[4,5,16,128]{3,2,1,0:T(8,128)}, u32[]{:S(2)}, u32[]{:S(2)}) collective-permute-start(f32[4,5,16,128]{3,2,1,0:T(8,128)} %get-tuple-element.72), channel_id=1, source_target_pairs={{112,0},{0,16},{16,32},{32,48},{48,64},{64,80},{80,96},{96,112},{1... | collective-permute-start | bytes 491528 | tf_op jit(solution)/shard_map/ppermute | solution.py:89
  60.4 14.6 %copy-start.4 = (f32[5,128,128]{2,1,0:T(8,128)S(1)}, f32[5,128,128]{2,1,0:T(8,128)}, u32[]{:S(2)}) copy-start(f32[5,128,128]{2,1,0:T(8,128)} %m_ref.5) | copy-start | bytes 983044
  60.4 14.6 %copy-start.5 = (f32[5,128,128]{2,1,0:T(8,128)S(1)}, f32[5,128,128]{2,1,0:T(8,128)}, u32[]{:S(2)}) copy-start(f32[5,128,128]{2,1,0:T(8,128)} %r_ref.5) | copy-start | bytes 983044
  60.4 14.6 %copy-start.15 = (bf16[256,256]{1,0:T(8,128)(2,1)S(1)}, bf16[256,256]{1,0:T(8,128)(2,1)}, u32[]{:S(2)}) copy-start(bf16[256,256]{1,0:T(8,128)(2,1)} %constant.10.clone.sel_ref.refs_11_) | copy-start | bytes 393220
  60.4 14.6 %copy-start.18 = (f32[1,256]{1,0:T(1,128)S(1)}, f32[1,256]{1,0:T(1,128)}, u32[]{:S(2)}) copy-start(f32[1,256]{1,0:T(1,128)} %constant.11.clone.qw_ref.refs_12_) | copy-start | bytes 3076
  60.4 22.1 %collective-permute-start.4 = (f32[4,5,16,128]{3,2,1,0:T(8,128)}, f32[4,5,16,128]{3,2,1,0:T(8,128)}, u32[]{:S(2)}, u32[]{:S(2)}) collective-permute-start(f32[4,5,16,128]{3,2,1,0:T(8,128)} %get-tuple-element.73), channel_id=1, source_target_pairs={{16,0},{32,16},{48,32},{64,48},{80,64},{96,80},{112,96},{0,112},{1... | collective-permute-start | bytes 491528 | tf_op jit(solution)/shard_map/ppermute | solution.py:89
  65.8 9.1 %copy-start = (f32[3,5,128,128]{3,2,1,0:T(8,128)S(1)}, f32[3,5,128,128]{3,2,1,0:T(8,128)}, u32[]{:S(2)}) copy-start(f32[3,5,128,128]{3,2,1,0:T(8,128)} %d_ref.3) | copy-start | bytes 2949124
  65.8 9.1 %copy-start.1 = (f32[3,5,128,128]{3,2,1,0:T(8,128)S(1)}, f32[3,5,128,128]{3,2,1,0:T(8,128)}, u32[]{:S(2)}) copy-start(f32[3,5,128,128]{3,2,1,0:T(8,128)} %v_ref.3) | copy-start | bytes 2949124
  65.8 9.1 %copy-start.7 = (f32[5,128,128]{2,1,0:T(8,128)S(1)}, f32[5,128,128]{2,1,0:T(8,128)}, u32[]{:S(2)}) copy-start(f32[5,128,128]{2,1,0:T(8,128)} %copy-done.6) | copy-start | bytes 983044
  65.8 9.1 %copy-start.9 = (f32[5,128,128]{2,1,0:T(8,128)S(1)}, f32[5,128,128]{2,1,0:T(8,128)}, u32[]{:S(2)}) copy-start(f32[5,128,128]{2,1,0:T(8,128)} %copy-done.8) | copy-start | bytes 983044
  71.3 18.9 %collective-permute-start.6 = (f32[4,24,128]{2,1,0:T(8,128)S(1)}, f32[4,24,128]{2,1,0:T(8,128)S(1)}, u32[]{:S(2)}, u32[]{:S(2)}) collective-permute-start(f32[4,24,128]{2,1,0:T(8,128)S(1)} %get-tuple-element.70), channel_id=1, source_target_pairs={{16,0},{32,16},{48,32},{64,48},{80,64},{96,80},{112,96},{0,112},{1... | collective-permute-start | bytes 147464 | tf_op jit(solution)/shard_map/ppermute | solution.py:89
  74.2 16.0 %collective-permute-start.7 = (f32[4,24,128]{2,1,0:T(8,128)S(1)}, f32[4,24,128]{2,1,0:T(8,128)S(1)}, u32[]{:S(2)}, u32[]{:S(2)}) collective-permute-start(f32[4,24,128]{2,1,0:T(8,128)S(1)} %get-tuple-element.71), channel_id=1, source_target_pairs={{112,0},{0,16},{16,32},{32,48},{48,64},{64,80},{80,96},{96,112},{1... | collective-permute-start | bytes 147464 | tf_op jit(solution)/shard_map/ppermute | solution.py:89
  76.5 1.1 %copy-start.10 = (f32[4,5,4,32,128]{4,3,2,1,0:T(8,128)}, f32[4,5,4,32,128]{4,3,2,1,0:T(8,128)S(1)}, u32[]{:S(2)}) copy-start(f32[4,5,4,32,128]{4,3,2,1,0:T(8,128)S(1)} %get-tuple-element.39.refs_0_) | copy-start | bytes 3932164
  77.6 1.1 %copy-start.11 = (f32[4,5,4,32,128]{4,3,2,1,0:T(8,128)}, f32[4,5,4,32,128]{4,3,2,1,0:T(8,128)S(1)}, u32[]{:S(2)}) copy-start(f32[4,5,4,32,128]{4,3,2,1,0:T(8,128)S(1)} %get-tuple-element.40.refs_1_) | copy-start | bytes 3932164
  78.7 0.8 copy-start.12
  79.5 0.8 copy-start.13
  80.3 0.8 copy-start.14
  81.8 0.6 copy-start.17
  82.5 7.8 %copy-start.2 = (bf16[3,2,256,256]{3,2,1,0:T(8,128)(2,1)S(1)}, bf16[3,2,256,256]{3,2,1,0:T(8,128)(2,1)}, u32[]{:S(2)}) copy-start(bf16[3,2,256,256]{3,2,1,0:T(8,128)(2,1)} %constant.9.clone.refs_14_.back_ref) | copy-start | bytes 2359300
  82.5 7.8 %copy-start.3 = (bf16[3,2,256,256]{3,2,1,0:T(8,128)(2,1)S(1)}, bf16[3,2,256,256]{3,2,1,0:T(8,128)(2,1)}, u32[]{:S(2)}) copy-start(bf16[3,2,256,256]{3,2,1,0:T(8,128)(2,1)} %constant.8.clone.refs_13_.grad_ref) | copy-start | bytes 2359300
  (1 other events, 0.6 us)

commit v2 on v1

--- a/solution.py
+++ b/solution.py
@@ -36,20 +36,43 @@
 
 
 DER, W = gll()
-BACK = (DER * W[:, None]).T
 PERIODIC = [2 * W[0], W[1], W[2], W[3]]
 
 
-def apply5(m, v):
-    s0, s1, m0, m1 = v[0] + v[4], v[1] + v[3], v[0] - v[4], v[1] - v[3]
-    f = lambda a: float(np.float32(a))
+def network():
+    odd = [[(DER[i, 0] - DER[i, 4]) / 2, (DER[i, 1] - DER[i, 3]) / 2] for i in (0, 1)]
+    even = [[(DER[i, 0] + DER[i, 4]) / 2, (DER[i, 1] + DER[i, 3]) / 2] for i in (0, 1)]
+    scale = [even[0][0], even[1][0], DER[2, 0]]
+    f = lambda x: float(np.float32(x))
+    p = [[f(odd[i][k] / scale[i]) for k in range(2)] for i in range(2)]
+    q = [f(even[i][1] / scale[i]) for i in range(2)]
+    scale = np.array(scale + scale[1::-1])
+    return p, q, f(DER[2, 1] / DER[2, 0]), W * scale**2
+
+
+ODD, EVEN, MIDDLE, POINT = network()
+
+
+def slopes(v):
+    twice = v[2] + v[2]
+    u0, u1 = (v[0] + v[4]) - twice, (v[1] + v[3]) - twice
+    m0, m1 = v[0] - v[4], v[1] - v[3]
     out = [None] * 5
     for i in (0, 1):
-        p = f((m[i, 0] - m[i, 4]) / 2) * m0 + f((m[i, 1] - m[i, 3]) / 2) * m1
-        q = f((m[i, 0] + m[i, 4]) / 2) * s0 + f((m[i, 1] + m[i, 3]) / 2) * s1 + f(m[i, 2]) * v[2]
+        p = ODD[i][0] * m0 + ODD[i][1] * m1
+        q = u0 + EVEN[i] * u1
         out[i], out[4 - i] = p + q, p - q
-    out[2] = f(m[2, 0]) * m0 + f(m[2, 1]) * m1
+    out[2] = m0 + MIDDLE * m1
     return out
+
+
+def tested(f):
+    ep, eq = [f[0] + f[4], f[1] + f[3]], [f[0] - f[4], f[1] - f[3]]
+    m0 = (ODD[0][0] * ep[0] + ODD[1][0] * ep[1]) + f[2]
+    m1 = (ODD[0][1] * ep[0] + ODD[1][1] * ep[1]) + MIDDLE * f[2]
+    u0 = eq[0] + eq[1]
+    u1 = EVEN[0] * eq[0] + EVEN[1] * eq[1]
+    return [u0 + m0, u1 + m1, -2.0 * (u0 + u1), u1 - m1, u0 - m0]
 
 
 def column_of(x, comp):
@@ -112,6 +135,10 @@
     return jnp.where(r == 0, f(PERIODIC[0]), jnp.where(r == 2, f(PERIODIC[2]), f(PERIODIC[1])))
 
 
+def moved(x, shift):
+    return pltpu.roll(x, shift % N, x.ndim - 1) if shift % N else x
+
+
 def lane_move(x, shift, start, width=16):
     shift %= 128
     y = pltpu.roll(x, shift, x.ndim - 1) if shift else x
@@ -119,16 +146,20 @@
     return jnp.where((lane >= start) & (lane < start + width), y, 0.0)
 
 
-WEST_GROUPS = ((0, 12, 116, 0), (12, 8, 120, 1), (20, 4, 124, 2))
-EAST_GROUPS = ((24, 9, 0, 0), (33, 5, 0, 1), (38, 1, 0, 2))
+WEST_GROUPS = ((0, 12, 116, 0), (21, 8, 120, 1), (34, 4, 124, 2))
+EAST_GROUPS = ((12, 9, 0, 0), (29, 5, 0, 1), (38, 1, 0, 2))
+TO_WEST = (0, 32, 64, 96, 16, 48, 80, 112)
+TO_EAST = (112, 16, 48, 80, 0, 32, 64, 96)
 
 
 def begin_kernel(
     d_ref, v_ref, m_ref, r_ref, tr_ref, id_ref,
     west_ref, east_ref, north_ref, south_ref, ln_ref, ls_ref, sent_ref,
-    buf, west_buf, east_buf, tr_buf, sent_buf, id_buf, in_sem, row_sem, out_sem, tr_sem, sent_sem,
+    buf, west_buf, east_buf, tr_buf, sent_buf, id_buf, row_buf, in_sem, row_sem, out_sem, tr_sem, sent_sem,
 ):
     copy = pltpu.make_async_copy
+    face_rows = copy(id_ref, row_buf, sent_sem.at[8])
+    face_rows.start()
     loads = []
     for z in range(5):
         loads.append(
@@ -146,10 +177,6 @@
         at = pl.ds(64 * g, 64)
         records.append(copy(tr_ref.at[:, at], tr_buf.at[:, at], tr_sem.at[g]))
         records[g].start()
-    mine = lane_ids((N, 4 * N)) // STEPS == lax.broadcasted_iota(jnp.int32, (N, 4 * N), 0)
-    spread = jnp.where(mine, jnp.broadcast_to(id_ref[...].astype(F32), (N, 4 * N)), 0.0).astype(BF16)
-    step = lax.broadcasted_iota(jnp.int32, (4 * N, N), 0) % STEPS == lane_ids((4 * N, N))
-    id_buf[...] = dot(spread, jnp.where(step, 1.0, 0.0).astype(BF16))
     lane = lane_ids((N, N))
     stores = []
     for z in range(5):
@@ -162,20 +189,25 @@
             stores.append(copy(buf.at[z, at, 0:H], low.at[:, z], row_sem.at[z, 2 * i + 1]))
         for c in stores[-4:]:
             c.start()
-        west = buf[z, 0]
-        east = pltpu.roll(west, N - 112, 1)
-        for a in range(1, 8):
-            x = buf[z, a]
-            west = jnp.where(lane < 16 * a, west, pltpu.roll(x, 16 * a, 1))
-            east = jnp.where(
-                lane < 16 * a, east, pltpu.roll(x, (16 * a - 112) % N, 1) if a != 7 else x
-            )
-        west_buf[z] = west
-        east_buf[z] = east
+        packed = []
+        for h in range(2):
+            x = buf[z, 4 * h]
+            for a in range(1, 4):
+                mask = (lane >= 32 * a - 16) & (lane < 32 * a + 16)
+                x = jnp.where(mask, pltpu.roll(buf[z, 4 * h + a], 32 * a, 1), x)
+            packed.append(x)
+        other = pltpu.roll(packed[1], 16, 1)
+        west_buf[z] = jnp.where(lane % 32 < 16, packed[0], other)
+        east_buf[z] = jnp.where(lane % 32 < 16, other, packed[0])
         stores.append(copy(west_buf.at[z], west_ref.at[z], out_sem.at[z, 0]))
         stores.append(copy(east_buf.at[z], east_ref.at[z], out_sem.at[z, 1]))
         for c in stores[-2:]:
             c.start()
+    face_rows.wait()
+    mine = lane_ids((N, 4 * N)) // STEPS == lax.broadcasted_iota(jnp.int32, (N, 4 * N), 0)
+    spread = jnp.where(mine, jnp.broadcast_to(row_buf[...].astype(F32), (N, 4 * N)), 0.0).astype(BF16)
+    step = lax.broadcasted_iota(jnp.int32, (4 * N, N), 0) % STEPS == lane_ids((4 * N, N))
+    id_buf[...] = dot(spread, jnp.where(step, 1.0, 0.0).astype(BF16))
     lane = lane_ids((16, N))
     for g in range(8):
         records[g].wait()
@@ -216,7 +248,7 @@
     dma = pltpu.SemaphoreType.DMA
     return pl.pallas_call(
         begin_kernel,
-        in_specs=[hbm] * 5 + [pl.BlockSpec(memory_space=pltpu.VMEM)],
+        in_specs=[hbm] * 6,
         out_specs=[hbm] * 7,
         out_shape=[pltpu.HBM((5, N, N), F32)] * 2
         + [pltpu.HBM((6, 5, H, N), F32)] * 2
@@ -229,15 +261,16 @@
             pltpu.VMEM((9, 4 * N, N), F32),
             pltpu.VMEM((40 * N, N), F32),
             pltpu.VMEM((N, N), F32),
+            pltpu.VMEM((1, STEPS * N), jnp.int32),
             dma((5, 4)),
             dma((5, 4)),
             dma((5, 2)),
             dma((8,)),
-            dma((8,)),
+            dma((9,)),
         ],
         compiler_params=pltpu.CompilerParams(vmem_limit_bytes=20 * 1024 * 1024),
         name="begin",
-    )(*in_hbm(d, v, m, r, records), ids)
+    )(*in_hbm(d, v, m, r, records, ids))
 
 
 def coefs_kernel(m_ref, r_ref, re_ref, rw_ref, out_ref):
@@ -258,13 +291,16 @@
     three(0, m_ref[0], r_ref[0], pick(lane % 4))
     mod = rho = jnp.ones(shape, F32)
     node = jnp.zeros(shape, jnp.int32)
-    for groups, src, base in ((WEST_GROUPS, rw_ref[0], 112), (EAST_GROUPS, re_ref[0], 0)):
+    for groups, src, base, at_lane in (
+        (WEST_GROUPS, rw_ref[0], 112, TO_EAST),
+        (EAST_GROUPS, re_ref[0], 0, TO_WEST),
+    ):
         for c in range(3):
             for off, width, col, _ in groups:
                 at = 40 * c + off
                 mask = (lane >= at) & (lane < at + width)
-                mod = jnp.where(mask, pltpu.roll(src, (at - 96 - (col - base)) % N, 1), mod)
-                rho = jnp.where(mask, pltpu.roll(src, (at - 112 - (col - base)) % N, 1), rho)
+                mod = jnp.where(mask, moved(src, at - at_lane[6] - (col - base)), mod)
+                rho = jnp.where(mask, moved(src, at - at_lane[7] - (col - base)), rho)
                 node = jnp.where(mask, lane - at, node)
     three(3, mod, rho, pick(node % 4))
 
@@ -281,29 +317,45 @@
     )(m, r, re, rw)
 
 
-def place_kernel(
-    arr_ref, co_hbm, b_ref, strip_ref, north_ref, south_ref,
-    inj_ref, last_ref, side_ref, vid_ref, ids_ref, co_ref, sem,
-):
-    to_co = pltpu.make_async_copy(co_hbm, co_ref, sem.at[1])
+def place_kernel(*refs):
+    (arr_ref, co_hbm), own, refs = refs[:2], refs[2:10], refs[10:]
+    (b_ref, strip_ref, north_ref, south_ref), fetched, refs = refs[:4], refs[4:18], refs[18:]
+    inj_ref, side_ref, vid_ref, ids_ref, co_ref, sem, own_sem = refs
+    copy = pltpu.make_async_copy
+    lane = lane_ids((N, N))
+    plane = jnp.where(lane < 8, lane % 4, lane - 5)
+    slot = jnp.where(lane < 4, 16, 8)
+    where_to = (arr_ref[:, 36, :].astype(jnp.int32) + N * plane) * slot
+    vid_ref[...] = jnp.transpose(where_to)[:16]
+    to_scalar = copy(vid_ref, ids_ref, sem.at[0])
+    to_scalar.start()
+    to_co = copy(co_hbm, co_ref, sem.at[1])
     to_co.start()
-    lane = lane_ids((N, N))
-    plane = jnp.where(lane < 4, lane, jnp.where(lane < 8, lane - 4, lane - 5))
-    vid_ref[...] = arr_ref[:, 36, :].astype(jnp.int32) + N * plane
-    to_scalar = pltpu.make_async_copy(vid_ref, ids_ref, sem.at[0])
-    to_scalar.start()
+    node = pl.ds(0, 32)
+    moves = []
+    for ch in range(4):
+        moves.append((own[0].at[ch], fetched[ch].at[:, :, node]))
+        moves.append((own[1].at[ch], fetched[4 + ch].at[:, :, node]))
+    for m in range(2):
+        moves.append((own[2].at[m], fetched[8].at[m, :, 0:4, node]))
+        moves.append((own[3].at[m], fetched[9].at[m, :, :, node]))
+        moves.append((own[4].at[m], fetched[10].at[m, :, :, node]))
+    for i in (5, 6, 7):
+        moves.append((own[i], fetched[6 + i].at[:, :, node]))
+    moves = [copy(x, y, own_sem.at[i]) for i, (x, y) in enumerate(moves)]
     to_scalar.wait()
+    for c in moves:
+        c.start()
 
     def body(s, carry):
+        tail = arr_ref[s, 32:40, :]
         for t in range(STEPS):
-            r = ids_ref[s, t]
-            inj_ref[pl.ds(pl.multiple_of(r * 8, 8), 8), :] = arr_ref[s, pl.ds(t, 8, stride=4), :]
-            last_ref[pl.ds(r, 1), :] = arr_ref[s, 32 + t : 33 + t, :]
-        sides = arr_ref[s, 36:40, :]
+            at = pl.multiple_of(ids_ref[t, s], 16)
+            inj_ref[pl.ds(at, 8), :] = arr_ref[s, pl.ds(t, 8, stride=4), :]
+            inj_ref[pl.ds(at + 8, 8), :] = tail
         for i in range(2):
             for t in range(3):
-                at = pl.multiple_of(ids_ref[s, 4 + 4 * i + t] * 4, 4)
-                side_ref[pl.ds(at, 4), :] = sides
+                side_ref[pl.ds(pl.multiple_of(ids_ref[4 + 4 * i + t, s], 8), 8), :] = tail
         return carry
 
     lax.fori_loop(0, 128, body, 0, unroll=8)
@@ -316,20 +368,17 @@
         co = [co_ref[i, rows, :] for i in range(6)]
         for t in range(STEPS):
             for c in range(3):
-                base = (t * N + y) * 8
-                inc = inj_ref[pl.ds(base + c, 8, stride=8), :]
-                vel = inj_ref[pl.ds(base + 3 + c, 8, stride=8), :]
-                if c < 2:
-                    dis = inj_ref[pl.ds(base + 6 + c, 8, stride=8), :]
-                else:
-                    dis = last_ref[pl.ds(t * N + y, 8), :]
+                base = (t * N + y) * 16
+                inc = inj_ref[pl.ds(base + c, 8, stride=16), :]
+                vel = inj_ref[pl.ds(base + 3 + c, 8, stride=16), :]
+                dis = inj_ref[pl.ds(base + (6 + c if c < 2 else 8 + t), 8, stride=16), :]
                 b_ref[t, c, rows, :] = co[0] * inc + co[1] * vel + co[2] * dis
         b = None
         for rho in range(3):
             x = jnp.zeros((8, N), F32)
             for i, groups in enumerate((WEST_GROUPS, EAST_GROUPS)):
                 for off, width, _, t in groups:
-                    part = side_ref[pl.ds(((3 * i + t) * N + y) * 4 + 1 + rho, 8, stride=4), :]
+                    part = side_ref[pl.ds(((3 * i + t) * N + y) * 8 + 5 + rho, 8, stride=8), :]
                     mask = (lane >= off) & (lane < off + width)
                     for c in (1, 2):
                         mask = mask | ((lane >= 40 * c + off) & (lane < 40 * c + off + width))
@@ -354,35 +403,49 @@
             x = b_ref.at[t, ch] if ch < 3 else strip_ref.at[t]
             north_ref[ch, at : at + n] = x[N - n :, :]
             south_ref[ch, at : at + n] = x[:n, :]
-
-
-def place(arrived, co):
+    for c in moves:
+        c.wait()
+
+
+PREPARED = (
+    *[jax.ShapeDtypeStruct((5, 4, E, N), F32)] * 8,
+    jax.ShapeDtypeStruct((2, 5, 5, E, N), F32),
+    jax.ShapeDtypeStruct((2, 5, 4, E, N), F32),
+    jax.ShapeDtypeStruct((2, 5, 4, E, N), F32),
+    jax.ShapeDtypeStruct((5, 4, E, 256), F32),
+    jax.ShapeDtypeStruct((2, 4, E, N), F32),
+    jax.ShapeDtypeStruct((2, 4, E, N), F32),
+)
+
+
+def place(arrived, co, own):
     whole = pl.BlockSpec(memory_space=pltpu.VMEM)
     return pl.pallas_call(
         place_kernel,
-        in_specs=[whole, pl.BlockSpec(memory_space=pltpu.HBM)],
-        out_specs=[whole] * 4,
+        in_specs=[whole] + [pl.BlockSpec(memory_space=pltpu.HBM)] * 9,
+        out_specs=[whole] * 18,
         out_shape=[
             jax.ShapeDtypeStruct((STEPS, 3, N, N), F32),
             jax.ShapeDtypeStruct((3, N, N), F32),
             jax.ShapeDtypeStruct((4, 24, N), F32),
             jax.ShapeDtypeStruct((4, 24, N), F32),
+            *PREPARED,
         ],
         scratch_shapes=[
-            pltpu.VMEM((STEPS * N * 8, N), F32),
-            pltpu.VMEM((STEPS * N, N), F32),
-            pltpu.VMEM((6 * N * 4, N), F32),
-            pltpu.VMEM((N, N), jnp.int32),
-            pltpu.SMEM((N, N), jnp.int32),
+            pltpu.VMEM((STEPS * N * 16, N), F32),
+            pltpu.VMEM((6 * N * 8, N), F32),
+            pltpu.VMEM((16, N), jnp.int32),
+            pltpu.SMEM((16, N), jnp.int32),
             pltpu.VMEM((6, N, N), F32),
             pltpu.SemaphoreType.DMA((2,)),
+            pltpu.SemaphoreType.DMA((17,)),
         ],
         compiler_params=pltpu.CompilerParams(vmem_limit_bytes=VMEM_LIMIT),
         name="place",
-    )(arrived, *in_hbm(co))
-
-
-def line_forces(d, k, kn, mn_ref, ce_ref, grad_ref, back_ref, channels, emit):
+    )(arrived, *in_hbm(co, *own))
+
+
+def line_forces(d, k, kn, mn_ref, md_ref, ce_ref, grad_ref, back_ref, channels, emit):
     live = E if channels == 4 else 32
     rows = 5 * 4 * live
 
@@ -391,8 +454,8 @@
         for z in range(5):
             v = [d[ch][z, j] for j in range(4)]
             v.append(pltpu.roll(v[0], E - 1, 0))
-            g = apply5(DER, v)
-            r = apply5(BACK * W[z], [g[i] * mn_ref[m, z, i] for i in range(5)])
+            g = slopes(v)
+            r = tested([g[i] * mn_ref[m, z, i] for i in range(5)])
             r[0] = r[0] + pltpu.roll(r[4], 1, 0)
             for j in range(4):
                 kn[ch][z, j] = r[j]
@@ -401,8 +464,8 @@
         m = ch // 3
         for j in range(4):
             x = [d[ch][z, j, :live] for z in range(5)]
-            g = apply5(DER, x)
-            r = apply5(BACK * PERIODIC[j], [g[z] * mn_ref[m, z, j, :live] for z in range(5)])
+            g = slopes(x)
+            r = tested([g[z] * md_ref[m, z, j, :live] for z in range(5)])
             for z in range(5):
                 emit(ch, j, z, x[z], (k[ch][z, j, :live] + kn[ch][z, j, :live]) + r[z])
 
@@ -429,11 +492,11 @@
         depth(3)
 
 
-def expand(xe, xw, src, step):
+def expand(xe, xw, first, step):
     out = None
     for c in range(3):
-        p = lane_move(xe, 32 * c - src - step * c, 32 * c)
-        p = p + lane_move(xw, 32 * c + 16 - src - step * c, 32 * c + 16)
+        p = lane_move(xe, 32 * c - TO_WEST[first + step * c], 32 * c)
+        p = p + lane_move(xw, 32 * c + 16 - TO_EAST[first + step * c], 32 * c + 16)
         out = p if out is None else out + p
     return out
 
@@ -441,7 +504,9 @@
 def fields(mod, rho, j, z, put):
     f = lambda a: float(np.float32(a))
     ew = east_weight(mod.shape)
-    put("mn", 0.5 * mod * ew)
+    half = 0.5 * mod * ew
+    put("mn", half * f(POINT[j] * W[z]))
+    put("md", half * f(POINT[z] * PERIODIC[j]))
     put("di", DT / (0.125 * rho * ew * (f(PERIODIC[j]) * f(W[z]))))
     if z == 0:
         area = 0.25 * ew * f(PERIODIC[j])
@@ -462,22 +527,22 @@
 
 def early_kernel(
     d_ref, v_ref, m_ref, r_ref, re_ref, rw_ref, sel_ref, qw_ref,
-    d_out, v_out, mn_out, di_out, ce_out, ai_out, as_out,
+    d_out, v_out, mn_out, md_out, di_out, ce_out, ai_out, as_out,
 ):
     f = lambda a: float(np.float32(a))
-    outs = {"mn": mn_out, "di": di_out, "ai": ai_out, "as": as_out}
+    outs = {"mn": mn_out, "md": md_out, "di": di_out, "ai": ai_out, "as": as_out}
 
     def plane(z):
         for j in range(4):
             own = pl.ds(j, 32, stride=4)
             xe, xw = re_ref[z, own, :], rw_ref[z, own, :]
-            vs = [v_ref[c, z, own, :] for c in range(3)] + [expand(xe, xw, 48, 16)]
-            ds = [d_ref[c, z, own, :] for c in range(3)] + [expand(xe, xw, 0, 16)]
+            vs = [v_ref[c, z, own, :] for c in range(3)] + [expand(xe, xw, 3, 1)]
+            ds = [d_ref[c, z, own, :] for c in range(3)] + [expand(xe, xw, 0, 1)]
             for ch in range(4):
                 v_out[ch, z, j] = vs[ch]
                 d_out[ch, z, j] = ds[ch] + DT * vs[ch]
-            mods = [m_ref[z, own, :], expand(xe, xw, 96, 0)]
-            rhos = [r_ref[z, own, :], strip_density(expand(xe, xw, 112, 0))]
+            mods = [m_ref[z, own, :], expand(xe, xw, 6, 0)]
+            rhos = [r_ref[z, own, :], strip_density(expand(xe, xw, 7, 0))]
             for m in range(2):
 
                 def put(name, x):
@@ -492,7 +557,7 @@
         plane(z)
 
 
-OWN_SHAPES = ((4, 5, 4, 32, N),) * 2 + ((2, 5, 4, 32, N),) * 2 + ((5, 4, 32, 256),) + ((2, 4, 32, N),) * 2
+OWN_SHAPES = ((4, 5, 4, 32, N),) * 2 + ((2, 5, 4, 32, N),) * 3 + ((5, 4, 32, 256),) + ((2, 4, 32, N),) * 2
 
 
 def early(d, v, m, r, re, rw, sel, qw):
@@ -500,7 +565,7 @@
     return pl.pallas_call(
         early_kernel,
         in_specs=[whole] * 8,
-        out_specs=[whole] * 7,
+        out_specs=[whole] * 8,
         out_shape=[jax.ShapeDtypeStruct(x, F32) for x in OWN_SHAPES],
         compiler_params=pltpu.CompilerParams(vmem_limit_bytes=16 * 1024 * 1024),
         name="early",
@@ -508,29 +573,18 @@
 
 
 def prepare_kernel(*refs):
-    own, halos, tables, refs = refs[:7], refs[7:11], refs[11:15], refs[15:]
-    (d0, d1, d2, d3, v0, v1, v2, v3, mn_ref, di_ref, ce_ref, ai_ref, as_ref), refs = refs[:13], refs[13:]
+    halos, tables, refs = refs[14:18], refs[18:22], refs[22:]
+    (d0, d1, d2, d3, v0, v1, v2, v3), refs = refs[:8], refs[8:]
+    (mn_ref, md_ref, di_ref, ce_ref, ai_ref, as_ref), refs = refs[:6], refs[6:]
     (k0, k1, k2, k3, n0, n1, n2, n3), refs = refs[:8], refs[8:]
-    buffers, (own_sem, halo_sem) = refs[:8], refs[8:]
+    buffers, (halo_sem,) = refs[:8], refs[8:]
     d_ref, v_ref = (d0, d1, d2, d3), (v0, v1, v2, v3)
     copy = pltpu.make_async_copy
-    node = pl.ds(0, 32)
     late = [copy(x, y, halo_sem.at[i]) for i, (x, y) in enumerate(zip((*halos, *tables), buffers))]
-    moves = []
-    for ch in range(4):
-        moves.append((own[0].at[ch], d_ref[ch].at[:, :, node]))
-        moves.append((own[1].at[ch], v_ref[ch].at[:, :, node]))
-    for m in range(2):
-        moves.append((own[2].at[m], mn_ref.at[m, :, 0:4, node]))
-        moves.append((own[3].at[m], di_ref.at[m, :, :, node]))
-    moves.append((own[4], ce_ref.at[:, :, node]))
-    moves.append((own[5], ai_ref.at[:, :, node]))
-    moves.append((own[6], as_ref.at[:, :, node]))
-    moves = [copy(x, y, own_sem.at[i]) for i, (x, y) in enumerate(moves)]
-    for c in late + moves:
+    for c in late:
         c.start()
     n_ref, s_ref, cn_ref, cs_ref, sel_ref, qw_ref, grad_ref, back_ref = buffers
-    outs = {"mn": mn_ref, "di": di_ref, "ai": ai_ref, "as": as_ref}
+    outs = {"mn": mn_ref, "md": md_ref, "di": di_ref, "ai": ai_ref, "as": as_ref}
     f = lambda a: float(np.float32(a))
     for c in late:
         c.wait()
@@ -544,13 +598,13 @@
     for z in range(5):
         for j in range(4):
             xe, xw, mod, rho = (halo((i, z), j, cn_ref, cs_ref) for i in (2, 3, 0, 1))
-            vs = [halo((3 + c, z), j) for c in range(3)] + [expand(xe, xw, 48, 16)]
-            ds = [halo((c, z), j) for c in range(3)] + [expand(xe, xw, 0, 16)]
+            vs = [halo((3 + c, z), j) for c in range(3)] + [expand(xe, xw, 3, 1)]
+            ds = [halo((c, z), j) for c in range(3)] + [expand(xe, xw, 0, 1)]
             for ch in range(4):
                 v_ref[ch][z, j, rest] = vs[ch]
                 d_ref[ch][z, j, rest] = ds[ch] + DT * vs[ch]
-            mods = [mod, expand(xe, xw, 96, 0)]
-            rhos = [rho, strip_density(expand(xe, xw, 112, 0))]
+            mods = [mod, expand(xe, xw, 6, 0)]
+            rhos = [rho, strip_density(expand(xe, xw, 7, 0))]
             for m in range(2):
 
                 def put(name, x):
@@ -565,8 +619,6 @@
         for j in range(4):
             at = (z * 4 + j) * 8
             ce_ref[z, j, rest] = c[at : at + 8] * (f(W[z]) * f(PERIODIC[j]))
-    for c in moves:
-        c.wait()
     for m in range(2):
         for z in range(5):
             mn_ref[m, z, 4] = pltpu.roll(mn_ref[m, z, 0], E - 1, 0)
@@ -579,37 +631,30 @@
         v_ref[ch][z, j] = v - di_ref[m, z, j] * k
 
     line_forces(
-        d_ref, (k0, k1, k2, k3), (n0, n1, n2, n3), mn_ref, ce_ref, grad_ref, back_ref, 4, emit
+        d_ref, (k0, k1, k2, k3), (n0, n1, n2, n3), mn_ref, md_ref, ce_ref, grad_ref, back_ref, 4, emit
     )
 
 
-def prepare(own, halos, tables):
+def prepare(fetched, halos, tables):
     grad, back, sel, qw = tables
     whole = pl.BlockSpec(memory_space=pltpu.VMEM)
-    state = jax.ShapeDtypeStruct((5, 4, E, N), F32)
     late = (*halos, sel, qw, grad, back)
     return pl.pallas_call(
         prepare_kernel,
-        in_specs=[pl.BlockSpec(memory_space=pltpu.HBM)] * 15,
-        out_specs=[whole] * 13,
-        out_shape=[
-            *[state] * 8,
-            jax.ShapeDtypeStruct((2, 5, 5, E, N), F32),
-            jax.ShapeDtypeStruct((2, 5, 4, E, N), F32),
-            jax.ShapeDtypeStruct((5, 4, E, 256), F32),
-            jax.ShapeDtypeStruct((2, 4, E, N), F32),
-            jax.ShapeDtypeStruct((2, 4, E, N), F32),
-        ],
+        in_specs=[whole] * 14 + [pl.BlockSpec(memory_space=pltpu.HBM)] * 8,
+        out_specs=[whole] * 14,
+        out_shape=PREPARED,
+        input_output_aliases={i: i for i in range(14)},
         scratch_shapes=[pltpu.VMEM((5, 4, E, N), F32)] * 8
         + [pltpu.VMEM(x.shape, x.dtype) for x in late]
-        + [pltpu.SemaphoreType.DMA((15,)), pltpu.SemaphoreType.DMA((8,))],
+        + [pltpu.SemaphoreType.DMA((8,))],
         compiler_params=pltpu.CompilerParams(vmem_limit_bytes=VMEM_LIMIT),
         name="prepare",
-    )(*in_hbm(*own, *late))
+    )(*fetched, *in_hbm(*late))
 
 
 def steps_kernel(
-    i0, i1, i2, i3, u0, u1, u2, u3, mn_ref, di_ref, ce_ref, ai_ref, as_ref,
+    i0, i1, i2, i3, u0, u1, u2, u3, mn_ref, md_ref, di_ref, ce_ref, ai_ref, as_ref,
     b_ref, bs_ref, bn_ref, bo_ref, grad_ref, back_ref,
     dout_ref, vout_ref,
     d0, d1, d2, d3, v0, v1, v2, v3, k0, k1, k2, k3, n0, n1, n2, n3, f_ref,
@@ -656,7 +701,7 @@
             v_ref[ch][z, j] = v
             d_ref[ch][z, j] = d + DT * v
 
-        line_forces(d_ref, k_ref, kn_ref, mn_ref, ce_ref, grad_ref, back_ref, 4, emit)
+        line_forces(d_ref, k_ref, kn_ref, mn_ref, md_ref, ce_ref, grad_ref, back_ref, 4, emit)
         return carry
 
     lax.fori_loop(1, 3, step, 0)
@@ -665,7 +710,7 @@
         dout_ref[ch, z, pl.ds(j, 32, stride=4), :] = d
         vout_ref[ch, z, pl.ds(j, 32, stride=4), :] = velocity(3, ch, j, z, d, k)
 
-    line_forces(d_ref, k_ref, kn_ref, mn_ref, ce_ref, grad_ref, back_ref, 3, final)
+    line_forces(d_ref, k_ref, kn_ref, mn_ref, md_ref, ce_ref, grad_ref, back_ref, 3, final)
 
 
 def steps(prepared, b, bs, bn, bo, tables):
@@ -673,7 +718,7 @@
     whole = pl.BlockSpec(memory_space=pltpu.VMEM)
     return pl.pallas_call(
         steps_kernel,
-        in_specs=[whole] * 19,
+        in_specs=[whole] * 20,
         out_specs=[whole] * 2,
         out_shape=[jax.ShapeDtypeStruct((3, 5, N, N), F32)] * 2,
         scratch_shapes=[pltpu.VMEM((5, 4, E, N), F32)] * 16 + [pltpu.VMEM((4, 4, 4, E, N), F32)],
@@ -701,13 +746,13 @@
     corner_south = shifted(late_north, "src", 1)
     co = coefs(modulus, density, from_east, from_west)
     own = early(displacement, velocity, modulus, density, from_east, from_west, *tables[2:])
-    b, b_strip, b_north, b_south = place(arrived, co)
+    b, b_strip, b_north, b_south, *fetched = place(arrived, co, own)
     b_from_south = shifted(b_north, "src", 1)
     b_from_north = shifted(b_south, "src", -1)
     from_north, from_south, corner_north, corner_south, _ = lax.optimization_barrier(
         (from_north, from_south, corner_north, corner_south, b)
     )
-    prepared = prepare(own, (from_north, from_south, corner_north, corner_south), tables)
+    prepared = prepare(fetched, (from_north, from_south, corner_north, corner_south), tables)
     return steps(prepared, b, b_strip, b_from_north, b_from_south, tables)
 
 

time: 103 us -> 107 us (1.039)
  local copies, waits for them, and re-layouts: 6.7 us -> 11.2 us
  Pallas kernels: 35.1 us -> 32.6 us
    unnamed x48 -> x42, local copies, waits for them, and re-layouts: 6.7 us -> 11.2 us
    pallas_call x5, Pallas kernels: 32.7 us -> 30.2 us  [the longest x1 11.9 us: steps(): pl.pallas_call(steps_kernel, in_specs=[whole] * 20, out_specs=[whole] * 2...]
  transfers between devices with their start and end apart: 9 -> 9, of which waited for: 2 -> 3; matrix products, arithmetic and copies ran while one was open for 1% -> 2% of each run, Pallas kernels for 17% -> 14%
where the time goes in v2:
time: 107 us; the launch traced here: 106 us
  Pallas kernels  32.6 us (30%)
  waiting for transfers between devices  31.1 us (29%)
  starting transfers between devices  29 us (27%)
  local copies, waits for them, and re-layouts  11.2 us (10%)
  other arithmetic  1.74 us (2%)
    ppermute x8, waiting for transfers between devices, shifted(): lax.ppermute(block, axis, [((i - distance) % n, i) for i in range(n)])  31.1 us
    ppermute x8, starting transfers between devices, shifted(): lax.ppermute(block, axis, [((i - distance) % n, i) for i in range(n)])  17.8 us
    pallas_call x1, Pallas kernels, steps(): pl.pallas_call(steps_kernel, in_specs=[whole] * 20, out_specs=[whole] * 2...  11.9 us
    unnamed x42, local copies, waits for them, and re-layouts  11.2 us
    all_to_all x1, starting transfers between devices, local(): lax.all_to_all(sent.reshape(N, 40, N), ('src', 'reg'), split_axis=0, conc...  11.2 us
    pallas_call x1, Pallas kernels, prepare(): pl.pallas_call(prepare_kernel, in_specs=[whole] * 14 + [pl.BlockSpec(memo...  5.9 us
    pallas_call x1, Pallas kernels, begin(): pl.pallas_call(begin_kernel, in_specs=[hbm] * 6, out_specs=[hbm] * 7, out...  5.41 us
    pallas_call x1, Pallas kernels, place(): pl.pallas_call(place_kernel, in_specs=[whole] + [pl.BlockSpec(memory_spac...  5.33 us
  transfers between devices with their start and end apart: 9, of which 3 were waited for; matrix products, arithmetic and copies ran while one was open for 2% of the time, Pallas kernels for 14%

profile of v2, /device:TPU:0, one launch (start us, length us, event | category | flops | bytes accessed | tf_op | source)
XLA Modules:
  0.0 106.4 jit_solution(1570316314550663658)
XLA Ops:
  0.6 5.4 %begin.1 = (f32[5,128,128]{2,1,0:T(8,128)}, f32[5,128,128]{2,1,0:T(8,128)}, f32[6,5,16,128]{3,2,1,0:T(8,128)}, f32[6,5,16,128]{3,2,1,0:T(8,128)}, f32[2,5,16,128...) custom-call(f32[3,5,128,128]{3,2,1,0:T(8,128)} %d_ref.3, f32[3,5,128,128]{3,2,1,0:T(8,128)} %v_ref.3, ...), custom_call_target="tpu_custom_call" | custom-call | tf_op jit(solution)/shard_map/begin/pallas_call | solution.py:249
  6.1 11.2 %all-to-all-start = ((f32[128,40,128]{2,1,0:T(8,128)}), f32[128,40,128]{2,1,0:T(8,128)S(1)}, u32[]{:S(2)}, u32[]{:S(2)}) async-start(f32[128,40,128]{2,1,0:T(8,128)} %bitcast.8), calls=%async_computation | async-start | bytes 5242880 | tf_op jit(solution)/shard_map/all_to_all | solution.py:739
  17.3 0.0 copy-start.16
  17.3 0.0 copy-start.19
  17.3 3.5 %collective-permute-start = (f32[5,128,128]{2,1,0:T(8,128)}, f32[5,128,128]{2,1,0:T(8,128)S(1)}, u32[]{:S(2)}, u32[]{:S(2)}) collective-permute-start(f32[5,128,128]{2,1,0:T(8,128)} %get-tuple-element.54), channel_id=1, source_target_pairs={{1,0},{2,1},{3,2},{4,3},{5,4},{6,5},{7,6},{8,7},{9,8},{10,9},{11,1... | collective-permute-start | bytes 983048 | tf_op jit(solution)/shard_map/ppermute | solution.py:112
  20.8 5.0 %collective-permute-start.2 = (f32[6,5,16,128]{3,2,1,0:T(8,128)}, f32[6,5,16,128]{3,2,1,0:T(8,128)}, u32[]{:S(2)}, u32[]{:S(2)}) collective-permute-start(f32[6,5,16,128]{3,2,1,0:T(8,128)} %get-tuple-element.78), channel_id=1, source_target_pairs={{16,0},{32,16},{48,32},{64,48},{80,64},{96,80},{112,96},{0,112},{1... | collective-permute-start | bytes 737288 | tf_op jit(solution)/shard_map/ppermute | solution.py:112
  25.9 26.9 %collective-permute-done.re_ref = f32[5,128,128]{2,1,0:T(8,128)S(1)} collective-permute-done((f32[5,128,128]{2,1,0:T(8,128)}, f32[5,128,128]{2,1,0:T(8,128)S(1)}, u32[]{:S(2)}, u32[]{:S(2)}) %collective-permute-start) | collective-permute-done | bytes 327712 | tf_op jit(solution)/shard_map/ppermute | solution.py:112
  52.7 3.2 %collective-permute-done.1.rw_ref = f32[5,128,128]{2,1,0:T(8,128)S(1)} collective-permute-done((f32[5,128,128]{2,1,0:T(8,128)}, f32[5,128,128]{2,1,0:T(8,128)S(1)}, u32[]{:S(2)}, u32[]{:S(2)}) %collective-permute-start.1) | collective-permute-done | bytes 327712 | tf_op jit(solution)/shard_map/ppermute | solution.py:112
  55.9 1.7 %fusion = (f32[4,5,16,128]{3,2,1,0:T(8,128)}, f32[4,5,16,128]{3,2,1,0:T(8,128)}) fusion(f32[1,5,128,128]{3,2,1,0:T(8,128)S(1)} %bitcast.7, f32[1,5,128,128]{3,2,1,0:T(8,128)S(1)} %bitcast.6, f32[2,5,16,128]{3,2,1,0:T(8,128)S(1)} %copy-done.20, f32[2,5,16,128]{3,2,1,0:T(8,128)} %get-tuple-element.80), kind=kLoop, calls=%fused_computation.1 | loop fusion | flops 163840 | bytes 1146880 | tf_op jit(solution)/shard_map/concatenate | solution.py:744
  57.7 2.7 %collective-permute-start.5 = (f32[4,5,16,128]{3,2,1,0:T(8,128)}, f32[4,5,16,128]{3,2,1,0:T(8,128)}, u32[]{:S(2)}, u32[]{:S(2)}) collective-permute-start(f32[4,5,16,128]{3,2,1,0:T(8,128)} %get-tuple-element.104), channel_id=1, source_target_pairs={{112,0},{0,16},{16,32},{32,48},{48,64},{64,80},{80,96},{96,112},{1... | collective-permute-start | bytes 491528 | tf_op jit(solution)/shard_map/ppermute | solution.py:112
  60.4 3.0 %collective-permute-start.4 = (f32[4,5,16,128]{3,2,1,0:T(8,128)}, f32[4,5,16,128]{3,2,1,0:T(8,128)}, u32[]{:S(2)}, u32[]{:S(2)}) collective-permute-start(f32[4,5,16,128]{3,2,1,0:T(8,128)} %get-tuple-element.105), channel_id=1, source_target_pairs={{16,0},{32,16},{48,32},{64,48},{80,64},{96,80},{112,96},{0,112},{1... | collective-permute-start | bytes 491528 | tf_op jit(solution)/shard_map/ppermute | solution.py:112
  63.3 2.4 %coefs.1.refs_1_ = f32[6,128,128]{2,1,0:T(8,128)} custom-call(f32[5,128,128]{2,1,0:T(8,128)} %m_ref.5, f32[5,128,128]{2,1,0:T(8,128)} %r_ref.5, f32[5,128,128]{2,1,0:T(8,128)} %copy-done.6, f32[5,128,128]{2,1,0:T(8,128)} %copy-done.8), custom_call_target="tpu_custom_call" | custom-call | tf_op jit(solution)/shard_map/coefs/pallas_call | solution.py:310
  65.7 1.2 %copy-done = f32[3,5,128,128]{3,2,1,0:T(8,128)S(1)} copy-done((f32[3,5,128,128]{3,2,1,0:T(8,128)S(1)}, f32[3,5,128,128]{3,2,1,0:T(8,128)}, u32[]{:S(2)}) %copy-start) | copy-done | bytes 983064
  66.9 1.2 %copy-done.1 = f32[3,5,128,128]{3,2,1,0:T(8,128)S(1)} copy-done((f32[3,5,128,128]{3,2,1,0:T(8,128)S(1)}, f32[3,5,128,128]{3,2,1,0:T(8,128)}, u32[]{:S(2)}) %copy-start.1) | copy-done | bytes 983064
  68.1 1.0 copy-done.7
  69.1 1.0 copy-done.9
  70.1 1.6 %early.1 = (f32[4,5,4,32,128]{4,3,2,1,0:T(8,128)S(1)}, f32[4,5,4,32,128]{4,3,2,1,0:T(8,128)S(1)}, f32[2,5,4,32,128]{4,3,2,1,0:T(8,128)S(1)}, f32[2,5,4,32,128]{4...) custom-call(f32[3,5,128,128]{3,2,1,0:T(8,128)S(1)} %copy-done, ...), custom_call_target="tpu_custom_call" | custom-call | tf_op jit(solution)/shard_map/early/pallas_call | solution.py:565
  71.7 1.1 %copy-done.10 = f32[4,5,4,32,128]{4,3,2,1,0:T(8,128)} copy-done((f32[4,5,4,32,128]{4,3,2,1,0:T(8,128)}, f32[4,5,4,32,128]{4,3,2,1,0:T(8,128)S(1)}, u32[]{:S(2)}) %copy-start.10) | copy-done | bytes 1310744
  72.8 1.1 %copy-done.11 = f32[4,5,4,32,128]{4,3,2,1,0:T(8,128)} copy-done((f32[4,5,4,32,128]{4,3,2,1,0:T(8,128)}, f32[4,5,4,32,128]{4,3,2,1,0:T(8,128)S(1)}, u32[]{:S(2)}) %copy-start.11) | copy-done | bytes 1310744
  73.9 0.8 copy-done.12
  74.7 0.8 copy-done.13
  75.6 0.8 copy-done.14
  76.4 0.8 copy-done.15
  77.2 0.7 copy-done.17
  77.9 0.7 copy-done.18
  78.6 5.3 %place.1 = (f32[4,3,128,128]{3,2,1,0:T(8,128)S(1)}, f32[3,128,128]{2,1,0:T(8,128)S(1)}, f32[4,24,128]{2,1,0:T(8,128)S(1)}, f32[4,24,128]{2,1,0:T(8,128)S(1)}, f3...) custom-call(f32[128,40,128]{2,1,0:T(8,128)S(1)} %all-to-all-done.ref, ...), custom_call_target="tpu_custom_call" | custom-call | tf_op jit(solution)/shard_map/place/pallas_call | solution.py:423
  83.9 2.9 %collective-permute-start.6 = (f32[4,24,128]{2,1,0:T(8,128)S(1)}, f32[4,24,128]{2,1,0:T(8,128)S(1)}, u32[]{:S(2)}, u32[]{:S(2)}) collective-permute-start(f32[4,24,128]{2,1,0:T(8,128)S(1)} %get-tuple-element.102), channel_id=1, source_target_pairs={{16,0},{32,16},{48,32},{64,48},{80,64},{96,80},{112,96},{0,112},{1... | collective-permute-start | bytes 147464 | tf_op jit(solution)/shard_map/ppermute | solution.py:112
  86.8 0.7 collective-permute-start.7
  87.5 0.0 copy-start.2
  87.5 5.9 %prepare.1 = (f32[5,4,40,128]{3,2,1,0:T(8,128)S(1)}, f32[5,4,40,128]{3,2,1,0:T(8,128)S(1)}, f32[5,4,40,128]{3,2,1,0:T(8,128)S(1)}, f32[5,4,40,128]{3,2,1,0:T(8,1...) custom-call(f32[5,4,40,128]{3,2,1,0:T(8,128)S(1)} %get-tuple-element, ...), custom_call_target="tpu_custom_call", output_to_operand_aliasing={{0}: (0, {}), {1}: (1, {}), {2}: (2, {}), {3}: (3, {}), {4}... | custom-call | tf_op jit(solution)/shard_map/prepare/pallas_call | solution.py:642
  93.5 1.0 collective-permute-done.7.bo_ref
  94.5 11.9 %steps.1 = (f32[3,5,128,128]{3,2,1,0:T(8,128)}, f32[3,5,128,128]{3,2,1,0:T(8,128)}) custom-call(f32[5,4,40,128]{3,2,1,0:T(8,128)S(1)} %get-tuple-element.87.i0, f32[5,4,40,128]{3,2,1,0:T(8,128)S(1)} %get-tuple-element.88.i1, f32[5,4,40,128]{3,2,1,0:T(8,128)S(1)} %get-tuple-element.89.i2, f32[5,4,40,128]{3,2,1,0:T(8,128)S(1)} %get-tuple-element.90.i3, ...), custom_call_target="tpu_custom_call" | custom-call | tf_op jit(solution)/shard_map/steps/pallas_call | solution.py:719
  (35 shorter events, 0.1 us)
Async XLA Ops:
  6.0 49.9 %copy-start.20 = (f32[2,5,16,128]{3,2,1,0:T(8,128)S(1)}, f32[2,5,16,128]{3,2,1,0:T(8,128)}, u32[]{:S(2)}) copy-start(f32[2,5,16,128]{3,2,1,0:T(8,128)} %get-tuple-element.81) | copy-start | bytes 245764
  6.1 72.5 %all-to-all-start = ((f32[128,40,128]{2,1,0:T(8,128)}), f32[128,40,128]{2,1,0:T(8,128)S(1)}, u32[]{:S(2)}, u32[]{:S(2)}) async-start(f32[128,40,128]{2,1,0:T(8,128)} %bitcast.8), calls=%async_computation | async-start | bytes 5242880 | tf_op jit(solution)/shard_map/all_to_all | solution.py:739
  17.2 48.5 %copy-start.4 = (f32[5,128,128]{2,1,0:T(8,128)S(1)}, f32[5,128,128]{2,1,0:T(8,128)}, u32[]{:S(2)}) copy-start(f32[5,128,128]{2,1,0:T(8,128)} %m_ref.5) | copy-start | bytes 983044
  17.3 48.5 %copy-start.5 = (f32[5,128,128]{2,1,0:T(8,128)S(1)}, f32[5,128,128]{2,1,0:T(8,128)}, u32[]{:S(2)}) copy-start(f32[5,128,128]{2,1,0:T(8,128)} %r_ref.5) | copy-start | bytes 983044
  17.3 48.4 %copy-start.16 = (bf16[256,256]{1,0:T(8,128)(2,1)S(1)}, bf16[256,256]{1,0:T(8,128)(2,1)}, u32[]{:S(2)}) copy-start(bf16[256,256]{1,0:T(8,128)(2,1)} %constant.10.clone.sel_ref.refs_18_) | copy-start | bytes 393220
  17.3 48.4 %copy-start.19 = (f32[1,256]{1,0:T(1,128)S(1)}, f32[1,256]{1,0:T(1,128)}, u32[]{:S(2)}) copy-start(f32[1,256]{1,0:T(1,128)} %constant.11.clone.qw_ref.refs_19_) | copy-start | bytes 3076
  17.3 35.5 %collective-permute-start = (f32[5,128,128]{2,1,0:T(8,128)}, f32[5,128,128]{2,1,0:T(8,128)S(1)}, u32[]{:S(2)}, u32[]{:S(2)}) collective-permute-start(f32[5,128,128]{2,1,0:T(8,128)} %get-tuple-element.54), channel_id=1, source_target_pairs={{1,0},{2,1},{3,2},{4,3},{5,4},{6,5},{7,6},{8,7},{9,8},{10,9},{11,1... | collective-permute-start | bytes 983048 | tf_op jit(solution)/shard_map/ppermute | solution.py:112
  20.8 35.1 %collective-permute-start.1 = (f32[5,128,128]{2,1,0:T(8,128)}, f32[5,128,128]{2,1,0:T(8,128)S(1)}, u32[]{:S(2)}, u32[]{:S(2)}) collective-permute-start(f32[5,128,128]{2,1,0:T(8,128)} %get-tuple-element.55), channel_id=1, source_target_pairs={{15,0},{0,1},{1,2},{2,3},{3,4},{4,5},{5,6},{6,7},{7,8},{8,9},{9,10... | collective-permute-start | bytes 983048 | tf_op jit(solution)/shard_map/ppermute | solution.py:112
  20.8 66.0 %collective-permute-start.2 = (f32[6,5,16,128]{3,2,1,0:T(8,128)}, f32[6,5,16,128]{3,2,1,0:T(8,128)}, u32[]{:S(2)}, u32[]{:S(2)}) collective-permute-start(f32[6,5,16,128]{3,2,1,0:T(8,128)} %get-tuple-element.78), channel_id=1, source_target_pairs={{16,0},{32,16},{48,32},{64,48},{80,64},{96,80},{112,96},{0,112},{1... | collective-permute-start | bytes 737288 | tf_op jit(solution)/shard_map/ppermute | solution.py:112
  25.9 61.6 %collective-permute-start.3 = (f32[6,5,16,128]{3,2,1,0:T(8,128)}, f32[6,5,16,128]{3,2,1,0:T(8,128)}, u32[]{:S(2)}, u32[]{:S(2)}) collective-permute-start(f32[6,5,16,128]{3,2,1,0:T(8,128)} %get-tuple-element.79), channel_id=1, source_target_pairs={{112,0},{0,16},{16,32},{32,48},{48,64},{64,80},{80,96},{96,112},{1... | collective-permute-start | bytes 737288 | tf_op jit(solution)/shard_map/ppermute | solution.py:112
  52.7 3.2 %copy-start.6 = (f32[5,128,128]{2,1,0:T(8,128)}, f32[5,128,128]{2,1,0:T(8,128)S(1)}, u32[]{:S(2)}) copy-start(f32[5,128,128]{2,1,0:T(8,128)S(1)} %collective-permute-done.re_ref) | copy-start | bytes 983044
  55.9 1.8 %copy-start.8 = (f32[5,128,128]{2,1,0:T(8,128)}, f32[5,128,128]{2,1,0:T(8,128)S(1)}, u32[]{:S(2)}) copy-start(f32[5,128,128]{2,1,0:T(8,128)S(1)} %collective-permute-done.1.rw_ref) | copy-start | bytes 983044
  57.7 29.8 %collective-permute-start.5 = (f32[4,5,16,128]{3,2,1,0:T(8,128)}, f32[4,5,16,128]{3,2,1,0:T(8,128)}, u32[]{:S(2)}, u32[]{:S(2)}) collective-permute-start(f32[4,5,16,128]{3,2,1,0:T(8,128)} %get-tuple-element.104), channel_id=1, source_target_pairs={{112,0},{0,16},{16,32},{32,48},{48,64},{64,80},{80,96},{96,112},{1... | collective-permute-start | bytes 491528 | tf_op jit(solution)/shard_map/ppermute | solution.py:112
  60.4 27.2 %collective-permute-start.4 = (f32[4,5,16,128]{3,2,1,0:T(8,128)}, f32[4,5,16,128]{3,2,1,0:T(8,128)}, u32[]{:S(2)}, u32[]{:S(2)}) collective-permute-start(f32[4,5,16,128]{3,2,1,0:T(8,128)} %get-tuple-element.105), channel_id=1, source_target_pairs={{16,0},{32,16},{48,32},{64,48},{80,64},{96,80},{112,96},{0,112},{1... | collective-permute-start | bytes 491528 | tf_op jit(solution)/shard_map/ppermute | solution.py:112
  65.7 1.2 %copy-start = (f32[3,5,128,128]{3,2,1,0:T(8,128)S(1)}, f32[3,5,128,128]{3,2,1,0:T(8,128)}, u32[]{:S(2)}) copy-start(f32[3,5,128,128]{3,2,1,0:T(8,128)} %d_ref.3) | copy-start | bytes 2949124
  66.9 1.2 %copy-start.1 = (f32[3,5,128,128]{3,2,1,0:T(8,128)S(1)}, f32[3,5,128,128]{3,2,1,0:T(8,128)}, u32[]{:S(2)}) copy-start(f32[3,5,128,128]{3,2,1,0:T(8,128)} %v_ref.3) | copy-start | bytes 2949124
  68.1 1.0 copy-start.7
  69.1 1.0 copy-start.9
  71.7 1.1 %copy-start.10 = (f32[4,5,4,32,128]{4,3,2,1,0:T(8,128)}, f32[4,5,4,32,128]{4,3,2,1,0:T(8,128)S(1)}, u32[]{:S(2)}) copy-start(f32[4,5,4,32,128]{4,3,2,1,0:T(8,128)S(1)} %get-tuple-element.56.refs_2_) | copy-start | bytes 3932164
  72.8 1.1 %copy-start.11 = (f32[4,5,4,32,128]{4,3,2,1,0:T(8,128)}, f32[4,5,4,32,128]{4,3,2,1,0:T(8,128)S(1)}, u32[]{:S(2)}) copy-start(f32[4,5,4,32,128]{4,3,2,1,0:T(8,128)S(1)} %get-tuple-element.57.refs_3_) | copy-start | bytes 3932164
  73.9 0.8 copy-start.12
  74.7 0.8 copy-start.13
  75.6 0.8 copy-start.14
  76.4 0.8 copy-start.15
  77.2 0.7 copy-start.17
  77.9 0.7 copy-start.18
  83.9 9.6 %collective-permute-start.6 = (f32[4,24,128]{2,1,0:T(8,128)S(1)}, f32[4,24,128]{2,1,0:T(8,128)S(1)}, u32[]{:S(2)}, u32[]{:S(2)}) collective-permute-start(f32[4,24,128]{2,1,0:T(8,128)S(1)} %get-tuple-element.102), channel_id=1, source_target_pairs={{16,0},{32,16},{48,32},{64,48},{80,64},{96,80},{112,96},{0,112},{1... | collective-permute-start | bytes 147464 | tf_op jit(solution)/shard_map/ppermute | solution.py:112
  86.8 7.7 %collective-permute-start.7 = (f32[4,24,128]{2,1,0:T(8,128)S(1)}, f32[4,24,128]{2,1,0:T(8,128)S(1)}, u32[]{:S(2)}, u32[]{:S(2)}) collective-permute-start(f32[4,24,128]{2,1,0:T(8,128)S(1)} %get-tuple-element.103), channel_id=1, source_target_pairs={{112,0},{0,16},{16,32},{32,48},{48,64},{64,80},{80,96},{96,112},{1... | collective-permute-start | bytes 147464 | tf_op jit(solution)/shard_map/ppermute | solution.py:112
  87.5 7.0 %copy-start.2 = (bf16[3,2,256,256]{3,2,1,0:T(8,128)(2,1)S(1)}, bf16[3,2,256,256]{3,2,1,0:T(8,128)(2,1)}, u32[]{:S(2)}) copy-start(bf16[3,2,256,256]{3,2,1,0:T(8,128)(2,1)} %constant.9.clone.refs_21_.back_ref) | copy-start | bytes 2359300
  87.5 7.0 %copy-start.3 = (bf16[3,2,256,256]{3,2,1,0:T(8,128)(2,1)S(1)}, bf16[3,2,256,256]{3,2,1,0:T(8,128)(2,1)}, u32[]{:S(2)}) copy-start(bf16[3,2,256,256]{3,2,1,0:T(8,128)(2,1)} %constant.8.clone.refs_20_.grad_ref) | copy-start | bytes 2359300

commit v3 on v2

--- a/solution.py
+++ b/solution.py
@@ -318,8 +318,8 @@
 
 
 def place_kernel(*refs):
-    (arr_ref, co_hbm), own, refs = refs[:2], refs[2:10], refs[10:]
-    (b_ref, strip_ref, north_ref, south_ref), fetched, refs = refs[:4], refs[4:18], refs[18:]
+    (arr_ref, co_hbm), own, refs = refs[:2], refs[2:11], refs[11:]
+    (b_ref, strip_ref, north_ref, south_ref), fetched, refs = refs[:4], refs[4:22], refs[22:]
     inj_ref, side_ref, vid_ref, ids_ref, co_ref, sem, own_sem = refs
     copy = pltpu.make_async_copy
     lane = lane_ids((N, N))
@@ -342,6 +342,7 @@
         moves.append((own[4].at[m], fetched[10].at[m, :, :, node]))
     for i in (5, 6, 7):
         moves.append((own[i], fetched[6 + i].at[:, :, node]))
+    moves.extend((own[8].at[ch], fetched[14 + ch]) for ch in range(4))
     moves = [copy(x, y, own_sem.at[i]) for i, (x, y) in enumerate(moves)]
     to_scalar.wait()
     for c in moves:
@@ -422,14 +423,15 @@
     whole = pl.BlockSpec(memory_space=pltpu.VMEM)
     return pl.pallas_call(
         place_kernel,
-        in_specs=[whole] + [pl.BlockSpec(memory_space=pltpu.HBM)] * 9,
-        out_specs=[whole] * 18,
+        in_specs=[whole] + [pl.BlockSpec(memory_space=pltpu.HBM)] * 10,
+        out_specs=[whole] * 22,
         out_shape=[
             jax.ShapeDtypeStruct((STEPS, 3, N, N), F32),
             jax.ShapeDtypeStruct((3, N, N), F32),
             jax.ShapeDtypeStruct((4, 24, N), F32),
             jax.ShapeDtypeStruct((4, 24, N), F32),
             *PREPARED,
+            *[jax.ShapeDtypeStruct((5, 4, 32, N), F32)] * 4,
         ],
         scratch_shapes=[
             pltpu.VMEM((STEPS * N * 16, N), F32),
@@ -438,7 +440,7 @@
             pltpu.SMEM((16, N), jnp.int32),
             pltpu.VMEM((6, N, N), F32),
             pltpu.SemaphoreType.DMA((2,)),
-            pltpu.SemaphoreType.DMA((17,)),
+            pltpu.SemaphoreType.DMA((21,)),
         ],
         compiler_params=pltpu.CompilerParams(vmem_limit_bytes=VMEM_LIMIT),
         name="place",
@@ -492,6 +494,28 @@
         depth(3)
 
 
+def row_forces(d, k, at, into, n, md_ref, ce_ref, grad_ref, back_ref):
+    rows = 5 * 4 * n
+    sh, sl = split2(d[3][:, :, at].reshape(rows, N))
+    strip = None
+    for c in range(3):
+        mh, ml = split2(d[c][:, :, at].reshape(rows, N))
+        hi = jnp.concatenate([mh, sh], axis=1)
+        lo = jnp.concatenate([ml, sl], axis=1)
+        g = dot(hi, grad_ref[c, 0]) + dot(lo, grad_ref[c, 0]) + dot(hi, grad_ref[c, 1])
+        fh, fl = split2(g * ce_ref[:, :, at].reshape(rows, 256))
+        f = dot(fh, back_ref[c, 0]) + dot(fl, back_ref[c, 0]) + dot(fh, back_ref[c, 1])
+        k[c][:, :, into] = f[:, :N].reshape(5, 4, n, N)
+        strip = f[:, N:] if strip is None else strip + f[:, N:]
+    k[3][:, :, into] = strip.reshape(5, 4, n, N)
+    for ch in range(4):
+        for j in range(4):
+            g = slopes([d[ch][z, j, at] for z in range(5)])
+            r = tested([g[z] * md_ref[ch // 3, z, j, at] for z in range(5)])
+            for z in range(5):
+                k[ch][z, j, into] = k[ch][z, j, into] + r[z]
+
+
 def expand(xe, xw, first, step):
     out = None
     for c in range(3):
@@ -526,8 +550,8 @@
 
 
 def early_kernel(
-    d_ref, v_ref, m_ref, r_ref, re_ref, rw_ref, sel_ref, qw_ref,
-    d_out, v_out, mn_out, md_out, di_out, ce_out, ai_out, as_out,
+    d_ref, v_ref, m_ref, r_ref, re_ref, rw_ref, sel_ref, qw_ref, grad_ref, back_ref,
+    d_out, v_out, mn_out, md_out, di_out, ce_out, ai_out, as_out, k_out,
 ):
     f = lambda a: float(np.float32(a))
     outs = {"mn": mn_out, "md": md_out, "di": di_out, "ai": ai_out, "as": as_out}
@@ -555,28 +579,38 @@
 
     for z in range(5):
         plane(z)
-
-
-OWN_SHAPES = ((4, 5, 4, 32, N),) * 2 + ((2, 5, 4, 32, N),) * 3 + ((5, 4, 32, 256),) + ((2, 4, 32, N),) * 2
-
-
-def early(d, v, m, r, re, rw, sel, qw):
+    node = slice(0, 32)
+    d, k = [d_out.at[ch] for ch in range(4)], [k_out.at[ch] for ch in range(4)]
+    row_forces(d, k, node, node, 32, md_out, ce_out, grad_ref, back_ref)
+
+
+OWN_SHAPES = (
+    *((4, 5, 4, 32, N),) * 2,
+    *((2, 5, 4, 32, N),) * 3,
+    (5, 4, 32, 256),
+    *((2, 4, 32, N),) * 2,
+    (4, 5, 4, 32, N),
+)
+
+
+def early(d, v, m, r, re, rw, tables):
+    grad, back, sel, qw = tables
     whole = pl.BlockSpec(memory_space=pltpu.VMEM)
     return pl.pallas_call(
         early_kernel,
-        in_specs=[whole] * 8,
-        out_specs=[whole] * 8,
+        in_specs=[whole] * 10,
+        out_specs=[whole] * 9,
         out_shape=[jax.ShapeDtypeStruct(x, F32) for x in OWN_SHAPES],
         compiler_params=pltpu.CompilerParams(vmem_limit_bytes=16 * 1024 * 1024),
         name="early",
-    )(d, v, m, r, re, rw, sel, qw)
+    )(d, v, m, r, re, rw, sel, qw, grad, back)
 
 
 def prepare_kernel(*refs):
-    halos, tables, refs = refs[14:18], refs[18:22], refs[22:]
+    own_k, halos, tables, refs = refs[14:18], refs[18:22], refs[22:26], refs[26:]
     (d0, d1, d2, d3, v0, v1, v2, v3), refs = refs[:8], refs[8:]
     (mn_ref, md_ref, di_ref, ce_ref, ai_ref, as_ref), refs = refs[:6], refs[6:]
-    (k0, k1, k2, k3, n0, n1, n2, n3), refs = refs[:8], refs[8:]
+    halo_k, refs = refs[:4], refs[4:]
     buffers, (halo_sem,) = refs[:8], refs[8:]
     d_ref, v_ref = (d0, d1, d2, d3), (v0, v1, v2, v3)
     copy = pltpu.make_async_copy
@@ -623,16 +657,20 @@
         for z in range(5):
             mn_ref[m, z, 4] = pltpu.roll(mn_ref[m, z, 0], E - 1, 0)
 
-    def emit(ch, j, z, d, k):
+    row_forces(d_ref, halo_k, rest, slice(0, 8), 8, md_ref, ce_ref, grad_ref, back_ref)
+    for ch in range(4):
         m = ch // 3
-        v = v_ref[ch][z, j]
-        if z == 0:
-            k = k + ai_ref[m, j] * v + as_ref[m, j] * d
-        v_ref[ch][z, j] = v - di_ref[m, z, j] * k
-
-    line_forces(
-        d_ref, (k0, k1, k2, k3), (n0, n1, n2, n3), mn_ref, md_ref, ce_ref, grad_ref, back_ref, 4, emit
-    )
+        for z in range(5):
+            d = [d_ref[ch][z, j] for j in range(4)]
+            g = slopes(d + [pltpu.roll(d[0], E - 1, 0)])
+            r = tested([g[i] * mn_ref[m, z, i] for i in range(5)])
+            r[0] = r[0] + pltpu.roll(r[4], 1, 0)
+            for j in range(4):
+                v = v_ref[ch][z, j]
+                k = jnp.concatenate([own_k[ch][z, j], halo_k[ch][z, j]], axis=0) + r[j]
+                if z == 0:
+                    k = k + ai_ref[m, j] * v + as_ref[m, j] * d[j]
+                v_ref[ch][z, j] = v - di_ref[m, z, j] * k
 
 
 def prepare(fetched, halos, tables):
@@ -641,11 +679,11 @@
     late = (*halos, sel, qw, grad, back)
     return pl.pallas_call(
         prepare_kernel,
-        in_specs=[whole] * 14 + [pl.BlockSpec(memory_space=pltpu.HBM)] * 8,
+        in_specs=[whole] * 18 + [pl.BlockSpec(memory_space=pltpu.HBM)] * 8,
         out_specs=[whole] * 14,
         out_shape=PREPARED,
         input_output_aliases={i: i for i in range(14)},
-        scratch_shapes=[pltpu.VMEM((5, 4, E, N), F32)] * 8
+        scratch_shapes=[pltpu.VMEM((5, 4, 8, N), F32)] * 4
         + [pltpu.VMEM(x.shape, x.dtype) for x in late]
         + [pltpu.SemaphoreType.DMA((8,))],
         compiler_params=pltpu.CompilerParams(vmem_limit_bytes=VMEM_LIMIT),
@@ -745,7 +783,7 @@
     corner_north = shifted(late_south, "src", -1)
     corner_south = shifted(late_north, "src", 1)
     co = coefs(modulus, density, from_east, from_west)
-    own = early(displacement, velocity, modulus, density, from_east, from_west, *tables[2:])
+    own = early(displacement, velocity, modulus, density, from_east, from_west, tables)
     b, b_strip, b_north, b_south, *fetched = place(arrived, co, own)
     b_from_south = shifted(b_north, "src", 1)
     b_from_north = shifted(b_south, "src", -1)

time: 107 us -> 113 us (1.056)
  local copies, waits for them, and re-layouts: 11.2 us -> 15.4 us
  waiting for transfers between devices: 31.1 us -> 33.1 us
    unnamed x42 -> x46, local copies, waits for them, and re-layouts: 11.2 us -> 15.4 us
    ppermute x8, waiting for transfers between devices: 31.1 us -> 33.1 us  [shifted(): lax.ppermute(block, axis, [((i - distance) % n, i) for i in range(n)])]
  transfers between devices with their start and end apart: 9 -> 9, of which waited for: 3 -> 3; matrix products, arithmetic and copies ran while one was open for 2% -> 2% of each run, Pallas kernels for 14% -> 13%
where the time goes in v3:
time: 113 us; the launch traced here: 112 us
  waiting for transfers between devices  33.1 us (29%)
  Pallas kernels  32.5 us (29%)
  starting transfers between devices  29 us (26%)
  local copies, waits for them, and re-layouts  15.4 us (14%)
  other arithmetic  1.81 us (2%)
    ppermute x8, waiting for transfers between devices, shifted(): lax.ppermute(block, axis, [((i - distance) % n, i) for i in range(n)])  33.1 us
    ppermute x8, starting transfers between devices, shifted(): lax.ppermute(block, axis, [((i - distance) % n, i) for i in range(n)])  17.8 us
    unnamed x46, local copies, waits for them, and re-layouts  15.4 us
    pallas_call x1, Pallas kernels, steps(): pl.pallas_call(steps_kernel, in_specs=[whole] * 20, out_specs=[whole] * 2...  11.9 us
    all_to_all x1, starting transfers between devices, local(): lax.all_to_all(sent.reshape(N, 40, N), ('src', 'reg'), split_axis=0, conc...  11.2 us
    pallas_call x1, Pallas kernels, begin(): pl.pallas_call(begin_kernel, in_specs=[hbm] * 6, out_specs=[hbm] * 7, out...  5.39 us
    pallas_call x1, Pallas kernels, place(): pl.pallas_call(place_kernel, in_specs=[whole] + [pl.BlockSpec(memory_spac...  5.38 us
    pallas_call x1, Pallas kernels, prepare(): pl.pallas_call(prepare_kernel, in_specs=[whole] * 18 + [pl.BlockSpec(memo...  3.96 us
  transfers between devices with their start and end apart: 9, of which 3 were waited for; matrix products, arithmetic and copies ran while one was open for 2% of the time, Pallas kernels for 13%

profile of v3, /device:TPU:0, one launch (start us, length us, event | category | flops | bytes accessed | tf_op | source)
XLA Modules:
  0.0 112.5 jit_solution(3223424708878327708)
XLA Ops:
  0.6 5.4 %begin.1 = (f32[5,128,128]{2,1,0:T(8,128)}, f32[5,128,128]{2,1,0:T(8,128)}, f32[6,5,16,128]{3,2,1,0:T(8,128)}, f32[6,5,16,128]{3,2,1,0:T(8,128)}, f32[2,5,16,128...) custom-call(f32[3,5,128,128]{3,2,1,0:T(8,128)} %d_ref.3, f32[3,5,128,128]{3,2,1,0:T(8,128)} %v_ref.3, ...), custom_call_target="tpu_custom_call" | custom-call | tf_op jit(solution)/shard_map/begin/pallas_call | solution.py:249
  6.0 11.2 %all-to-all-start = ((f32[128,40,128]{2,1,0:T(8,128)}), f32[128,40,128]{2,1,0:T(8,128)S(1)}, u32[]{:S(2)}, u32[]{:S(2)}) async-start(f32[128,40,128]{2,1,0:T(8,128)} %bitcast.8), calls=%async_computation | async-start | bytes 5242880 | tf_op jit(solution)/shard_map/all_to_all | solution.py:777
  17.3 3.5 %collective-permute-start = (f32[5,128,128]{2,1,0:T(8,128)}, f32[5,128,128]{2,1,0:T(8,128)S(1)}, u32[]{:S(2)}, u32[]{:S(2)}) collective-permute-start(f32[5,128,128]{2,1,0:T(8,128)} %get-tuple-element.59), channel_id=1, source_target_pairs={{1,0},{2,1},{3,2},{4,3},{5,4},{6,5},{7,6},{8,7},{9,8},{10,9},{11,1... | collective-permute-start | bytes 983048 | tf_op jit(solution)/shard_map/ppermute | solution.py:112
  20.8 5.0 %collective-permute-start.2 = (f32[6,5,16,128]{3,2,1,0:T(8,128)}, f32[6,5,16,128]{3,2,1,0:T(8,128)}, u32[]{:S(2)}, u32[]{:S(2)}) collective-permute-start(f32[6,5,16,128]{3,2,1,0:T(8,128)} %get-tuple-element.88), channel_id=1, source_target_pairs={{16,0},{32,16},{48,32},{64,48},{80,64},{96,80},{112,96},{0,112},{1... | collective-permute-start | bytes 737288 | tf_op jit(solution)/shard_map/ppermute | solution.py:112
  25.8 26.9 %collective-permute-done.re_ref = f32[5,128,128]{2,1,0:T(8,128)S(1)} collective-permute-done((f32[5,128,128]{2,1,0:T(8,128)}, f32[5,128,128]{2,1,0:T(8,128)S(1)}, u32[]{:S(2)}, u32[]{:S(2)}) %collective-permute-start) | collective-permute-done | bytes 327712 | tf_op jit(solution)/shard_map/ppermute | solution.py:112
  52.7 3.2 %collective-permute-done.1.rw_ref = f32[5,128,128]{2,1,0:T(8,128)S(1)} collective-permute-done((f32[5,128,128]{2,1,0:T(8,128)}, f32[5,128,128]{2,1,0:T(8,128)S(1)}, u32[]{:S(2)}, u32[]{:S(2)}) %collective-permute-start.1) | collective-permute-done | bytes 327712 | tf_op jit(solution)/shard_map/ppermute | solution.py:112
  55.9 1.8 %fusion = (f32[4,5,16,128]{3,2,1,0:T(8,128)}, f32[4,5,16,128]{3,2,1,0:T(8,128)}) fusion(f32[1,5,128,128]{3,2,1,0:T(8,128)S(1)} %bitcast.7, f32[1,5,128,128]{3,2,1,0:T(8,128)S(1)} %bitcast.6, f32[2,5,16,128]{3,2,1,0:T(8,128)} %get-tuple-element.91, f32[2,5,16,128]{3,2,1,0:T(8,128)} %get-tuple-element.90), kind=kLoop, calls=%fused_computation.1 | loop fusion | flops 163840 | bytes 1146880 | tf_op jit(solution)/shard_map/concatenate | solution.py:782
  57.7 2.7 %collective-permute-start.5 = (f32[4,5,16,128]{3,2,1,0:T(8,128)}, f32[4,5,16,128]{3,2,1,0:T(8,128)}, u32[]{:S(2)}, u32[]{:S(2)}) collective-permute-start(f32[4,5,16,128]{3,2,1,0:T(8,128)} %get-tuple-element.114), channel_id=1, source_target_pairs={{112,0},{0,16},{16,32},{32,48},{48,64},{64,80},{80,96},{96,112},{1... | collective-permute-start | bytes 491528 | tf_op jit(solution)/shard_map/ppermute | solution.py:112
  60.4 3.0 %collective-permute-start.4 = (f32[4,5,16,128]{3,2,1,0:T(8,128)}, f32[4,5,16,128]{3,2,1,0:T(8,128)}, u32[]{:S(2)}, u32[]{:S(2)}) collective-permute-start(f32[4,5,16,128]{3,2,1,0:T(8,128)} %get-tuple-element.115), channel_id=1, source_target_pairs={{16,0},{32,16},{48,32},{64,48},{80,64},{96,80},{112,96},{0,112},{1... | collective-permute-start | bytes 491528 | tf_op jit(solution)/shard_map/ppermute | solution.py:112
  63.4 2.4 %coefs.1.refs_1_ = f32[6,128,128]{2,1,0:T(8,128)} custom-call(f32[5,128,128]{2,1,0:T(8,128)} %m_ref.5, f32[5,128,128]{2,1,0:T(8,128)} %r_ref.5, f32[5,128,128]{2,1,0:T(8,128)} %copy-done.8, f32[5,128,128]{2,1,0:T(8,128)} %copy-done.10), custom_call_target="tpu_custom_call" | custom-call | tf_op jit(solution)/shard_map/coefs/pallas_call | solution.py:310
  65.8 1.1 copy-done.2
  66.9 1.2 %copy-done.4 = f32[3,5,128,128]{3,2,1,0:T(8,128)S(1)} copy-done((f32[3,5,128,128]{3,2,1,0:T(8,128)S(1)}, f32[3,5,128,128]{3,2,1,0:T(8,128)}, u32[]{:S(2)}) %copy-start.4) | copy-done | bytes 983064
  68.1 1.2 %copy-done.5 = f32[3,5,128,128]{3,2,1,0:T(8,128)S(1)} copy-done((f32[3,5,128,128]{3,2,1,0:T(8,128)S(1)}, f32[3,5,128,128]{3,2,1,0:T(8,128)}, u32[]{:S(2)}) %copy-start.5) | copy-done | bytes 983064
  69.3 1.0 copy-done.6
  70.3 1.0 copy-done.7
  71.3 1.0 copy-done.9
  72.3 1.0 copy-done.11
  73.2 3.4 %early.1 = (f32[4,5,4,32,128]{4,3,2,1,0:T(8,128)S(1)}, f32[4,5,4,32,128]{4,3,2,1,0:T(8,128)S(1)}, f32[2,5,4,32,128]{4,3,2,1,0:T(8,128)S(1)}, f32[2,5,4,32,128]{4...) custom-call(f32[3,5,128,128]{3,2,1,0:T(8,128)S(1)} %copy-done.4, ...), custom_call_target="tpu_custom_call" | custom-call | tf_op jit(solution)/shard_map/early/pallas_call | solution.py:599
  76.6 1.1 copy-done.12
  77.7 1.1 copy-done.13
  78.8 1.1 copy-done.14
  79.9 0.8 copy-done.15
  80.7 0.8 copy-done.16
  81.5 0.8 copy-done.17
  82.4 0.9 copy-done.18
  83.9 0.7 copy-done.21
  84.6 5.4 %place.1 = (f32[4,3,128,128]{3,2,1,0:T(8,128)S(1)}, f32[3,128,128]{2,1,0:T(8,128)S(1)}, f32[4,24,128]{2,1,0:T(8,128)S(1)}, f32[4,24,128]{2,1,0:T(8,128)S(1)}, f3...) custom-call(f32[128,40,128]{2,1,0:T(8,128)S(1)} %all-to-all-done.ref, ...), custom_call_target="tpu_custom_call" | custom-call | tf_op jit(solution)/shard_map/place/pallas_call | solution.py:424
  90.0 2.9 %collective-permute-start.6 = (f32[4,24,128]{2,1,0:T(8,128)S(1)}, f32[4,24,128]{2,1,0:T(8,128)S(1)}, u32[]{:S(2)}, u32[]{:S(2)}) collective-permute-start(f32[4,24,128]{2,1,0:T(8,128)S(1)} %get-tuple-element.112), channel_id=1, source_target_pairs={{16,0},{32,16},{48,32},{64,48},{80,64},{96,80},{112,96},{0,112},{1... | collective-permute-start | bytes 147464 | tf_op jit(solution)/shard_map/ppermute | solution.py:112
  92.9 0.7 collective-permute-start.7
  93.6 4.0 %prepare.1 = (f32[5,4,40,128]{3,2,1,0:T(8,128)S(1)}, f32[5,4,40,128]{3,2,1,0:T(8,128)S(1)}, f32[5,4,40,128]{3,2,1,0:T(8,128)S(1)}, f32[5,4,40,128]{3,2,1,0:T(8,1...) custom-call(f32[5,4,40,128]{3,2,1,0:T(8,128)S(1)} %get-tuple-element, ...), custom_call_target="tpu_custom_call", output_to_operand_aliasing={{0}: (0, {}), {1}: (1, {}), {2}: (2, {}), {3}: (3, {}), {4}... | custom-call | tf_op jit(solution)/shard_map/prepare/pallas_call | solution.py:680
  97.6 3.0 %collective-permute-done.7.bo_ref = f32[4,24,128]{2,1,0:T(8,128)S(1)} collective-permute-done((f32[4,24,128]{2,1,0:T(8,128)S(1)}, f32[4,24,128]{2,1,0:T(8,128)S(1)}, u32[]{:S(2)}, u32[]{:S(2)}) %collective-permute-start.7) | collective-permute-done | bytes 49184 | tf_op jit(solution)/shard_map/ppermute | solution.py:112
  100.6 11.9 %steps.1 = (f32[3,5,128,128]{3,2,1,0:T(8,128)}, f32[3,5,128,128]{3,2,1,0:T(8,128)}) custom-call(f32[5,4,40,128]{3,2,1,0:T(8,128)S(1)} %get-tuple-element.97.i0, f32[5,4,40,128]{3,2,1,0:T(8,128)S(1)} %get-tuple-element.98.i1, f32[5,4,40,128]{3,2,1,0:T(8,128)S(1)} %get-tuple-element.99.i2, f32[5,4,40,128]{3,2,1,0:T(8,128)S(1)} %get-tuple-element.100.i3, ...), custom_call_target="tpu_custom_call" | custom-call | tf_op jit(solution)/shard_map/steps/pallas_call | solution.py:757
  (39 shorter events, 0.7 us)
Async XLA Ops:
  6.0 78.5 %all-to-all-start = ((f32[128,40,128]{2,1,0:T(8,128)}), f32[128,40,128]{2,1,0:T(8,128)S(1)}, u32[]{:S(2)}, u32[]{:S(2)}) async-start(f32[128,40,128]{2,1,0:T(8,128)} %bitcast.8), calls=%async_computation | async-start | bytes 5242880 | tf_op jit(solution)/shard_map/all_to_all | solution.py:777
  17.2 48.6 %copy-start = (bf16[3,2,256,256]{3,2,1,0:T(8,128)(2,1)S(1)}, bf16[3,2,256,256]{3,2,1,0:T(8,128)(2,1)}, u32[]{:S(2)}) copy-start(bf16[3,2,256,256]{3,2,1,0:T(8,128)(2,1)} %constant.9.clone.back_ref.refs_25_) | copy-start | bytes 2359300
  17.2 48.6 %copy-start.19 = (bf16[256,256]{1,0:T(8,128)(2,1)S(1)}, bf16[256,256]{1,0:T(8,128)(2,1)}, u32[]{:S(2)}) copy-start(bf16[256,256]{1,0:T(8,128)(2,1)} %constant.10.clone.sel_ref.refs_22_) | copy-start | bytes 393220
  17.2 48.6 %copy-start.22 = (f32[1,256]{1,0:T(1,128)S(1)}, f32[1,256]{1,0:T(1,128)}, u32[]{:S(2)}) copy-start(f32[1,256]{1,0:T(1,128)} %constant.11.clone.qw_ref.refs_23_) | copy-start | bytes 3076
  17.3 35.5 %collective-permute-start = (f32[5,128,128]{2,1,0:T(8,128)}, f32[5,128,128]{2,1,0:T(8,128)S(1)}, u32[]{:S(2)}, u32[]{:S(2)}) collective-permute-start(f32[5,128,128]{2,1,0:T(8,128)} %get-tuple-element.59), channel_id=1, source_target_pairs={{1,0},{2,1},{3,2},{4,3},{5,4},{6,5},{7,6},{8,7},{9,8},{10,9},{11,1... | collective-permute-start | bytes 983048 | tf_op jit(solution)/shard_map/ppermute | solution.py:112
  20.8 35.1 %collective-permute-start.1 = (f32[5,128,128]{2,1,0:T(8,128)}, f32[5,128,128]{2,1,0:T(8,128)S(1)}, u32[]{:S(2)}, u32[]{:S(2)}) collective-permute-start(f32[5,128,128]{2,1,0:T(8,128)} %get-tuple-element.60), channel_id=1, source_target_pairs={{15,0},{0,1},{1,2},{2,3},{3,4},{4,5},{5,6},{6,7},{7,8},{8,9},{9,10... | collective-permute-start | bytes 983048 | tf_op jit(solution)/shard_map/ppermute | solution.py:112
  20.8 72.1 %collective-permute-start.2 = (f32[6,5,16,128]{3,2,1,0:T(8,128)}, f32[6,5,16,128]{3,2,1,0:T(8,128)}, u32[]{:S(2)}, u32[]{:S(2)}) collective-permute-start(f32[6,5,16,128]{3,2,1,0:T(8,128)} %get-tuple-element.88), channel_id=1, source_target_pairs={{16,0},{32,16},{48,32},{64,48},{80,64},{96,80},{112,96},{0,112},{1... | collective-permute-start | bytes 737288 | tf_op jit(solution)/shard_map/ppermute | solution.py:112
  25.8 67.7 %collective-permute-start.3 = (f32[6,5,16,128]{3,2,1,0:T(8,128)}, f32[6,5,16,128]{3,2,1,0:T(8,128)}, u32[]{:S(2)}, u32[]{:S(2)}) collective-permute-start(f32[6,5,16,128]{3,2,1,0:T(8,128)} %get-tuple-element.89), channel_id=1, source_target_pairs={{112,0},{0,16},{16,32},{32,48},{48,64},{64,80},{80,96},{96,112},{1... | collective-permute-start | bytes 737288 | tf_op jit(solution)/shard_map/ppermute | solution.py:112
  52.7 3.2 %copy-start.8 = (f32[5,128,128]{2,1,0:T(8,128)}, f32[5,128,128]{2,1,0:T(8,128)S(1)}, u32[]{:S(2)}) copy-start(f32[5,128,128]{2,1,0:T(8,128)S(1)} %collective-permute-done.re_ref) | copy-start | bytes 983044
  55.9 1.8 %copy-start.10 = (f32[5,128,128]{2,1,0:T(8,128)}, f32[5,128,128]{2,1,0:T(8,128)S(1)}, u32[]{:S(2)}) copy-start(f32[5,128,128]{2,1,0:T(8,128)S(1)} %collective-permute-done.1.rw_ref) | copy-start | bytes 983044
  57.7 35.9 %collective-permute-start.5 = (f32[4,5,16,128]{3,2,1,0:T(8,128)}, f32[4,5,16,128]{3,2,1,0:T(8,128)}, u32[]{:S(2)}, u32[]{:S(2)}) collective-permute-start(f32[4,5,16,128]{3,2,1,0:T(8,128)} %get-tuple-element.114), channel_id=1, source_target_pairs={{112,0},{0,16},{16,32},{32,48},{48,64},{64,80},{80,96},{96,112},{1... | collective-permute-start | bytes 491528 | tf_op jit(solution)/shard_map/ppermute | solution.py:112
  60.4 33.2 %collective-permute-start.4 = (f32[4,5,16,128]{3,2,1,0:T(8,128)}, f32[4,5,16,128]{3,2,1,0:T(8,128)}, u32[]{:S(2)}, u32[]{:S(2)}) collective-permute-start(f32[4,5,16,128]{3,2,1,0:T(8,128)} %get-tuple-element.115), channel_id=1, source_target_pairs={{16,0},{32,16},{48,32},{64,48},{80,64},{96,80},{112,96},{0,112},{1... | collective-permute-start | bytes 491528 | tf_op jit(solution)/shard_map/ppermute | solution.py:112
  65.8 1.1 %copy-start.2 = (bf16[3,2,256,256]{3,2,1,0:T(8,128)(2,1)S(1)}, bf16[3,2,256,256]{3,2,1,0:T(8,128)(2,1)}, u32[]{:S(2)}) copy-start(bf16[3,2,256,256]{3,2,1,0:T(8,128)(2,1)} %constant.8.clone.grad_ref.refs_24_) | copy-start | bytes 2359300
  66.9 1.2 %copy-start.4 = (f32[3,5,128,128]{3,2,1,0:T(8,128)S(1)}, f32[3,5,128,128]{3,2,1,0:T(8,128)}, u32[]{:S(2)}) copy-start(f32[3,5,128,128]{3,2,1,0:T(8,128)} %d_ref.3) | copy-start | bytes 2949124
  68.1 1.2 %copy-start.5 = (f32[3,5,128,128]{3,2,1,0:T(8,128)S(1)}, f32[3,5,128,128]{3,2,1,0:T(8,128)}, u32[]{:S(2)}) copy-start(f32[3,5,128,128]{3,2,1,0:T(8,128)} %v_ref.3) | copy-start | bytes 2949124
  69.3 1.0 copy-start.6
  70.3 1.0 copy-start.7
  71.3 1.0 copy-start.9
  72.3 1.0 copy-start.11
  76.6 1.1 copy-start.12
  77.7 1.1 copy-start.13
  78.8 1.1 copy-start.14
  79.9 0.8 copy-start.15
  80.7 0.8 copy-start.16
  81.5 0.8 copy-start.17
  82.4 0.9 copy-start.18
  83.3 0.7 copy-start.20
  83.9 0.7 copy-start.21
  90.0 7.6 %collective-permute-start.6 = (f32[4,24,128]{2,1,0:T(8,128)S(1)}, f32[4,24,128]{2,1,0:T(8,128)S(1)}, u32[]{:S(2)}, u32[]{:S(2)}) collective-permute-start(f32[4,24,128]{2,1,0:T(8,128)S(1)} %get-tuple-element.112), channel_id=1, source_target_pairs={{16,0},{32,16},{48,32},{64,48},{80,64},{96,80},{112,96},{0,112},{1... | collective-permute-start | bytes 147464 | tf_op jit(solution)/shard_map/ppermute | solution.py:112
  92.9 7.7 %collective-permute-start.7 = (f32[4,24,128]{2,1,0:T(8,128)S(1)}, f32[4,24,128]{2,1,0:T(8,128)S(1)}, u32[]{:S(2)}, u32[]{:S(2)}) collective-permute-start(f32[4,24,128]{2,1,0:T(8,128)S(1)} %get-tuple-element.113), channel_id=1, source_target_pairs={{112,0},{0,16},{16,32},{32,48},{48,64},{64,80},{80,96},{96,112},{1... | collective-permute-start | bytes 147464 | tf_op jit(solution)/shard_map/ppermute | solution.py:112
  93.6 7.0 %copy-start.1 = (bf16[3,2,256,256]{3,2,1,0:T(8,128)(2,1)S(1)}, bf16[3,2,256,256]{3,2,1,0:T(8,128)(2,1)}, u32[]{:S(2)}) copy-start(bf16[3,2,256,256]{3,2,1,0:T(8,128)(2,1)} %constant.9.clone.back_ref.refs_25_) | copy-start | bytes 2359300
  93.6 7.0 %copy-start.3 = (bf16[3,2,256,256]{3,2,1,0:T(8,128)(2,1)S(1)}, bf16[3,2,256,256]{3,2,1,0:T(8,128)(2,1)}, u32[]{:S(2)}) copy-start(bf16[3,2,256,256]{3,2,1,0:T(8,128)(2,1)} %constant.8.clone.grad_ref.refs_24_) | copy-start | bytes 2359300

commit v4 on v3

--- a/solution.py
+++ b/solution.py
@@ -516,6 +516,17 @@
                 k[ch][z, j, into] = k[ch][z, j, into] + r[z]
 
 
+def north_update(ch, d_ref, mn_ref, own_k, halo_k, emit):
+    for z in range(5):
+        d = [d_ref[ch][z, j] for j in range(4)]
+        g = slopes(d + [pltpu.roll(d[0], E - 1, 0)])
+        r = tested([g[i] * mn_ref[ch // 3, z, i] for i in range(5)])
+        r[0] = r[0] + pltpu.roll(r[4], 1, 0)
+        for j in range(4):
+            k = jnp.concatenate([own_k[ch][z, j], halo_k[ch][z, j]], axis=0) + r[j]
+            emit(ch, j, z, d[j], k)
+
+
 def expand(xe, xw, first, step):
     out = None
     for c in range(3):
@@ -607,9 +618,11 @@
 
 
 def prepare_kernel(*refs):
-    own_k, halos, tables, refs = refs[14:18], refs[18:22], refs[22:26], refs[26:]
+    own_k, (b_ref, strip_ref), halos, tables, refs = (
+        refs[14:18], refs[18:20], refs[20:24], refs[24:28], refs[28:]
+    )
     (d0, d1, d2, d3, v0, v1, v2, v3), refs = refs[:8], refs[8:]
-    (mn_ref, md_ref, di_ref, ce_ref, ai_ref, as_ref), refs = refs[:6], refs[6:]
+    (mn_ref, md_ref, di_ref, ce_ref, ai_ref, as_ref), next_k, refs = refs[:6], refs[6:10], refs[10:]
     halo_k, refs = refs[:4], refs[4:]
     buffers, (halo_sem,) = refs[:8], refs[8:]
     d_ref, v_ref = (d0, d1, d2, d3), (v0, v1, v2, v3)
@@ -658,44 +671,53 @@
             mn_ref[m, z, 4] = pltpu.roll(mn_ref[m, z, 0], E - 1, 0)
 
     row_forces(d_ref, halo_k, rest, slice(0, 8), 8, md_ref, ce_ref, grad_ref, back_ref)
+
+    def emit(ch, j, z, d, k):
+        m = ch // 3
+        v = v_ref[ch][z, j]
+        if z == 0:
+            k = k + ai_ref[m, j] * v + as_ref[m, j] * d
+        v_ref[ch][z, j] = v - di_ref[m, z, j] * k
+
     for ch in range(4):
-        m = ch // 3
-        for z in range(5):
-            d = [d_ref[ch][z, j] for j in range(4)]
-            g = slopes(d + [pltpu.roll(d[0], E - 1, 0)])
-            r = tested([g[i] * mn_ref[m, z, i] for i in range(5)])
-            r[0] = r[0] + pltpu.roll(r[4], 1, 0)
-            for j in range(4):
-                v = v_ref[ch][z, j]
-                k = jnp.concatenate([own_k[ch][z, j], halo_k[ch][z, j]], axis=0) + r[j]
+        north_update(ch, d_ref, mn_ref, own_k, halo_k, emit)
+    node = slice(0, 32)
+    for ch in range(4):
+        for j in range(4):
+            own = pl.ds(j, 32, stride=4)
+            x = b_ref[0, ch, own, :] if ch < 3 else strip_ref[0, own, :]
+            for z in range(5):
+                v = v_ref[ch][z, j, node]
                 if z == 0:
-                    k = k + ai_ref[m, j] * v + as_ref[m, j] * d[j]
-                v_ref[ch][z, j] = v - di_ref[m, z, j] * k
-
-
-def prepare(fetched, halos, tables):
+                    v = v + di_ref[ch // 3, z, j, node] * x
+                    v_ref[ch][z, j, node] = v
+                d_ref[ch][z, j, node] = d_ref[ch][z, j, node] + DT * v
+    row_forces(d_ref, next_k, node, node, 32, md_ref, ce_ref, grad_ref, back_ref)
+
+
+def prepare(fetched, b, strip, halos, tables):
     grad, back, sel, qw = tables
     whole = pl.BlockSpec(memory_space=pltpu.VMEM)
     late = (*halos, sel, qw, grad, back)
     return pl.pallas_call(
         prepare_kernel,
-        in_specs=[whole] * 18 + [pl.BlockSpec(memory_space=pltpu.HBM)] * 8,
-        out_specs=[whole] * 14,
-        out_shape=PREPARED,
+        in_specs=[whole] * 20 + [pl.BlockSpec(memory_space=pltpu.HBM)] * 8,
+        out_specs=[whole] * 18,
+        out_shape=(*PREPARED, *[jax.ShapeDtypeStruct((5, 4, 32, N), F32)] * 4),
         input_output_aliases={i: i for i in range(14)},
         scratch_shapes=[pltpu.VMEM((5, 4, 8, N), F32)] * 4
         + [pltpu.VMEM(x.shape, x.dtype) for x in late]
         + [pltpu.SemaphoreType.DMA((8,))],
         compiler_params=pltpu.CompilerParams(vmem_limit_bytes=VMEM_LIMIT),
         name="prepare",
-    )(*fetched, *in_hbm(*late))
+    )(*fetched, b, strip, *in_hbm(*late))
 
 
 def steps_kernel(
     i0, i1, i2, i3, u0, u1, u2, u3, mn_ref, md_ref, di_ref, ce_ref, ai_ref, as_ref,
-    b_ref, bs_ref, bn_ref, bo_ref, grad_ref, back_ref,
+    o0, o1, o2, o3, b_ref, bs_ref, bn_ref, bo_ref, grad_ref, back_ref,
     dout_ref, vout_ref,
-    d0, d1, d2, d3, v0, v1, v2, v3, k0, k1, k2, k3, n0, n1, n2, n3, f_ref,
+    d0, d1, d2, d3, v0, v1, v2, v3, k0, k1, k2, k3, n0, n1, n2, n3, f_ref, *halo_k,
 ):
     d_in, v_in = (i0, i1, i2, i3), (u0, u1, u2, u3)
     d_ref, v_ref = (d0, d1, d2, d3), (v0, v1, v2, v3)
@@ -716,14 +738,17 @@
             x = b_ref[3, ch, pl.ds(j, 32, stride=4), :]
             f_ref[3, ch, j] = jnp.concatenate([x, jnp.zeros((8, N), F32)], axis=0)
 
+    node, rest = slice(0, 32), slice(32, E)
     for ch in range(4):
         for j in range(4):
             for z in range(5):
-                v = v_in[ch][z, j]
+                v_ref[ch][z, j, node] = v_in[ch][z, j, node]
+                d_ref[ch][z, j, node] = d_in[ch][z, j, node]
+                v = v_in[ch][z, j, rest]
                 if z == 0:
-                    v = v + di_ref[ch // 3, z, j] * f_ref[0, ch, j]
-                v_ref[ch][z, j] = v
-                d_ref[ch][z, j] = d_in[ch][z, j] + DT * v
+                    v = v + di_ref[ch // 3, z, j, rest] * f_ref[0, ch, j, rest]
+                v_ref[ch][z, j, rest] = v
+                d_ref[ch][z, j, rest] = d_in[ch][z, j, rest] + DT * v
 
     def velocity(t, ch, j, z, d, k):
         m = ch // 3
@@ -733,16 +758,18 @@
             k = k + ai_ref[m, j, n] * v + as_ref[m, j, n] * d - f_ref[t, ch, j, n]
         return v - di_ref[m, z, j, n] * k
 
-    def step(t, carry):
-        def emit(ch, j, z, d, k):
+    def emit(t):
+        def put(ch, j, z, d, k):
             v = velocity(t, ch, j, z, d, k)
             v_ref[ch][z, j] = v
             d_ref[ch][z, j] = d + DT * v
 
-        line_forces(d_ref, k_ref, kn_ref, mn_ref, md_ref, ce_ref, grad_ref, back_ref, 4, emit)
-        return carry
-
-    lax.fori_loop(1, 3, step, 0)
+        return put
+
+    row_forces(d_ref, halo_k, rest, slice(0, 8), 8, md_ref, ce_ref, grad_ref, back_ref)
+    for ch in range(4):
+        north_update(ch, d_ref, mn_ref, (o0, o1, o2, o3), halo_k, emit(1))
+    line_forces(d_ref, k_ref, kn_ref, mn_ref, md_ref, ce_ref, grad_ref, back_ref, 4, emit(2))
 
     def final(ch, j, z, d, k):
         dout_ref[ch, z, pl.ds(j, 32, stride=4), :] = d
@@ -756,10 +783,12 @@
     whole = pl.BlockSpec(memory_space=pltpu.VMEM)
     return pl.pallas_call(
         steps_kernel,
-        in_specs=[whole] * 20,
+        in_specs=[whole] * 24,
         out_specs=[whole] * 2,
         out_shape=[jax.ShapeDtypeStruct((3, 5, N, N), F32)] * 2,
-        scratch_shapes=[pltpu.VMEM((5, 4, E, N), F32)] * 16 + [pltpu.VMEM((4, 4, 4, E, N), F32)],
+        scratch_shapes=[pltpu.VMEM((5, 4, E, N), F32)] * 16
+        + [pltpu.VMEM((4, 4, 4, E, N), F32)]
+        + [pltpu.VMEM((5, 4, 8, N), F32)] * 4,
         compiler_params=pltpu.CompilerParams(vmem_limit_bytes=VMEM_LIMIT),
         name="steps",
     )(*prepared, b, bs, bn, bo, grad, back)
@@ -790,7 +819,7 @@
     from_north, from_south, corner_north, corner_south, _ = lax.optimization_barrier(
         (from_north, from_south, corner_north, corner_south, b)
     )
-    prepared = prepare(fetched, (from_north, from_south, corner_north, corner_south), tables)
+    prepared = prepare(fetched, b, b_strip, (from_north, from_south, corner_north, corner_south), tables)
     return steps(prepared, b, b_strip, b_from_north, b_from_south, tables)
 
 

time: 113 us -> 110 us (0.973)
  waiting for transfers between devices: 33.1 us -> 31.1 us
  Pallas kernels: 32.5 us -> 31 us
    ppermute x8, waiting for transfers between devices: 33.1 us -> 31.1 us  [shifted(): lax.ppermute(block, axis, [((i - distance) % n, i) for i in range(n)])]
    pallas_call x2, Pallas kernels: 15.9 us -> 14.4 us  [the longest x1 8.43 us: steps(): pl.pallas_call(steps_kernel, in_specs=[whole] * 24, out_specs=[whole] * 2...]
  transfers between devices with their start and end apart: 9 -> 9, of which waited for: 3 -> 3; matrix products, arithmetic and copies ran while one was open for 2% -> 2% of each run, Pallas kernels for 13% -> 16%
where the time goes in v4:
time: 110 us; the launch traced here: 109 us
  waiting for transfers between devices  31.1 us (28%)
  Pallas kernels  31 us (28%)
  starting transfers between devices  29 us (26%)
  local copies, waits for them, and re-layouts  15.4 us (14%)
  other arithmetic  1.81 us (2%)
    ppermute x8, waiting for transfers between devices, shifted(): lax.ppermute(block, axis, [((i - distance) % n, i) for i in range(n)])  31.1 us
    ppermute x8, starting transfers between devices, shifted(): lax.ppermute(block, axis, [((i - distance) % n, i) for i in range(n)])  17.8 us
    unnamed x46, local copies, waits for them, and re-layouts  15.4 us
    all_to_all x1, starting transfers between devices, local(): lax.all_to_all(sent.reshape(N, 40, N), ('src', 'reg'), split_axis=0, conc...  11.2 us
    pallas_call x1, Pallas kernels, steps(): pl.pallas_call(steps_kernel, in_specs=[whole] * 24, out_specs=[whole] * 2...  8.43 us
    pallas_call x1, Pallas kernels, prepare(): pl.pallas_call(prepare_kernel, in_specs=[whole] * 20 + [pl.BlockSpec(memo...  5.95 us
    pallas_call x1, Pallas kernels, begin(): pl.pallas_call(begin_kernel, in_specs=[hbm] * 6, out_specs=[hbm] * 7, out...  5.39 us
    pallas_call x1, Pallas kernels, place(): pl.pallas_call(place_kernel, in_specs=[whole] + [pl.BlockSpec(memory_spac...  5.38 us
  transfers between devices with their start and end apart: 9, of which 3 were waited for; matrix products, arithmetic and copies ran while one was open for 2% of the time, Pallas kernels for 16%

profile of v4, /device:TPU:0, one launch (start us, length us, event | category | flops | bytes accessed | tf_op | source)
XLA Modules:
  0.0 109.0 jit_solution(2911011894624681217)
XLA Ops:
  0.6 5.4 %begin.1 = (f32[5,128,128]{2,1,0:T(8,128)}, f32[5,128,128]{2,1,0:T(8,128)}, f32[6,5,16,128]{3,2,1,0:T(8,128)}, f32[6,5,16,128]{3,2,1,0:T(8,128)}, f32[2,5,16,128...) custom-call(f32[3,5,128,128]{3,2,1,0:T(8,128)} %d_ref.3, f32[3,5,128,128]{3,2,1,0:T(8,128)} %v_ref.3, ...), custom_call_target="tpu_custom_call" | custom-call | tf_op jit(solution)/shard_map/begin/pallas_call | solution.py:249
  6.0 11.2 %all-to-all-start = ((f32[128,40,128]{2,1,0:T(8,128)}), f32[128,40,128]{2,1,0:T(8,128)S(1)}, u32[]{:S(2)}, u32[]{:S(2)}) async-start(f32[128,40,128]{2,1,0:T(8,128)} %bitcast.8), calls=%async_computation | async-start | bytes 5242880 | tf_op jit(solution)/shard_map/all_to_all | solution.py:806
  17.3 3.5 %collective-permute-start = (f32[5,128,128]{2,1,0:T(8,128)}, f32[5,128,128]{2,1,0:T(8,128)S(1)}, u32[]{:S(2)}, u32[]{:S(2)}) collective-permute-start(f32[5,128,128]{2,1,0:T(8,128)} %get-tuple-element.63), channel_id=1, source_target_pairs={{1,0},{2,1},{3,2},{4,3},{5,4},{6,5},{7,6},{8,7},{9,8},{10,9},{11,1... | collective-permute-start | bytes 983048 | tf_op jit(solution)/shard_map/ppermute | solution.py:112
  20.8 5.0 %collective-permute-start.2 = (f32[6,5,16,128]{3,2,1,0:T(8,128)}, f32[6,5,16,128]{3,2,1,0:T(8,128)}, u32[]{:S(2)}, u32[]{:S(2)}) collective-permute-start(f32[6,5,16,128]{3,2,1,0:T(8,128)} %get-tuple-element.94), channel_id=1, source_target_pairs={{16,0},{32,16},{48,32},{64,48},{80,64},{96,80},{112,96},{0,112},{1... | collective-permute-start | bytes 737288 | tf_op jit(solution)/shard_map/ppermute | solution.py:112
  25.8 26.9 %collective-permute-done.re_ref = f32[5,128,128]{2,1,0:T(8,128)S(1)} collective-permute-done((f32[5,128,128]{2,1,0:T(8,128)}, f32[5,128,128]{2,1,0:T(8,128)S(1)}, u32[]{:S(2)}, u32[]{:S(2)}) %collective-permute-start) | collective-permute-done | bytes 327712 | tf_op jit(solution)/shard_map/ppermute | solution.py:112
  52.7 3.2 %collective-permute-done.1.rw_ref = f32[5,128,128]{2,1,0:T(8,128)S(1)} collective-permute-done((f32[5,128,128]{2,1,0:T(8,128)}, f32[5,128,128]{2,1,0:T(8,128)S(1)}, u32[]{:S(2)}, u32[]{:S(2)}) %collective-permute-start.1) | collective-permute-done | bytes 327712 | tf_op jit(solution)/shard_map/ppermute | solution.py:112
  55.9 1.8 %fusion = (f32[4,5,16,128]{3,2,1,0:T(8,128)}, f32[4,5,16,128]{3,2,1,0:T(8,128)}) fusion(f32[1,5,128,128]{3,2,1,0:T(8,128)S(1)} %bitcast.7, f32[1,5,128,128]{3,2,1,0:T(8,128)S(1)} %bitcast.6, f32[2,5,16,128]{3,2,1,0:T(8,128)} %get-tuple-element.97, f32[2,5,16,128]{3,2,1,0:T(8,128)} %get-tuple-element.96), kind=kLoop, calls=%fused_computation.1 | loop fusion | flops 163840 | bytes 1146880 | tf_op jit(solution)/shard_map/concatenate | solution.py:811
  57.7 2.7 %collective-permute-start.5 = (f32[4,5,16,128]{3,2,1,0:T(8,128)}, f32[4,5,16,128]{3,2,1,0:T(8,128)}, u32[]{:S(2)}, u32[]{:S(2)}) collective-permute-start(f32[4,5,16,128]{3,2,1,0:T(8,128)} %get-tuple-element.122), channel_id=1, source_target_pairs={{112,0},{0,16},{16,32},{32,48},{48,64},{64,80},{80,96},{96,112},{1... | collective-permute-start | bytes 491528 | tf_op jit(solution)/shard_map/ppermute | solution.py:112
  60.4 3.0 %collective-permute-start.4 = (f32[4,5,16,128]{3,2,1,0:T(8,128)}, f32[4,5,16,128]{3,2,1,0:T(8,128)}, u32[]{:S(2)}, u32[]{:S(2)}) collective-permute-start(f32[4,5,16,128]{3,2,1,0:T(8,128)} %get-tuple-element.123), channel_id=1, source_target_pairs={{16,0},{32,16},{48,32},{64,48},{80,64},{96,80},{112,96},{0,112},{1... | collective-permute-start | bytes 491528 | tf_op jit(solution)/shard_map/ppermute | solution.py:112
  63.4 2.4 %coefs.1.refs_1_ = f32[6,128,128]{2,1,0:T(8,128)} custom-call(f32[5,128,128]{2,1,0:T(8,128)} %m_ref.5, f32[5,128,128]{2,1,0:T(8,128)} %r_ref.5, f32[5,128,128]{2,1,0:T(8,128)} %copy-done.8, f32[5,128,128]{2,1,0:T(8,128)} %copy-done.10), custom_call_target="tpu_custom_call" | custom-call | tf_op jit(solution)/shard_map/coefs/pallas_call | solution.py:310
  65.8 1.1 %copy-done.2 = bf16[3,2,256,256]{3,2,1,0:T(8,128)(2,1)S(1)} copy-done((bf16[3,2,256,256]{3,2,1,0:T(8,128)(2,1)S(1)}, bf16[3,2,256,256]{3,2,1,0:T(8,128)(2,1)}, u32[]{:S(2)}) %copy-start.2) | copy-done | bytes 786456
  66.9 1.2 %copy-done.4 = f32[3,5,128,128]{3,2,1,0:T(8,128)S(1)} copy-done((f32[3,5,128,128]{3,2,1,0:T(8,128)S(1)}, f32[3,5,128,128]{3,2,1,0:T(8,128)}, u32[]{:S(2)}) %copy-start.4) | copy-done | bytes 983064
  68.1 1.2 %copy-done.5 = f32[3,5,128,128]{3,2,1,0:T(8,128)S(1)} copy-done((f32[3,5,128,128]{3,2,1,0:T(8,128)S(1)}, f32[3,5,128,128]{3,2,1,0:T(8,128)}, u32[]{:S(2)}) %copy-start.5) | copy-done | bytes 983064
  69.3 1.0 copy-done.6
  70.3 1.0 copy-done.7
  71.3 1.0 copy-done.9
  72.3 1.0 copy-done.11
  73.2 3.4 %early.1 = (f32[4,5,4,32,128]{4,3,2,1,0:T(8,128)S(1)}, f32[4,5,4,32,128]{4,3,2,1,0:T(8,128)S(1)}, f32[2,5,4,32,128]{4,3,2,1,0:T(8,128)S(1)}, f32[2,5,4,32,128]{4...) custom-call(f32[3,5,128,128]{3,2,1,0:T(8,128)S(1)} %copy-done.4, ...), custom_call_target="tpu_custom_call" | custom-call | tf_op jit(solution)/shard_map/early/pallas_call | solution.py:610
  76.6 1.1 copy-done.12
  77.7 1.1 %copy-done.13 = f32[4,5,4,32,128]{4,3,2,1,0:T(8,128)} copy-done((f32[4,5,4,32,128]{4,3,2,1,0:T(8,128)}, f32[4,5,4,32,128]{4,3,2,1,0:T(8,128)S(1)}, u32[]{:S(2)}) %copy-start.13) | copy-done | bytes 1310744
  78.8 1.1 copy-done.14
  79.9 0.8 copy-done.15
  80.7 0.8 copy-done.16
  81.5 0.8 copy-done.17
  82.4 0.9 copy-done.18
  83.9 0.7 copy-done.21
  84.6 5.4 %place.1 = (f32[4,3,128,128]{3,2,1,0:T(8,128)S(1)}, f32[3,128,128]{2,1,0:T(8,128)S(1)}, f32[4,24,128]{2,1,0:T(8,128)S(1)}, f32[4,24,128]{2,1,0:T(8,128)S(1)}, f3...) custom-call(f32[128,40,128]{2,1,0:T(8,128)S(1)} %all-to-all-done.ref, ...), custom_call_target="tpu_custom_call" | custom-call | tf_op jit(solution)/shard_map/place/pallas_call | solution.py:424
  90.0 2.9 %collective-permute-start.6 = (f32[4,24,128]{2,1,0:T(8,128)S(1)}, f32[4,24,128]{2,1,0:T(8,128)S(1)}, u32[]{:S(2)}, u32[]{:S(2)}) collective-permute-start(f32[4,24,128]{2,1,0:T(8,128)S(1)} %get-tuple-element.120), channel_id=1, source_target_pairs={{16,0},{32,16},{48,32},{64,48},{80,64},{96,80},{112,96},{0,112},{1... | collective-permute-start | bytes 147464 | tf_op jit(solution)/shard_map/ppermute | solution.py:112
  92.9 0.7 collective-permute-start.7
  93.6 6.0 %prepare.1 = (f32[5,4,40,128]{3,2,1,0:T(8,128)S(1)}, f32[5,4,40,128]{3,2,1,0:T(8,128)S(1)}, f32[5,4,40,128]{3,2,1,0:T(8,128)S(1)}, f32[5,4,40,128]{3,2,1,0:T(8,1...) custom-call(f32[5,4,40,128]{3,2,1,0:T(8,128)S(1)} %get-tuple-element, ...), custom_call_target="tpu_custom_call", output_to_operand_aliasing={{0}: (0, {}), {1}: (1, {}), {2}: (2, {}), {3}: (3, {}), {4}... | custom-call | tf_op jit(solution)/shard_map/prepare/pallas_call | solution.py:702
  99.6 1.0 collective-permute-done.7.bo_ref
  100.6 8.4 %steps.1 = (f32[3,5,128,128]{3,2,1,0:T(8,128)}, f32[3,5,128,128]{3,2,1,0:T(8,128)}) custom-call(f32[5,4,40,128]{3,2,1,0:T(8,128)S(1)} %get-tuple-element.102.i0, f32[5,4,40,128]{3,2,1,0:T(8,128)S(1)} %get-tuple-element.103.i1, f32[5,4,40,128]{3,2,1,0:T(8,128)S(1)} %get-tuple-element.104.i2, f32[5,4,40,128]{3,2,1,0:T(8,128)S(1)} %get-tuple-element.105.i3, ...), custom_call_target="tpu_custom_call" | custom-call | tf_op jit(solution)/shard_map/steps/pallas_call | solution.py:784
  (39 shorter events, 0.7 us)
Async XLA Ops:
  6.0 78.5 %all-to-all-start = ((f32[128,40,128]{2,1,0:T(8,128)}), f32[128,40,128]{2,1,0:T(8,128)S(1)}, u32[]{:S(2)}, u32[]{:S(2)}) async-start(f32[128,40,128]{2,1,0:T(8,128)} %bitcast.8), calls=%async_computation | async-start | bytes 5242880 | tf_op jit(solution)/shard_map/all_to_all | solution.py:806
  17.2 48.6 %copy-start = (bf16[3,2,256,256]{3,2,1,0:T(8,128)(2,1)S(1)}, bf16[3,2,256,256]{3,2,1,0:T(8,128)(2,1)}, u32[]{:S(2)}) copy-start(bf16[3,2,256,256]{3,2,1,0:T(8,128)(2,1)} %constant.9.clone.back_ref.refs_27_) | copy-start | bytes 2359300
  17.2 48.6 %copy-start.19 = (bf16[256,256]{1,0:T(8,128)(2,1)S(1)}, bf16[256,256]{1,0:T(8,128)(2,1)}, u32[]{:S(2)}) copy-start(bf16[256,256]{1,0:T(8,128)(2,1)} %constant.10.clone.sel_ref.refs_24_) | copy-start | bytes 393220
  17.2 48.6 %copy-start.22 = (f32[1,256]{1,0:T(1,128)S(1)}, f32[1,256]{1,0:T(1,128)}, u32[]{:S(2)}) copy-start(f32[1,256]{1,0:T(1,128)} %constant.11.clone.qw_ref.refs_25_) | copy-start | bytes 3076
  17.3 35.5 %collective-permute-start = (f32[5,128,128]{2,1,0:T(8,128)}, f32[5,128,128]{2,1,0:T(8,128)S(1)}, u32[]{:S(2)}, u32[]{:S(2)}) collective-permute-start(f32[5,128,128]{2,1,0:T(8,128)} %get-tuple-element.63), channel_id=1, source_target_pairs={{1,0},{2,1},{3,2},{4,3},{5,4},{6,5},{7,6},{8,7},{9,8},{10,9},{11,1... | collective-permute-start | bytes 983048 | tf_op jit(solution)/shard_map/ppermute | solution.py:112
  20.8 35.1 %collective-permute-start.1 = (f32[5,128,128]{2,1,0:T(8,128)}, f32[5,128,128]{2,1,0:T(8,128)S(1)}, u32[]{:S(2)}, u32[]{:S(2)}) collective-permute-start(f32[5,128,128]{2,1,0:T(8,128)} %get-tuple-element.64), channel_id=1, source_target_pairs={{15,0},{0,1},{1,2},{2,3},{3,4},{4,5},{5,6},{6,7},{7,8},{8,9},{9,10... | collective-permute-start | bytes 983048 | tf_op jit(solution)/shard_map/ppermute | solution.py:112
  20.8 72.1 %collective-permute-start.2 = (f32[6,5,16,128]{3,2,1,0:T(8,128)}, f32[6,5,16,128]{3,2,1,0:T(8,128)}, u32[]{:S(2)}, u32[]{:S(2)}) collective-permute-start(f32[6,5,16,128]{3,2,1,0:T(8,128)} %get-tuple-element.94), channel_id=1, source_target_pairs={{16,0},{32,16},{48,32},{64,48},{80,64},{96,80},{112,96},{0,112},{1... | collective-permute-start | bytes 737288 | tf_op jit(solution)/shard_map/ppermute | solution.py:112
  25.8 67.7 %collective-permute-start.3 = (f32[6,5,16,128]{3,2,1,0:T(8,128)}, f32[6,5,16,128]{3,2,1,0:T(8,128)}, u32[]{:S(2)}, u32[]{:S(2)}) collective-permute-start(f32[6,5,16,128]{3,2,1,0:T(8,128)} %get-tuple-element.95), channel_id=1, source_target_pairs={{112,0},{0,16},{16,32},{32,48},{48,64},{64,80},{80,96},{96,112},{1... | collective-permute-start | bytes 737288 | tf_op jit(solution)/shard_map/ppermute | solution.py:112
  52.7 3.2 %copy-start.8 = (f32[5,128,128]{2,1,0:T(8,128)}, f32[5,128,128]{2,1,0:T(8,128)S(1)}, u32[]{:S(2)}) copy-start(f32[5,128,128]{2,1,0:T(8,128)S(1)} %collective-permute-done.re_ref) | copy-start | bytes 983044
  55.9 1.8 %copy-start.10 = (f32[5,128,128]{2,1,0:T(8,128)}, f32[5,128,128]{2,1,0:T(8,128)S(1)}, u32[]{:S(2)}) copy-start(f32[5,128,128]{2,1,0:T(8,128)S(1)} %collective-permute-done.1.rw_ref) | copy-start | bytes 983044
  57.7 35.9 %collective-permute-start.5 = (f32[4,5,16,128]{3,2,1,0:T(8,128)}, f32[4,5,16,128]{3,2,1,0:T(8,128)}, u32[]{:S(2)}, u32[]{:S(2)}) collective-permute-start(f32[4,5,16,128]{3,2,1,0:T(8,128)} %get-tuple-element.122), channel_id=1, source_target_pairs={{112,0},{0,16},{16,32},{32,48},{48,64},{64,80},{80,96},{96,112},{1... | collective-permute-start | bytes 491528 | tf_op jit(solution)/shard_map/ppermute | solution.py:112
  60.4 33.2 %collective-permute-start.4 = (f32[4,5,16,128]{3,2,1,0:T(8,128)}, f32[4,5,16,128]{3,2,1,0:T(8,128)}, u32[]{:S(2)}, u32[]{:S(2)}) collective-permute-start(f32[4,5,16,128]{3,2,1,0:T(8,128)} %get-tuple-element.123), channel_id=1, source_target_pairs={{16,0},{32,16},{48,32},{64,48},{80,64},{96,80},{112,96},{0,112},{1... | collective-permute-start | bytes 491528 | tf_op jit(solution)/shard_map/ppermute | solution.py:112
  65.8 1.1 %copy-start.2 = (bf16[3,2,256,256]{3,2,1,0:T(8,128)(2,1)S(1)}, bf16[3,2,256,256]{3,2,1,0:T(8,128)(2,1)}, u32[]{:S(2)}) copy-start(bf16[3,2,256,256]{3,2,1,0:T(8,128)(2,1)} %constant.8.clone.grad_ref.refs_26_) | copy-start | bytes 2359300
  66.9 1.2 %copy-start.4 = (f32[3,5,128,128]{3,2,1,0:T(8,128)S(1)}, f32[3,5,128,128]{3,2,1,0:T(8,128)}, u32[]{:S(2)}) copy-start(f32[3,5,128,128]{3,2,1,0:T(8,128)} %d_ref.3) | copy-start | bytes 2949124
  68.1 1.2 %copy-start.5 = (f32[3,5,128,128]{3,2,1,0:T(8,128)S(1)}, f32[3,5,128,128]{3,2,1,0:T(8,128)}, u32[]{:S(2)}) copy-start(f32[3,5,128,128]{3,2,1,0:T(8,128)} %v_ref.3) | copy-start | bytes 2949124
  69.3 1.0 copy-start.6
  70.3 1.0 copy-start.7
  71.3 1.0 copy-start.9
  72.3 1.0 copy-start.11
  76.6 1.1 copy-start.12
  77.7 1.1 %copy-start.13 = (f32[4,5,4,32,128]{4,3,2,1,0:T(8,128)}, f32[4,5,4,32,128]{4,3,2,1,0:T(8,128)S(1)}, u32[]{:S(2)}) copy-start(f32[4,5,4,32,128]{4,3,2,1,0:T(8,128)S(1)} %get-tuple-element.66.refs_3_) | copy-start | bytes 3932164
  78.8 1.1 copy-start.14
  79.9 0.8 copy-start.15
  80.7 0.8 copy-start.16
  81.5 0.8 copy-start.17
  82.4 0.9 copy-start.18
  83.3 0.7 copy-start.20
  83.9 0.7 copy-start.21
  90.0 9.6 %collective-permute-start.6 = (f32[4,24,128]{2,1,0:T(8,128)S(1)}, f32[4,24,128]{2,1,0:T(8,128)S(1)}, u32[]{:S(2)}, u32[]{:S(2)}) collective-permute-start(f32[4,24,128]{2,1,0:T(8,128)S(1)} %get-tuple-element.120), channel_id=1, source_target_pairs={{16,0},{32,16},{48,32},{64,48},{80,64},{96,80},{112,96},{0,112},{1... | collective-permute-start | bytes 147464 | tf_op jit(solution)/shard_map/ppermute | solution.py:112
  92.9 7.7 %collective-permute-start.7 = (f32[4,24,128]{2,1,0:T(8,128)S(1)}, f32[4,24,128]{2,1,0:T(8,128)S(1)}, u32[]{:S(2)}, u32[]{:S(2)}) collective-permute-start(f32[4,24,128]{2,1,0:T(8,128)S(1)} %get-tuple-element.121), channel_id=1, source_target_pairs={{112,0},{0,16},{16,32},{32,48},{48,64},{64,80},{80,96},{96,112},{1... | collective-permute-start | bytes 147464 | tf_op jit(solution)/shard_map/ppermute | solution.py:112
  93.6 7.0 %copy-start.1 = (bf16[3,2,256,256]{3,2,1,0:T(8,128)(2,1)S(1)}, bf16[3,2,256,256]{3,2,1,0:T(8,128)(2,1)}, u32[]{:S(2)}) copy-start(bf16[3,2,256,256]{3,2,1,0:T(8,128)(2,1)} %constant.9.clone.back_ref.refs_27_) | copy-start | bytes 2359300
  93.6 7.0 %copy-start.3 = (bf16[3,2,256,256]{3,2,1,0:T(8,128)(2,1)S(1)}, bf16[3,2,256,256]{3,2,1,0:T(8,128)(2,1)}, u32[]{:S(2)}) copy-start(bf16[3,2,256,256]{3,2,1,0:T(8,128)(2,1)} %constant.8.clone.grad_ref.refs_26_) | copy-start | bytes 2359300
